TPU v7x, 512 devices: a whole 4x8x8 slice. The times are simulated.
512 devices in a mesh: head: 8 (over z), tok: 64 (over x, y, core).
Axes of the slice: x: 4, y: 8, z: 8, core: 2. Of those that a mesh axis runs over, the one named last changes fastest.
Arguments:
- patches: bfloat16 [32768, 1280], P('tok')
- row_table: bfloat16 [64, 1280], replicated, may hold values from -0.59765625 to 0.59765625
- col_table: bfloat16 [64, 1280], replicated, may hold values from -0.59765625 to 0.59765625
- qkv_weight: bfloat16 [3, 1280, 1280], P(None, 'head'), may hold values from -0.15625 to 0.15625
- out_weight: bfloat16 [1280, 1280], P('head'), may hold values from -0.15625 to 0.15625
- merge_weight: bfloat16 [1280, 5120], P('head'), may hold values from -0.078125 to 0.078125
- segment_ids: int32 [32768], P('tok'), may hold values from 0 to 63, as said below
- image_grids: int32 [64, 2], replicated, may hold values from 2 to 62, as said below
- image_offsets: int32 [64], replicated, may hold values from 0 to 32736, as said below
- owners: int32 [64], replicated, may hold values from 0 to 63, each once
Outputs:
- delivered: bfloat16 [15872, 1280], P('tok', 'head')
Inputs may be any that keep to these rules, and one draw needn't show every extreme that they name: `segment_ids`: tokens of each image are consecutive and images follow in order; the pair p of token blocks (tokens 2 * p * 512 to 2 * (p + 1) * 512 - 1) holds exactly images 2 * p and 2 * p + 1, with no padding. `image_grids`: heights are even, widths are 16, and height times width is the image's token count. Within an image each 2x2 window of patches is four consecutive tokens (top left, top right, bottom left, bottom right), windows in row-major order. The longest image has exactly 992 tokens. `image_offsets`: the first token of each image, consistent with segment_ids. `owners`: every device index along tok owns exactly one image.
All inputs are finite; a program needn't handle non-finite values.
Results may differ from a plain program's by a relative error of at most 0.019.
Values may be sent and summed in bfloat16 or wider, within the bound.
No kernel may reach another device: no remote copies, remote signals or barrier semaphores. Data moves between devices by JAX's collectives and lax.ppermute only.
A program may use at most 64 MiB of HBM per device.

v0:
```python
import math

import jax
import jax.numpy as jnp
from jax import lax
from jax.sharding import PartitionSpec as P

HEAD_DIM = 80
CAP = 248


def partner(x, axis, apart):
    return lax.ppermute(x, axis, [(i, i ^ 1 << apart) for i in range(lax.axis_size(axis))])


def layer_norm(values):
    centered = values - jnp.mean(values, axis=-1, keepdims=True)
    variance = jnp.mean(centered * centered, axis=-1, keepdims=True)
    return centered * lax.rsqrt(variance + 1e-06)


def grid_place(token_pos, start_tok, width_now):
    local_pos = token_pos - start_tok
    window = local_pos // 4
    quarter = local_pos % 4
    half_width = jnp.maximum(width_now // 2, 1)
    row_index = 2 * (window // half_width) + quarter // 2
    col_index = 2 * (window % half_width) + quarter % 2
    return (row_index, col_index)


def dot_last(left, right):
    return lax.dot_general(
        left, right, (((1,), (1,)), ((), ())), preferred_element_type=jnp.float32
    )


def on_device(
    patches,
    row_table,
    col_table,
    qkv_weight,
    out_weight,
    merge_weight,
    segment_ids,
    image_grids,
    image_offsets,
    owners,
):
    block_rows = patches.shape[0]
    width_here = qkv_weight.shape[1]
    heads_here = width_here // HEAD_DIM
    image_count = owners.shape[0]
    image_ids = jnp.arange(image_count, dtype=jnp.int32)
    token_pos = lax.axis_index("tok") * block_rows + jnp.arange(block_rows, dtype=jnp.int32)
    member = segment_ids[:, None] == image_ids[None, :]
    start_tok = jnp.sum(jnp.where(member, image_offsets[None, :], 0), axis=1)
    width_now = jnp.sum(jnp.where(member, image_grids[None, :, 1], 0), axis=1)
    row_index, col_index = grid_place(token_pos, start_tok, width_now)
    side_ids = jnp.arange(row_table.shape[0], dtype=jnp.int32)
    row_onehot = (row_index[:, None] == side_ids[None, :]).astype(jnp.bfloat16)
    col_onehot = (col_index[:, None] == side_ids[None, :]).astype(jnp.bfloat16)
    resid = (
        patches.astype(jnp.float32)
        + jnp.dot(row_onehot, row_table, preferred_element_type=jnp.float32)
        + jnp.dot(col_onehot, col_table, preferred_element_type=jnp.float32)
    )
    normed = layer_norm(resid).astype(jnp.bfloat16)
    query_rows = dot_last(normed, qkv_weight[0]).astype(jnp.bfloat16)
    key_rows = dot_last(normed, qkv_weight[1]).astype(jnp.bfloat16)
    value_rows = dot_last(normed, qkv_weight[2]).astype(jnp.bfloat16)
    seg_wire = segment_ids.astype(jnp.bfloat16)
    far_keys, far_values, far_seg = partner((key_rows, value_rows, seg_wire), "tok", 0)
    query_heads = query_rows.reshape(block_rows, heads_here, HEAD_DIM)
    key_heads = jnp.concatenate([key_rows, far_keys], axis=0).reshape(
        2 * block_rows, heads_here, HEAD_DIM
    )
    value_heads = jnp.concatenate([value_rows, far_values], axis=0).reshape(
        2 * block_rows, heads_here, HEAD_DIM
    )
    query_seg = seg_wire.astype(jnp.float32)
    key_seg = jnp.concatenate([seg_wire, far_seg], axis=0).astype(jnp.float32)
    scores = jnp.einsum(
        "qhd,khd->hqk", query_heads, key_heads, preferred_element_type=jnp.float32
    ) * (1.0 / math.sqrt(HEAD_DIM))
    same_image = query_seg[:, None] == key_seg[None, :]
    raw_weights = jnp.where(same_image[None], jnp.exp(scores), 0.0)
    weight_sum = jnp.sum(raw_weights, axis=-1, keepdims=True)
    attn_probs = (raw_weights / weight_sum).astype(jnp.bfloat16)
    mixed = jnp.einsum("hqk,khd->qhd", attn_probs, value_heads, preferred_element_type=jnp.float32)
    attended = mixed.reshape(block_rows, width_here).astype(jnp.bfloat16)
    partial_sum = jnp.dot(attended, out_weight, preferred_element_type=jnp.float32)
    head_total = lax.psum(partial_sum.astype(jnp.bfloat16), "head").astype(jnp.float32)
    normed_two = layer_norm(resid + head_total).astype(jnp.bfloat16)
    merged = normed_two.reshape(block_rows // 4, 4 * normed_two.shape[1])
    projected = dot_last(merged, merge_weight).astype(jnp.bfloat16)
    owner_mask = owners == lax.axis_index("tok")
    image_id = jnp.sum(jnp.where(owner_mask, image_ids, 0))
    chosen = image_ids == image_id
    first_row = jnp.sum(jnp.where(chosen, image_offsets, 0)) // 4
    merged_count = jnp.sum(jnp.where(chosen, image_grids[:, 0] * image_grids[:, 1], 0)) // 4
    slot_ids = jnp.arange(CAP, dtype=jnp.int32)
    piece_rows = lax.all_gather(projected, "tok", axis=0, tiled=True)
    row_ids = jnp.arange(piece_rows.shape[0], dtype=jnp.int32)
    slot_of = row_ids - first_row
    inside = row_ids < first_row + merged_count
    selector = (slot_of[None, :] == slot_ids[:, None]) & inside[None, :]
    owner_rows = jnp.dot(
        selector.astype(jnp.bfloat16), piece_rows, preferred_element_type=jnp.float32
    )
    return owner_rows.astype(jnp.bfloat16)


def solution(mesh):
    placed = (
        P("tok", None),
        P(),
        P(),
        P(None, "head", None),
        P("head", None),
        P("head", None),
        P("tok"),
        P(),
        P(),
        P(),
    )
    return jax.shard_map(
        on_device, mesh=mesh, in_specs=placed, out_specs=P("tok", "head"), check_vma=False
    )
```

profile of v0, /device:TPU:1, one launch (start us, length us, event | category | flops | bytes accessed | tf_op | source)
XLA Modules:
  0.0 213.2 jit_solution(1868882156168978352)
XLA Ops:
  6.5 0.0 copy-start
  6.5 0.0 all-reduce.2.cloned.1.call-start
  6.5 0.8 slice_bitcast_fusion
  7.4 0.8 select_reduce_fusion
  8.1 0.1 fusion.25
  8.3 2.0 convolution_add_fusion.1
  10.3 0.0 copy-done.5
  10.3 0.6 fusion.36
  10.9 0.4 multiply_reduce_fusion.1
  11.4 0.0 copy-start.6
  11.4 0.3 multiply_convert_fusion.1
  11.7 0.7 copy-done.1
  12.4 0.7 copy-done.9
  13.1 0.6 convolution_convert_fusion.3
  13.7 8.8 %collective-permute-start = (bf16[512,160]{0,1:T(8,128)(2,1)S(1)}, bf16[512,160]{0,1:T(8,128)(2,1)S(1)}, u32[]{:S(2)}, u32[]{:S(2)}) collective-permute-start(bf16[512,160]{0,1:T(8,128)(2,1)S(1)} %convolution_convert_fusion.3), channel_id=1, source_target_pairs={{0,1},{1,0},{2,3},{3,2},{4,5},{5,4},{6,7},{7,6},{8,9},{9,8},{10,11... | collective-permute-start | bytes 491528 | tf_op jit(solution)/shard_map/ppermute | solution.py:13
  22.5 0.0 copy-done.6
  22.5 1.9 collective-permute-start.1
  24.5 0.6 convolution_convert_fusion.1
  25.0 2.4 %collective-permute-start.2 = (bf16[512,160]{0,1:T(8,128)(2,1)S(1)}, bf16[512,160]{0,1:T(8,128)(2,1)S(1)}, u32[]{:S(2)}, u32[]{:S(2)}) collective-permute-start(bf16[512,160]{0,1:T(8,128)(2,1)S(1)} %convolution_convert_fusion.1), channel_id=1, source_target_pairs={{0,1},{1,0},{2,3},{3,2},{4,5},{5,4},{6,7},{7,6},{8,9},{9,8},{10,11... | collective-permute-start | bytes 491528 | tf_op jit(solution)/shard_map/ppermute | solution.py:13
  27.5 0.6 convolution_convert_fusion.2
  28.0 0.0 collective-permute-done.1
  28.1 0.4 broadcast_compare_fusion
  28.4 0.0 collective-permute-done.2
  28.5 1.5 fusion.5
  30.0 0.0 collective-permute-done
  30.0 0.0 copy-start.4
  30.0 1.4 fusion.7
  31.4 0.0 copy-done.4
  31.4 1.6 convolution_convert_fusion
  33.0 0.0 all-reduce.2.cloned.1.call-update
  33.1 0.0 all-gather.2.cloned.1.call-start
  33.1 78.2 %all-reduce.2.cloned.1.call-done = bf16[512,1280]{1,0:T(8,128)(2,1)} async-done(((bf16[512,1280]{1,0:T(8,128)(2,1)}), bf16[512,1280]{1,0:T(8,128)(2,1)}) %all-reduce.2.cloned.1.call-update) | async-done | bytes 1310736 | tf_op jit(solution)/shard_map/psum | solution.py:93
  111.4 2.6 %fusion.11 = f32[512]{0:T(512)S(1)} fusion(f32[512,1280]{1,0:T(8,128)} %copy-done.1, bf16[512,1280]{1,0:T(8,128)(2,1)} %all-reduce.2.cloned.1.call-done), kind=kLoop, calls=%fused_computation.24 | loop fusion | flops 1965568 | bytes 3934208 | tf_op jit(solution)/shard_map/reduce_sum | solution.py:17
  114.0 0.3 copy-done.2
  114.3 0.4 copy-done.3
  114.6 0.5 multiply_reduce_fusion
  115.2 1.5 multiply_convert_fusion
  116.7 2.5 %reshape.198 = bf16[128,5120]{1,0:T(8,128)(2,1)S(1)} reshape(bf16[512,1280]{1,0:T(8,128)(2,1)} %multiply_convert_fusion) | data formatting | bytes 2621440 | tf_op jit(solution)/shard_map/reshape | solution.py:95
  119.2 0.0 copy-done
  119.2 1.2 convolution_convert_fusion.4
  120.4 0.0 all-gather.2.cloned.1.call-update
  120.5 0.0 copy-done.10
  120.5 0.6 fusion.32
  121.1 0.0 copy-done.7
  121.1 0.0 copy-done.8
  121.1 1.3 fusion.30
  127.3 74.8 %all-gather.2.cloned.1.call-done = bf16[8192,160]{0,1:T(8,128)(2,1)} async-done(((bf16[128,160]{0,1:T(8,128)(2,1)}), bf16[8192,160]{0,1:T(8,128)(2,1)}) %all-gather.2.cloned.1.call-update) | async-done | bytes 2621456 | tf_op jit(solution)/shard_map/all_gather | solution.py:103
  202.1 4.3 %fusion.8 = bf16[248,160]{0,1:T(8,128)(2,1)} fusion(bf16[8192,160]{0,1:T(8,128)(2,1)} %all-gather.2.cloned.1.call-done, s32[8192]{0:T(1024)S(1)} %iota_subtract_fusion, pred[8192]{0:T(1024)(128)(4,1)S(1)} %iota_compare_fusion.6), kind=kOutput, calls=%fused_computation.21 | convolution fusion | flops 654220032 | bytes 2741760 | tf_op jit(solution)/shard_map/dot_general | solution.py:108
  (18 shorter events, 0.1 us)
Async XLA Ops:
  6.5 112.7 %copy-start = (bf16[160,5120]{1,0:T(8,128)(2,1)S(1)}, bf16[160,5120]{1,0:T(8,128)(2,1)}, u32[]{:S(2)}) copy-start(bf16[160,5120]{1,0:T(8,128)(2,1)} %param.15) | copy-start | bytes 4915204
  6.5 3.7 %copy-start.5 = (bf16[64,1280]{1,0:T(8,128)(2,1)S(1)}, bf16[64,1280]{1,0:T(8,128)(2,1)}, u32[]{:S(2)}) copy-start(bf16[64,1280]{1,0:T(8,128)(2,1)} %param.12) | copy-start | bytes 491524
  6.5 104.8 %all-reduce.2.cloned.1.call-start = ((), (), s32[]{:S(2)}) async-start(), calls=%async_computation | async-start | bytes 2621440 | tf_op jit(solution)/shard_map/psum | solution.py:93
  10.9 1.5 copy-start.1
  11.3 1.8 copy-start.9
  11.4 11.2 %copy-start.6 = (s32[512]{0:T(512)S(1)}, s32[512]{0:T(512)}, u32[]{:S(2)}) copy-start(s32[512]{0:T(512)} %param.16) | copy-start | bytes 6148
  13.7 16.3 %collective-permute-start = (bf16[512,160]{0,1:T(8,128)(2,1)S(1)}, bf16[512,160]{0,1:T(8,128)(2,1)S(1)}, u32[]{:S(2)}, u32[]{:S(2)}) collective-permute-start(bf16[512,160]{0,1:T(8,128)(2,1)S(1)} %convolution_convert_fusion.3), channel_id=1, source_target_pairs={{0,1},{1,0},{2,3},{3,2},{4,5},{5,4},{6,7},{7,6},{8,9},{9,8},{10,11... | collective-permute-start | bytes 491528 | tf_op jit(solution)/shard_map/ppermute | solution.py:13
  22.5 5.5 %collective-permute-start.1 = (bf16[512]{0:T(512)(128)(2,1)S(1)}, bf16[512]{0:T(512)(128)(2,1)S(1)}, u32[]{:S(2)}, u32[]{:S(2)}) collective-permute-start(bf16[512]{0:T(512)(128)(2,1)S(1)} %get-tuple-element.8), channel_id=1, source_target_pairs={{0,1},{1,0},{2,3},{3,2},{4,5},{5,4},{6,7},{7,6},{8,9},{9,8},{10,11... | collective-permute-start | bytes 3080 | tf_op jit(solution)/shard_map/ppermute | solution.py:13
  25.0 3.4 %collective-permute-start.2 = (bf16[512,160]{0,1:T(8,128)(2,1)S(1)}, bf16[512,160]{0,1:T(8,128)(2,1)S(1)}, u32[]{:S(2)}, u32[]{:S(2)}) collective-permute-start(bf16[512,160]{0,1:T(8,128)(2,1)S(1)} %convolution_convert_fusion.1), channel_id=1, source_target_pairs={{0,1},{1,0},{2,3},{3,2},{4,5},{5,4},{6,7},{7,6},{8,9},{9,8},{10,11... | collective-permute-start | bytes 491528 | tf_op jit(solution)/shard_map/ppermute | solution.py:13
  30.0 1.4 copy-start.4
  33.1 169.0 %all-gather.2.cloned.1.call-start = ((), (), s32[]{:S(2)}) async-start(), calls=%async_computation.1 | async-start | bytes 2662400 | tf_op jit(solution)/shard_map/all_gather | solution.py:103
  111.4 2.9 %copy-start.2 = (f32[512,1280]{1,0:T(8,128)S(1)}, f32[512,1280]{1,0:T(8,128)}, u32[]{:S(2)}) copy-start(f32[512,1280]{1,0:T(8,128)} %copy-done.1) | copy-start | bytes 7864324
  111.4 3.3 %copy-start.3 = (bf16[512,1280]{1,0:T(8,128)(2,1)S(1)}, bf16[512,1280]{1,0:T(8,128)(2,1)}, u32[]{:S(2)}) copy-start(bf16[512,1280]{1,0:T(8,128)(2,1)} %all-reduce.2.cloned.1.call-done) | copy-start | bytes 3932164
  116.7 3.8 %copy-start.10 = (s32[64]{0:T(128)S(1)}, s32[64]{0:T(128)}, u32[]{:S(2)}) copy-start(s32[64]{0:T(128)} %param.19) | copy-start | bytes 772
  116.7 4.4 %copy-start.7 = (s32[64]{0:T(128)S(1)}, s32[64]{0:T(128)}, u32[]{:S(2)}) copy-start(s32[64]{0:T(128)} %param.18) | copy-start | bytes 772
  116.7 4.4 %copy-start.8 = (s32[64,2]{0,1:T(2,128)S(1)}, s32[64,2]{0,1:T(2,128)}, u32[]{:S(2)}) copy-start(s32[64,2]{0,1:T(2,128)} %param.17) | copy-start | bytes 1540
Sparse Core Ops, SparseCore 0:
  33.2 78.1 all-reduce.1
  120.6 81.4 all-gather.1
where the time goes:
time: 214 us; the launch traced here: 213 us
  waiting for transfers between devices  153 us (71%)
  between operations  18.4 us (9%)
  matrix products  14.4 us (7%)
  starting transfers between devices  13.2 us (6%)
  other arithmetic  8.66 us (4%)
  local copies, waits for them, and re-layouts  5.5 us (3%)
    psum x1, waiting for transfers between devices, on_device(): lax.psum(partial_sum.astype(jnp.bfloat16), 'head').astype(jnp.float32)  78.2 us
    all_gather x1, waiting for transfers between devices, on_device(): piece_rows = lax.all_gather(projected, 'tok', axis=0, tiled=True)  74.8 us
    ppermute x3, starting transfers between devices, partner(): lax.ppermute(x, axis, [(i, i ^ 1 << apart) for i in range(lax.axis_size(a...  13.1 us
    dot_general x1, matrix products, on_device(): jnp.dot(selector.astype(jnp.bfloat16), piece_rows, preferred_element_type...  4.35 us
  transfers between devices with their start and end apart: 5, of which 2 were waited for; matrix products, arithmetic and copies ran while one was open for 2% of the time, Pallas kernels for 0%

commit v1 on v0

--- a/solution.py
+++ b/solution.py
@@ -47,6 +47,7 @@
     image_offsets,
     owners,
 ):
+    full_weight = lax.all_gather(out_weight, "head", axis=0, tiled=True)
     block_rows = patches.shape[0]
     width_here = qkv_weight.shape[1]
     heads_here = width_here // HEAD_DIM
@@ -89,24 +90,46 @@
     attn_probs = (raw_weights / weight_sum).astype(jnp.bfloat16)
     mixed = jnp.einsum("hqk,khd->qhd", attn_probs, value_heads, preferred_element_type=jnp.float32)
     attended = mixed.reshape(block_rows, width_here).astype(jnp.bfloat16)
-    partial_sum = jnp.dot(attended, out_weight, preferred_element_type=jnp.float32)
-    head_total = lax.psum(partial_sum.astype(jnp.bfloat16), "head").astype(jnp.float32)
+    group = lax.axis_size("head")
+    sent = jnp.broadcast_to(attended[None], (group,) + attended.shape)
+    gathered = lax.all_to_all(sent, "head", 0, 0, tiled=True)
+    head_total = jnp.einsum(
+        "ztf,zfd->td",
+        gathered,
+        full_weight.reshape(group, width_here, -1),
+        preferred_element_type=jnp.float32,
+    )
     normed_two = layer_norm(resid + head_total).astype(jnp.bfloat16)
     merged = normed_two.reshape(block_rows // 4, 4 * normed_two.shape[1])
     projected = dot_last(merged, merge_weight).astype(jnp.bfloat16)
+
+    places = lax.axis_size("tok")
+    rows_here = projected.shape[0]
+    share = rows_here // places
+    spread = lax.all_to_all(projected.reshape(places, share, width_here), "tok", 0, 0, tiled=True)
+    pair_ids = jnp.arange(places // 2, dtype=jnp.int32)
+    place_ids = jnp.arange(places, dtype=jnp.int32)
+    wanted = (owners.reshape(-1, 2)[None, :, :] == place_ids[:, None, None]).any(axis=2)
+    pieces = jnp.dot(
+        wanted.astype(jnp.bfloat16),
+        spread.reshape(places // 2, 2 * share * width_here),
+        preferred_element_type=jnp.float32,
+    ).astype(jnp.bfloat16)
+    pair_rows = lax.all_to_all(
+        pieces.reshape(places, 2 * share, width_here), "tok", 0, 0, tiled=True
+    ).reshape(2 * rows_here, width_here)
+
     owner_mask = owners == lax.axis_index("tok")
     image_id = jnp.sum(jnp.where(owner_mask, image_ids, 0))
-    chosen = image_ids == image_id
-    first_row = jnp.sum(jnp.where(chosen, image_offsets, 0)) // 4
-    merged_count = jnp.sum(jnp.where(chosen, image_grids[:, 0] * image_grids[:, 1], 0)) // 4
+    first_row = jnp.sum(jnp.where(owner_mask, image_offsets, 0)) // 4 - (image_id // 2) * 2 * rows_here
+    merged_count = jnp.sum(jnp.where(owner_mask, image_grids[:, 0] * image_grids[:, 1], 0)) // 4
     slot_ids = jnp.arange(CAP, dtype=jnp.int32)
-    piece_rows = lax.all_gather(projected, "tok", axis=0, tiled=True)
-    row_ids = jnp.arange(piece_rows.shape[0], dtype=jnp.int32)
-    slot_of = row_ids - first_row
-    inside = row_ids < first_row + merged_count
-    selector = (slot_of[None, :] == slot_ids[:, None]) & inside[None, :]
+    got_ids = jnp.arange(2 * rows_here, dtype=jnp.int32)
+    row_of = (got_ids // share % 2) * rows_here + got_ids // (2 * share) * share + got_ids % share
+    slot_of = row_of - first_row
+    selector = (slot_of[None, :] == slot_ids[:, None]) & (slot_ids < merged_count)[:, None]
     owner_rows = jnp.dot(
-        selector.astype(jnp.bfloat16), piece_rows, preferred_element_type=jnp.float32
+        selector.astype(jnp.bfloat16), pair_rows, preferred_element_type=jnp.float32
     )
     return owner_rows.astype(jnp.bfloat16)
 

time: 214 us -> 147 us (0.69)
  waiting for transfers between devices: 153 us -> 67.3 us
  starting transfers between devices: 13.2 us -> 32.6 us
  other arithmetic: 8.66 us -> 3.64 us
  between operations: 18.4 us -> 21.2 us
    psum x1 -> x0, waiting for transfers between devices: 78.2 us -> none  [on_device(): lax.psum(partial_sum.astype(jnp.bfloat16), 'head').astype(jnp.float32)]
    all_gather x1, waiting for transfers between devices: 74.8 us -> 6.37 us  [on_device(): full_weight = lax.all_gather(out_weight, 'head', axis=0, tiled=True)]
    all_to_all x0 -> x3, waiting for transfers between devices: none -> 60.2 us  [the longest x1 44.9 us: on_device(): gathered = lax.all_to_all(sent, 'head', 0, 0, tiled=True)]
    all_to_all x0 -> x3, starting transfers between devices: none -> 19.5 us  [the longest x1 10.4 us: on_device(): lax.all_to_all(projected.reshape(places, share, width_here), 'tok', 0, 0,...]
    reduce_sum x3 -> x1, other arithmetic: 4.54 us -> 0.74 us  [on_device(): jnp.sum(jnp.where(owner_mask, image_grids[:, 0] * image_grids[:, 1], 0))]
    dot_general x2 -> x3, matrix products: 5.98 us -> 5.97 us  [the longest x1 4.83 us: on_device(): jnp.einsum('ztf,zfd->td', gathered, full_weight.reshape(group, width_here...]
  transfers between devices with their start and end apart: 5 -> 7, of which waited for: 2 -> 4; matrix products, arithmetic and copies ran while one was open for 2% -> 8% of each run, Pallas kernels for 0% -> 0%
where the time goes in v1:
time: 147 us
  waiting for transfers between devices  67.3 us (46%)
  starting transfers between devices  32.6 us (22%)
  between operations  21.2 us (14%)
  matrix products  15.1 us (10%)
  local copies, waits for them, and re-layouts  6.95 us (5%)
  other arithmetic  3.64 us (2%)
    all_to_all x1, waiting for transfers between devices, on_device(): gathered = lax.all_to_all(sent, 'head', 0, 0, tiled=True)  44.9 us
    ppermute x3, starting transfers between devices, partner(): lax.ppermute(x, axis, [(i, i ^ 1 << apart) for i in range(lax.axis_size(a...  13.1 us
    all_to_all x1, starting transfers between devices, on_device(): lax.all_to_all(projected.reshape(places, share, width_here), 'tok', 0, 0,...  10.4 us
    all_to_all x1, waiting for transfers between devices, on_device(): lax.all_to_all(projected.reshape(places, share, width_here), 'tok', 0, 0,...  9.7 us
    all_gather x1, waiting for transfers between devices, on_device(): full_weight = lax.all_gather(out_weight, 'head', axis=0, tiled=True)  6.37 us
    all_to_all x1, waiting for transfers between devices, on_device(): lax.all_to_all(pieces.reshape(places, 2 * share, width_here), 'tok', 0, 0...  5.53 us
    dot_general x1, matrix products, on_device(): jnp.einsum('ztf,zfd->td', gathered, full_weight.reshape(group, width_here...  4.83 us
    all_to_all x1, starting transfers between devices, on_device(): gathered = lax.all_to_all(sent, 'head', 0, 0, tiled=True)  4.66 us
  transfers between devices with their start and end apart: 7, of which 4 were waited for; matrix products, arithmetic and copies ran while one was open for 8% of the time, Pallas kernels for 0%

profile of v1, /device:TPU:1, one launch (start us, length us, event | category | flops | bytes accessed | tf_op | source)
XLA Modules:
  0.0 146.8 jit_solution(14957617930545872145)
XLA Ops:
  6.5 0.7 all-gather.2.cloned.1.call-update
  7.3 0.7 slice_bitcast_fusion
  7.9 0.8 select_reduce_fusion
  8.7 0.1 fusion.22
  8.9 2.0 %convolution_add_fusion.1 = f32[512,1280]{1,0:T(8,128)S(1)} fusion(bf16[64,1280]{1,0:T(8,128)(2,1)} %param.11, bf16[512,1280]{1,0:T(8,128)(2,1)} %param.10, s32[512]{0:T(512)S(1)} %get-tuple-element.13), kind=kOutput, calls=%fused_computation.3 | convolution fusion | flops 85229568 | bytes 4098048 | tf_op jit(solution)/shard_map/dot_general | solution.py:66
  10.9 0.6 fusion.41
  11.5 0.4 multiply_reduce_fusion.1
  11.9 0.0 copy-start.3
  12.0 0.3 multiply_convert_fusion.1
  12.3 0.8 copy-done.1
  13.0 0.7 copy-done.7
  13.7 0.6 convolution_convert_fusion
  14.3 8.8 %collective-permute-start.2 = (bf16[512,160]{0,1:T(8,128)(2,1)S(1)}, bf16[512,160]{0,1:T(8,128)(2,1)S(1)}, u32[]{:S(2)}, u32[]{:S(2)}) collective-permute-start(bf16[512,160]{0,1:T(8,128)(2,1)S(1)} %convolution_convert_fusion), channel_id=1, source_target_pairs={{0,1},{1,0},{2,3},{3,2},{4,5},{5,4},{6,7},{7,6},{8,9},{9,8},{10,11... | collective-permute-start | bytes 491528 | tf_op jit(solution)/shard_map/ppermute | solution.py:13
  23.1 1.9 %collective-permute-start.1 = (bf16[512]{0:T(512)(128)(2,1)S(1)}, bf16[512]{0:T(512)(128)(2,1)S(1)}, u32[]{:S(2)}, u32[]{:S(2)}) collective-permute-start(bf16[512]{0:T(512)(128)(2,1)S(1)} %get-tuple-element.11), channel_id=1, source_target_pairs={{0,1},{1,0},{2,3},{3,2},{4,5},{5,4},{6,7},{7,6},{8,9},{9,8},{10,11... | collective-permute-start | bytes 3080 | tf_op jit(solution)/shard_map/ppermute | solution.py:13
  25.0 0.6 convolution_convert_fusion.2
  25.6 2.4 %collective-permute-start = (bf16[512,160]{0,1:T(8,128)(2,1)S(1)}, bf16[512,160]{0,1:T(8,128)(2,1)S(1)}, u32[]{:S(2)}, u32[]{:S(2)}) collective-permute-start(bf16[512,160]{0,1:T(8,128)(2,1)S(1)} %convolution_convert_fusion.2), channel_id=1, source_target_pairs={{0,1},{1,0},{2,3},{3,2},{4,5},{5,4},{6,7},{7,6},{8,9},{9,8},{10,11... | collective-permute-start | bytes 491528 | tf_op jit(solution)/shard_map/ppermute | solution.py:13
  28.0 0.6 convolution_convert_fusion.1
  28.6 0.4 broadcast_compare_fusion
  29.0 0.0 collective-permute-done.2
  29.1 1.5 %fusion = (f32[2,512]{1,0:T(2,128)S(1)}, f32[2,512,1024]{2,1,0:T(8,128)S(1)}) fusion(pred[512,1024]{1,0:T(8,128)(4,1)S(1)} %broadcast_compare_fusion, bf16[512,2,80]{0,2,1:T(8,128)(2,1)S(1)} %bitcast.49, bf16[1024,2,80]{0,2,1:T(8,128)(2,1)S(1)} %bitcast.46), kind=kOutput, calls=%fused_computation.4 | convolution fusion | flops 170916864 | bytes 5214208 | tf_op jit(solution)/shard_map/qhd,khd->hqk/dot_general | solution.py:84
  30.6 1.4 fusion.3
  31.9 0.0 copy-start.5
  32.0 0.0 copy-start.4
  32.0 0.0 copy-start.6
  32.0 1.2 broadcast_in_dim.69
  33.2 4.7 %all-to-all-start = ((bf16[8,512,160]{1,2,0:T(8,128)(2,1)}), bf16[8,512,160]{1,2,0:T(8,128)(2,1)S(1)}, u32[]{:S(2)}, u32[]{:S(2)}) async-start(bf16[8,512,160]{1,2,0:T(8,128)(2,1)} %broadcast_in_dim.69), calls=%async_computation | async-start | bytes 2621440 | tf_op jit(solution)/shard_map/all_to_all | solution.py:95
  37.8 0.1 eq.109
  38.0 0.7 fusion.37
  40.0 0.1 copy.12
  41.4 44.9 %all-to-all-done = bf16[8,512,160]{1,2,0:T(8,128)(2,1)S(1)} async-done(((bf16[8,512,160]{1,2,0:T(8,128)(2,1)}), bf16[8,512,160]{1,2,0:T(8,128)(2,1)S(1)}, u32[]{:S(2)}, u32[]{:S(2)}) %all-to-all-start) | async-done | bytes 1310752 | tf_op jit(solution)/shard_map/all_to_all | solution.py:95
  86.3 6.4 %all-gather.2.cloned.1.call-done = bf16[1280,1280]{1,0:T(8,128)(2,1)} async-done(((bf16[160,1280]{1,0:T(8,128)(2,1)}), bf16[1280,1280]{1,0:T(8,128)(2,1)}) %all-gather.2.cloned.1.call-update) | async-done | bytes 3276816 | tf_op jit(solution)/shard_map/all_gather | solution.py:50
  92.7 4.8 %fusion.42 = (f32[512]{0:T(512)S(1)}, f32[512,1280]{1,0:T(8,128)S(1)}) fusion(f32[512,1280]{1,0:T(8,128)} %copy-done.1, bf16[8,512,160]{1,2,0:T(8,128)(2,1)S(1)} %all-to-all-done, bf16[8,160,1280]{2,1,0:T(8,128)(2,1)} %bitcast.45), kind=kOutput, calls=%fused_computation.113 | convolution fusion | flops 1679031808 | bytes 9832448 | tf_op jit(solution)/shard_map/ztf,zfd->td/dot_general | solution.py:96
  97.5 0.4 multiply_reduce_fusion
  98.0 0.3 multiply_convert_fusion
  98.3 1.7 %reshape.260 = bf16[128,5120]{1,0:T(8,128)(2,1)} reshape(bf16[512,1280]{1,0:T(8,128)(2,1)S(1)} %multiply_convert_fusion) | data formatting | bytes 2621440 | tf_op jit(solution)/shard_map/reshape | solution.py:103
  100.0 1.9 %convolution_convert_fusion.5 = bf16[128,160]{0,1:T(8,128)(2,1)S(1)} fusion(bf16[128,5120]{1,0:T(8,128)(2,1)} %reshape.260, bf16[160,5120]{1,0:T(8,128)(2,1)S(1)} %copy-done), kind=kOutput, calls=%fused_computation.18 | convolution fusion | flops 209735680 | bytes 2990080 | tf_op jit(solution)/shard_map/dot_general | solution.py:33
  101.9 0.1 copy.13
  102.0 0.7 reshape.261
  102.7 10.4 %all-to-all-start.1 = ((bf16[64,2,160]{2,1,0:T(2,128)(2,1)}), bf16[64,2,160]{2,1,0:T(2,128)(2,1)S(1)}, u32[]{:S(2)}, u32[]{:S(2)}) async-start(bf16[64,2,160]{2,1,0:T(2,128)(2,1)} %reshape.261), calls=%async_computation.1 | async-start | bytes 131072 | tf_op jit(solution)/shard_map/all_to_all | solution.py:109
  113.1 0.1 fusion.16
  113.2 9.7 %all-to-all-done.1 = bf16[64,2,160]{2,1,0:T(2,128)(2,1)S(1)} async-done(((bf16[64,2,160]{2,1,0:T(2,128)(2,1)}), bf16[64,2,160]{2,1,0:T(2,128)(2,1)S(1)}, u32[]{:S(2)}, u32[]{:S(2)}) %all-to-all-start.1) | async-done | bytes 40992 | tf_op jit(solution)/shard_map/all_to_all | solution.py:109
  122.9 0.1 reshape.262
  123.0 0.2 convolution_convert_fusion.4
  123.2 0.8 reshape.263
  124.0 4.4 %all-to-all-start.2 = ((bf16[64,4,160]{2,1,0:T(4,128)(2,1)}), bf16[64,4,160]{2,1,0:T(4,128)(2,1)S(1)}, u32[]{:S(2)}, u32[]{:S(2)}) async-start(bf16[64,4,160]{2,1,0:T(4,128)(2,1)} %reshape.263), calls=%async_computation.2 | async-start | bytes 262144 | tf_op jit(solution)/shard_map/all_to_all | solution.py:118
  133.4 5.5 %all-to-all-done.2 = bf16[64,4,160]{2,1,0:T(4,128)(2,1)S(1)} async-done(((bf16[64,4,160]{2,1,0:T(4,128)(2,1)}), bf16[64,4,160]{2,1,0:T(4,128)(2,1)S(1)}, u32[]{:S(2)}, u32[]{:S(2)}) %all-to-all-start.2) | async-done | bytes 81952 | tf_op jit(solution)/shard_map/all_to_all | solution.py:118
  138.9 0.1 reshape.264
  139.0 0.9 convolution_convert_fusion.3
  (23 shorter events, 0.1 us)
Async XLA Ops:
  6.5 93.4 %copy-start = (bf16[160,5120]{1,0:T(8,128)(2,1)S(1)}, bf16[160,5120]{1,0:T(8,128)(2,1)}, u32[]{:S(2)}) copy-start(bf16[160,5120]{1,0:T(8,128)(2,1)} %param.15) | copy-start | bytes 4915204
  6.5 4.3 %copy-start.2 = (bf16[64,1280]{1,0:T(8,128)(2,1)S(1)}, bf16[64,1280]{1,0:T(8,128)(2,1)}, u32[]{:S(2)}) copy-start(bf16[64,1280]{1,0:T(8,128)(2,1)} %param.12) | copy-start | bytes 491524
  6.5 86.2 %all-gather.2.cloned.1.call-start = ((), (), s32[]{:S(2)}) async-start(), calls=%async_computation.3 | async-start | bytes 3686400 | tf_op jit(solution)/shard_map/all_gather | solution.py:50
  11.5 1.5 %copy-start.1 = (f32[512,1280]{1,0:T(8,128)}, f32[512,1280]{1,0:T(8,128)S(1)}, u32[]{:S(2)}) copy-start(f32[512,1280]{1,0:T(8,128)S(1)} %get-tuple-element.15) | copy-start | bytes 7864324
  11.9 1.8 %copy-start.7 = (bf16[3,160,1280]{2,1,0:T(8,128)(2,1)S(1)}, bf16[3,160,1280]{2,1,0:T(8,128)(2,1)}, u32[]{:S(2)}) copy-start(bf16[3,160,1280]{2,1,0:T(8,128)(2,1)} %param.13) | copy-start | bytes 3686404
  11.9 11.2 %copy-start.3 = (s32[512]{0:T(512)S(1)}, s32[512]{0:T(512)}, u32[]{:S(2)}) copy-start(s32[512]{0:T(512)} %param.16) | copy-start | bytes 6148
  14.3 14.7 %collective-permute-start.2 = (bf16[512,160]{0,1:T(8,128)(2,1)S(1)}, bf16[512,160]{0,1:T(8,128)(2,1)S(1)}, u32[]{:S(2)}, u32[]{:S(2)}) collective-permute-start(bf16[512,160]{0,1:T(8,128)(2,1)S(1)} %convolution_convert_fusion), channel_id=1, source_target_pairs={{0,1},{1,0},{2,3},{3,2},{4,5},{5,4},{6,7},{7,6},{8,9},{9,8},{10,11... | collective-permute-start | bytes 491528 | tf_op jit(solution)/shard_map/ppermute | solution.py:13
  23.1 5.5 %collective-permute-start.1 = (bf16[512]{0:T(512)(128)(2,1)S(1)}, bf16[512]{0:T(512)(128)(2,1)S(1)}, u32[]{:S(2)}, u32[]{:S(2)}) collective-permute-start(bf16[512]{0:T(512)(128)(2,1)S(1)} %get-tuple-element.11), channel_id=1, source_target_pairs={{0,1},{1,0},{2,3},{3,2},{4,5},{5,4},{6,7},{7,6},{8,9},{9,8},{10,11... | collective-permute-start | bytes 3080 | tf_op jit(solution)/shard_map/ppermute | solution.py:13
  25.6 3.4 %collective-permute-start = (bf16[512,160]{0,1:T(8,128)(2,1)S(1)}, bf16[512,160]{0,1:T(8,128)(2,1)S(1)}, u32[]{:S(2)}, u32[]{:S(2)}) collective-permute-start(bf16[512,160]{0,1:T(8,128)(2,1)S(1)} %convolution_convert_fusion.2), channel_id=1, source_target_pairs={{0,1},{1,0},{2,3},{3,2},{4,5},{5,4},{6,7},{7,6},{8,9},{9,8},{10,11... | collective-permute-start | bytes 491528 | tf_op jit(solution)/shard_map/ppermute | solution.py:13
  31.9 5.9 %copy-start.5 = (s32[64]{0:T(128)S(1)}, s32[64]{0:T(128)}, u32[]{:S(2)}) copy-start(s32[64]{0:T(128)} %param.19) | copy-start | bytes 772
  32.0 6.0 %copy-start.4 = (s32[64]{0:T(128)S(1)}, s32[64]{0:T(128)}, u32[]{:S(2)}) copy-start(s32[64]{0:T(128)} %param.18) | copy-start | bytes 772
  32.0 6.0 %copy-start.6 = (s32[64,2]{0,1:T(2,128)S(1)}, s32[64,2]{0,1:T(2,128)}, u32[]{:S(2)}) copy-start(s32[64,2]{0,1:T(2,128)} %param.17) | copy-start | bytes 1540
  33.2 53.2 %all-to-all-start = ((bf16[8,512,160]{1,2,0:T(8,128)(2,1)}), bf16[8,512,160]{1,2,0:T(8,128)(2,1)S(1)}, u32[]{:S(2)}, u32[]{:S(2)}) async-start(bf16[8,512,160]{1,2,0:T(8,128)(2,1)} %broadcast_in_dim.69), calls=%async_computation | async-start | bytes 2621440 | tf_op jit(solution)/shard_map/all_to_all | solution.py:95
  102.7 20.2 %all-to-all-start.1 = ((bf16[64,2,160]{2,1,0:T(2,128)(2,1)}), bf16[64,2,160]{2,1,0:T(2,128)(2,1)S(1)}, u32[]{:S(2)}, u32[]{:S(2)}) async-start(bf16[64,2,160]{2,1,0:T(2,128)(2,1)} %reshape.261), calls=%async_computation.1 | async-start | bytes 131072 | tf_op jit(solution)/shard_map/all_to_all | solution.py:109
  124.0 14.9 %all-to-all-start.2 = ((bf16[64,4,160]{2,1,0:T(4,128)(2,1)}), bf16[64,4,160]{2,1,0:T(4,128)(2,1)S(1)}, u32[]{:S(2)}, u32[]{:S(2)}) async-start(bf16[64,4,160]{2,1,0:T(4,128)(2,1)} %reshape.263), calls=%async_computation.2 | async-start | bytes 262144 | tf_op jit(solution)/shard_map/all_to_all | solution.py:118
Sparse Core Ops, SparseCore 0:
  9.4 83.2 all-gather.1

commit v2 on v1

v2 whole, which is shorter than its diff:
```python
import math

import jax
import jax.numpy as jnp
from jax import lax
from jax.experimental import pallas as pl
from jax.experimental.pallas import tpu as pltpu
from jax.sharding import PartitionSpec as P

HEAD_DIM = 80
CAP = 248
WIDTH = 16
LANES = 128
SCALE = 1.0 / math.sqrt(HEAD_DIM)
MASKED = -1e30

VMEM = pl.BlockSpec(memory_space=pltpu.VMEM)
SMEM = pl.BlockSpec(memory_space=pltpu.SMEM)


def partner(x, axis, apart):
    return lax.ppermute(x, axis, [(i, i ^ 1 << apart) for i in range(lax.axis_size(axis))])


def normalize(values):
    centered = values - jnp.mean(values, axis=-1, keepdims=True)
    variance = jnp.mean(centered * centered, axis=-1, keepdims=True)
    return centered * lax.rsqrt(variance + 1e-06)


def dot(left, right, dims):
    return lax.dot_general(left, right, (dims, ((), ())), preferred_element_type=jnp.float32)


def front_kernel(offsets, patches, row_table, col_table, weight, resid, queries, pairs):
    rows = patches.shape[0]
    side = row_table.shape[0]
    place = lax.axis_index("tok")
    first = place // 2 * 2
    position = place * rows + lax.broadcasted_iota(jnp.int32, (rows, 2 * side), 0)
    start = jnp.where(position >= offsets[first + 1], offsets[first + 1], offsets[first])
    local = position - start
    window = local >> 2
    quarter = local & 3
    half = WIDTH // 2
    row = 2 * (window // half) + (quarter >> 1)
    col = 2 * (window % half) + (quarter & 1)
    lane = lax.broadcasted_iota(jnp.int32, (rows, 2 * side), 1)
    onehot = lane == jnp.where(lane < side, row, col + side)
    tables = jnp.concatenate([row_table[...], col_table[...]], axis=0)
    onehot = jnp.where(onehot, 1.0, 0.0).astype(jnp.bfloat16)
    values = patches[...].astype(jnp.float32) + dot(onehot, tables, ((1,), (0,)))
    resid[...] = values
    normed = normalize(values).astype(jnp.bfloat16)
    width = weight.shape[1]
    wide = weight[...].reshape(3 * width, weight.shape[2])
    out = dot(wide, normed, ((1,), (1,))).astype(jnp.bfloat16)
    queries[...] = out[:width]
    pairs[...] = out[width:]


def attend_kernel(offsets, queries, near, far, out):
    rows = queries.shape[1]
    width = queries.shape[0]
    place = lax.axis_index("tok")
    core = place % 2
    border = offsets[place // 2 * 2 + 1]
    ahead = jnp.where(core == 0, rows, -rows)
    query_pos = place * rows + lax.broadcasted_iota(jnp.int32, (1, rows), 1)
    key_pos = place * rows + lax.broadcasted_iota(jnp.int32, (rows, 1), 0)
    query_side = jnp.where(query_pos >= border, 1, 0)
    near_side = jnp.where(key_pos >= border, 1, 0)
    far_side = jnp.where(key_pos + ahead >= border, 1, 0)
    for head in range(width // HEAD_DIM):
        own = slice(head * HEAD_DIM, (head + 1) * HEAD_DIM)
        value = slice(width + head * HEAD_DIM, width + (head + 1) * HEAD_DIM)
        query = queries[own, :]
        near_scores = dot(near[own, :], query, ((0,), (0,)))
        far_scores = dot(far[own, :], query, ((0,), (0,)))
        near_scores = jnp.where(near_side == query_side, near_scores * SCALE, MASKED)
        far_scores = jnp.where(far_side == query_side, far_scores * SCALE, MASKED)
        top = jnp.maximum(
            jnp.max(near_scores, axis=0, keepdims=True), jnp.max(far_scores, axis=0, keepdims=True)
        )
        near_expo = jnp.exp(near_scores - top)
        far_expo = jnp.exp(far_scores - top)
        total = jnp.sum(near_expo, axis=0, keepdims=True) + jnp.sum(far_expo, axis=0, keepdims=True)
        mixed = dot(near[value, :], near_expo.astype(jnp.bfloat16), ((1,), (0,)))
        mixed += dot(far[value, :], far_expo.astype(jnp.bfloat16), ((1,), (0,)))
        mixed = (mixed / total).astype(jnp.bfloat16)
        slot = pl.multiple_of(jnp.where(core == head, 0, HEAD_DIM), 16)
        for copy in range(out.shape[0]):
            out[copy, pl.ds(slot, HEAD_DIM), :] = mixed


def merge_kernel(gathered, own_weight, other_weight, resid, merge_weight, out, attended, normed):
    group = gathered.shape[0]
    depth = group * HEAD_DIM
    for head in range(2):
        for place in range(group):
            attended[pl.ds(head * depth + place * HEAD_DIM, HEAD_DIM), :] = gathered[
                place, head * HEAD_DIM : (head + 1) * HEAD_DIM, :
            ]
    total = resid[...] + dot(attended[:depth, :], own_weight[...], ((0,), (0,)))
    total += dot(attended[depth:, :], other_weight[...], ((0,), (0,)))
    rows, width = total.shape
    total = normalize(total)
    for tile in range(width // LANES):
        normed[tile] = total[:, tile * LANES : (tile + 1) * LANES]
    projected = jnp.zeros(out.shape, jnp.float32)
    for quarter in range(4):
        part = [
            normed[tile, pl.ds(quarter, rows // 4, stride=4), :] for tile in range(width // LANES)
        ]
        part = jnp.concatenate(part, axis=1).astype(jnp.bfloat16)
        weight = merge_weight[:, quarter * width : (quarter + 1) * width]
        projected += dot(part, weight, ((1,), (1,)))
    out[...] = projected.astype(out.dtype)


def on_device(
    patches,
    row_table,
    col_table,
    qkv_weight,
    out_weight,
    merge_weight,
    segment_ids,
    image_grids,
    image_offsets,
    owners,
):
    block_rows, width = patches.shape
    width_here = qkv_weight.shape[1]
    group = lax.axis_size("head")
    places = lax.axis_size("tok")
    place = lax.axis_index("tok")
    params = pltpu.CompilerParams(vmem_limit_bytes=50 * 2**20)

    half_weight = lax.dynamic_slice_in_dim(out_weight, place % 2 * HEAD_DIM, HEAD_DIM, 0)
    own_weight = lax.all_gather(half_weight, "head", axis=0, tiled=True)
    other_weight = partner(own_weight, "tok", 0)

    resid, queries, near = pl.pallas_call(
        front_kernel,
        out_shape=(
            jax.ShapeDtypeStruct((block_rows, width), jnp.float32),
            jax.ShapeDtypeStruct((width_here, block_rows), jnp.bfloat16),
            jax.ShapeDtypeStruct((2 * width_here, block_rows), jnp.bfloat16),
        ),
        in_specs=[SMEM, VMEM, VMEM, VMEM, VMEM],
        out_specs=(VMEM, VMEM, VMEM),
        compiler_params=params,
    )(image_offsets, patches, row_table, col_table, qkv_weight)
    far = partner(near, "tok", 0)
    sent = pl.pallas_call(
        attend_kernel,
        out_shape=jax.ShapeDtypeStruct((group, width_here, block_rows), jnp.bfloat16),
        in_specs=[SMEM, VMEM, VMEM, VMEM],
        out_specs=VMEM,
        compiler_params=params,
    )(image_offsets, queries, near, far)
    gathered = lax.all_to_all(sent, "head", 0, 0, tiled=True)
    projected = pl.pallas_call(
        merge_kernel,
        out_shape=jax.ShapeDtypeStruct((block_rows // 4, width_here), jnp.bfloat16),
        in_specs=[VMEM, VMEM, VMEM, VMEM, VMEM],
        out_specs=VMEM,
        scratch_shapes=[
            pltpu.VMEM((group * width_here, block_rows), jnp.bfloat16),
            pltpu.VMEM((width // LANES, block_rows, LANES), jnp.float32),
        ],
        compiler_params=params,
    )(gathered, own_weight, other_weight, resid, merge_weight)

    rows_here = projected.shape[0]
    share = rows_here // places
    spread = lax.all_to_all(projected.reshape(places, share, width_here), "tok", 0, 0, tiled=True)
    place_ids = jnp.arange(places, dtype=jnp.int32)
    wanted = (owners.reshape(-1, 2)[None, :, :] == place_ids[:, None, None]).any(axis=2)
    pieces = jnp.dot(
        wanted.astype(jnp.bfloat16),
        spread.reshape(places // 2, 2 * share * width_here),
        preferred_element_type=jnp.float32,
    ).astype(jnp.bfloat16)
    pair_rows = lax.all_to_all(
        pieces.reshape(places, 2 * share, width_here), "tok", 0, 0, tiled=True
    ).reshape(2 * rows_here, width_here)

    image_ids = jnp.arange(owners.shape[0], dtype=jnp.int32)
    owner_mask = owners == place
    image_id = jnp.sum(jnp.where(owner_mask, image_ids, 0))
    first_row = jnp.sum(jnp.where(owner_mask, image_offsets, 0)) // 4
    first_row = first_row - (image_id // 2) * 2 * rows_here
    tokens = image_grids[:, 0] * image_grids[:, 1]
    merged_count = jnp.sum(jnp.where(owner_mask, tokens, 0)) // 4
    slot_ids = jnp.arange(CAP, dtype=jnp.int32)
    got_ids = jnp.arange(2 * rows_here, dtype=jnp.int32)
    row_of = (got_ids // share % 2) * rows_here + got_ids // (2 * share) * share + got_ids % share
    slot_of = row_of - first_row
    selector = (slot_of[None, :] == slot_ids[:, None]) & (slot_ids < merged_count)[:, None]
    owner_rows = jnp.dot(
        selector.astype(jnp.bfloat16), pair_rows, preferred_element_type=jnp.float32
    )
    return owner_rows.astype(jnp.bfloat16)


def solution(mesh):
    placed = (
        P("tok", None),
        P(),
        P(),
        P(None, "head", None),
        P("head", None),
        P("head", None),
        P("tok"),
        P(),
        P(),
        P(),
    )
    return jax.shard_map(
        on_device, mesh=mesh, in_specs=placed, out_specs=P("tok", "head"), check_vma=False
    )
```

time: 147 us -> 140 us (0.952)
  Pallas kernels: 0 us -> 14.6 us
  matrix products: 15.1 us -> 1.15 us
  waiting for transfers between devices: 67.3 us -> 56 us
  local copies, waits for them, and re-layouts: 6.95 us -> 11.3 us
  other arithmetic: 3.64 us -> 0.84 us
  starting transfers between devices: 32.6 us -> 34.3 us
    all_to_all x1, waiting for transfers between devices: 44.9 us -> 0.01 us  [on_device(): gathered = lax.all_to_all(sent, 'head', 0, 0, tiled=True)]
    all_gather x1, waiting for transfers between devices: 6.37 us -> 39.9 us  [on_device(): own_weight = lax.all_gather(half_weight, 'head', axis=0, tiled=True)]
    pallas_call x0 -> x3, Pallas kernels: none -> 14.6 us  [the longest x1 6.84 us: on_device(): pl.pallas_call(merge_kernel, out_shape=jax.ShapeDtypeStruct((block_rows /...]
    dot_general x9 -> x0, matrix products: 13.9 us -> none  [the longest x1 4.83 us: on_device(): jnp.einsum('ztf,zfd->td', gathered, full_weight.reshape(group, width_here...]
    unnamed x16 -> x22, local copies, waits for them, and re-layouts: 1.49 us -> 8.74 us
    ppermute x3 -> x2, starting transfers between devices: 13.1 us -> 14.9 us  [partner(): lax.ppermute(x, axis, [(i, i ^ 1 << apart) for i in range(lax.axis_size(a...]
    reshape x1 -> x0, local copies, waits for them, and re-layouts: 1.68 us -> none  [on_device(): merged = normed_two.reshape(block_rows // 4, 4 * normed_two.shape[1])]
    reduce_sum x4 -> x1, other arithmetic: 2.32 us -> 0.75 us  [on_device(): merged_count = jnp.sum(jnp.where(owner_mask, tokens, 0)) // 4]
  transfers between devices with their start and end apart: 7 -> 6, of which waited for: 4 -> 4; matrix products, arithmetic and copies ran while one was open for 8% -> 1% of each run, Pallas kernels for 0% -> 6%
where the time goes in v2:
time: 140 us
  waiting for transfers between devices  56 us (40%)
  starting transfers between devices  34.3 us (24%)
  between operations  21.5 us (15%)
  Pallas kernels  14.6 us (10%)
  local copies, waits for them, and re-layouts  11.3 us (8%)
    all_gather x1, waiting for transfers between devices, on_device(): own_weight = lax.all_gather(half_weight, 'head', axis=0, tiled=True)  39.9 us
    ppermute x2, starting transfers between devices, partner(): lax.ppermute(x, axis, [(i, i ^ 1 << apart) for i in range(lax.axis_size(a...  14.9 us
    all_to_all x1, starting transfers between devices, on_device(): lax.all_to_all(projected.reshape(places, share, width_here), 'tok', 0, 0,...  10.2 us
    all_to_all x1, waiting for transfers between devices, on_device(): lax.all_to_all(projected.reshape(places, share, width_here), 'tok', 0, 0,...  9.7 us
    unnamed x22, local copies, waits for them, and re-layouts  8.74 us
    pallas_call x1, Pallas kernels, on_device(): pl.pallas_call(merge_kernel, out_shape=jax.ShapeDtypeStruct((block_rows /...  6.84 us
    all_to_all x1, waiting for transfers between devices, on_device(): lax.all_to_all(pieces.reshape(places, 2 * share, width_here), 'tok', 0, 0...  5.14 us
    all_to_all x1, starting transfers between devices, on_device(): gathered = lax.all_to_all(sent, 'head', 0, 0, tiled=True)  4.79 us
  transfers between devices with their start and end apart: 6, of which 4 were waited for; matrix products, arithmetic and copies ran while one was open for 1% of the time, Pallas kernels for 6%

profile of v2, /device:TPU:1, one launch (start us, length us, event | category | flops | bytes accessed | tf_op | source)
XLA Modules:
  0.0 139.6 jit_solution(10267287050032624175)
XLA Ops:
  6.5 0.0 copy-start
  6.5 0.0 all-gather.2.cloned.1.call-start
  6.5 1.0 copy-done
  7.5 0.7 constant_dynamic-slice_fusion
  8.2 0.0 all-gather.2.cloned.1.call-update
  8.3 0.0 copy-start.2
  8.3 1.3 copy-done.2
  9.6 0.0 copy-start.3
  9.6 1.3 copy-done.3
  10.9 0.0 copy-start.4
  10.9 0.9 copy-done.4
  11.8 0.0 copy-start.5
  11.8 0.9 copy-done.5
  12.7 0.0 copy-start.6
  12.7 0.7 copy-done.6
  13.4 3.9 %shard_map.91 = (f32[512,1280]{1,0:T(8,128)}, bf16[160,512]{1,0:T(8,128)(2,1)S(1)}, bf16[320,512]{1,0:T(8,128)(2,1)S(1)}) custom-call(s32[64]{0:T(128)S(1)} %copy-done.6, bf16[512,1280]{1,0:T(8,128)(2,1)S(1)} %copy-done.2, bf16[64,1280]{1,0:T(8,128)(2,1)S(1)} %copy-done.4, bf16[64,1280]{1,0:T(8,128)(2,1)S(1)} %copy-done.5, bf16[3,160,1280]{2,1,0:T(8,128)(2,1)S(1)} %copy-done.3), custom_call_target="tpu_custom_call" | custom-call | tf_op jit(solution)/shard_map/pallas_call | solution.py:144
  17.3 8.8 %collective-permute-start = (bf16[320,512]{1,0:T(8,128)(2,1)S(1)}, bf16[320,512]{1,0:T(8,128)(2,1)S(1)}, u32[]{:S(2)}, u32[]{:S(2)}) collective-permute-start(bf16[320,512]{1,0:T(8,128)(2,1)S(1)} %get-tuple-element.9.near), channel_id=1, source_target_pairs={{0,1},{1,0},{2,3},{3,2},{4,5},{5,4},{6,7},{7,6},{8,9},{9,8},{10,11... | collective-permute-start | bytes 983048 | tf_op jit(solution)/shard_map/ppermute | solution.py:22
  26.1 1.2 collective-permute-done.far
  27.3 3.8 %shard_map.92 = bf16[8,160,512]{2,1,0:T(8,128)(2,1)} custom-call(s32[64]{0:T(128)S(1)} %copy-done.6, bf16[160,512]{1,0:T(8,128)(2,1)S(1)} %get-tuple-element.8.queries, bf16[320,512]{1,0:T(8,128)(2,1)S(1)} %get-tuple-element.9.near, bf16[320,512]{1,0:T(8,128)(2,1)S(1)} %collective-permute-done.far), custom_call_target="tpu_custom_call" | custom-call | tf_op jit(solution)/shard_map/pallas_call | solution.py:156
  31.1 0.0 copy-start.9
  31.1 0.0 copy-start.7
  31.1 0.0 copy-start.10
  31.1 4.8 %all-to-all-start = ((bf16[8,160,512]{2,1,0:T(8,128)(2,1)}), bf16[8,160,512]{2,1,0:T(8,128)(2,1)S(1)}, u32[]{:S(2)}, u32[]{:S(2)}) async-start(bf16[8,160,512]{2,1,0:T(8,128)(2,1)} %shard_map.92), calls=%async_computation | async-start | bytes 2621440 | tf_op jit(solution)/shard_map/all_to_all | solution.py:163
  35.9 39.9 %all-gather.2.cloned.1.call-done.own_weight = bf16[640,1280]{1,0:T(8,128)(2,1)} async-done(((bf16[80,1280]{1,0:T(8,128)(2,1)}), bf16[640,1280]{1,0:T(8,128)(2,1)}) %all-gather.2.cloned.1.call-update) | async-done | bytes 1638416 | tf_op jit(solution)/shard_map/all_gather | solution.py:141
  75.8 6.1 %collective-permute-start.1 = (bf16[640,1280]{1,0:T(8,128)(2,1)}, bf16[640,1280]{1,0:T(8,128)(2,1)S(1)}, u32[]{:S(2)}, u32[]{:S(2)}) collective-permute-start(bf16[640,1280]{1,0:T(8,128)(2,1)} %all-gather.2.cloned.1.call-done.own_weight), channel_id=1, source_target_pairs={{0,1},{1,0},{2,3},{3,2},{4,5},{5,4},{6,7},{7,6},{8,9},{9,8},{10,11... | collective-permute-start | bytes 4915208 | tf_op jit(solution)/shard_map/ppermute | solution.py:22
  81.9 0.0 copy-done.9
  81.9 0.1 eq.44
  82.0 0.0 copy-done.7
  82.0 0.0 copy-done.10
  82.1 0.8 fusion.14
  84.8 0.1 copy.10
  85.5 0.0 all-to-all-done.gathered
  85.5 0.0 collective-permute-done.1.other_weight
  85.5 0.0 copy-start.8
  85.5 1.2 copy-done.8
  86.7 1.4 %copy-done.1 = bf16[640,1280]{1,0:T(8,128)(2,1)S(1)} copy-done((bf16[640,1280]{1,0:T(8,128)(2,1)S(1)}, bf16[640,1280]{1,0:T(8,128)(2,1)}, u32[]{:S(2)}) %copy-start.1) | copy-done | bytes 1638424
  88.2 6.8 %shard_map.93 = bf16[128,160]{1,0:T(8,128)(2,1)S(1)} custom-call(bf16[8,160,512]{2,1,0:T(8,128)(2,1)S(1)} %all-to-all-done.gathered, bf16[640,1280]{1,0:T(8,128)(2,1)S(1)} %copy-done.1, bf16[640,1280]{1,0:T(8,128)(2,1)} %copy-done.8, f32[512,1280]{1,0:T(8,128)} %get-tuple-element.10.resid, bf16[160,5120]{1,0:T(8,128)(2,1)} %merge_weight.1), custom_call_target="tpu_custom_call" | custom-call | tf_op jit(solution)/shard_map/pallas_call | solution.py:164
  95.0 0.7 reshape.62
  95.7 10.2 %all-to-all-start.1 = ((bf16[64,2,160]{2,1,0:T(2,128)(2,1)}), bf16[64,2,160]{2,1,0:T(2,128)(2,1)S(1)}, u32[]{:S(2)}, u32[]{:S(2)}) async-start(bf16[64,2,160]{2,1,0:T(2,128)(2,1)} %reshape.62), calls=%async_computation.1 | async-start | bytes 131072 | tf_op jit(solution)/shard_map/all_to_all | solution.py:178
  105.9 0.1 fusion.4
  106.0 9.7 %all-to-all-done.1 = bf16[64,2,160]{2,1,0:T(2,128)(2,1)S(1)} async-done(((bf16[64,2,160]{2,1,0:T(2,128)(2,1)}), bf16[64,2,160]{2,1,0:T(2,128)(2,1)S(1)}, u32[]{:S(2)}, u32[]{:S(2)}) %all-to-all-start.1) | async-done | bytes 40992 | tf_op jit(solution)/shard_map/all_to_all | solution.py:178
  115.7 0.1 reshape.63
  115.8 0.2 convolution_convert_fusion.1
  116.0 0.8 reshape.64
  116.8 4.4 %all-to-all-start.2 = ((bf16[64,4,160]{2,1,0:T(4,128)(2,1)}), bf16[64,4,160]{2,1,0:T(4,128)(2,1)S(1)}, u32[]{:S(2)}, u32[]{:S(2)}) async-start(bf16[64,4,160]{2,1,0:T(4,128)(2,1)} %reshape.64), calls=%async_computation.2 | async-start | bytes 262144 | tf_op jit(solution)/shard_map/all_to_all | solution.py:186
  126.6 5.1 %all-to-all-done.2 = bf16[64,4,160]{2,1,0:T(4,128)(2,1)S(1)} async-done(((bf16[64,4,160]{2,1,0:T(4,128)(2,1)}), bf16[64,4,160]{2,1,0:T(4,128)(2,1)S(1)}, u32[]{:S(2)}, u32[]{:S(2)}) %all-to-all-start.2) | async-done | bytes 81952 | tf_op jit(solution)/shard_map/all_to_all | solution.py:186
  131.7 0.1 reshape.65
  131.8 0.9 convolution_convert_fusion
  (3 shorter events, 0.0 us)
Async XLA Ops:
  6.5 1.0 copy-start
  6.5 69.3 %all-gather.2.cloned.1.call-start = ((), (), s32[]{:S(2)}) async-start(), calls=%async_computation.3 | async-start | bytes 1843200 | tf_op jit(solution)/shard_map/all_gather | solution.py:141
  8.3 1.3 copy-start.2
  9.6 1.3 copy-start.3
  10.9 0.9 copy-start.4
  11.8 0.9 copy-start.5
  12.7 0.7 copy-start.6
  17.3 10.0 %collective-permute-start = (bf16[320,512]{1,0:T(8,128)(2,1)S(1)}, bf16[320,512]{1,0:T(8,128)(2,1)S(1)}, u32[]{:S(2)}, u32[]{:S(2)}) collective-permute-start(bf16[320,512]{1,0:T(8,128)(2,1)S(1)} %get-tuple-element.9.near), channel_id=1, source_target_pairs={{0,1},{1,0},{2,3},{3,2},{4,5},{5,4},{6,7},{7,6},{8,9},{9,8},{10,11... | collective-permute-start | bytes 983048 | tf_op jit(solution)/shard_map/ppermute | solution.py:22
  31.1 50.8 %copy-start.9 = (s32[64]{0:T(128)S(1)}, s32[64]{0:T(128)}, u32[]{:S(2)}) copy-start(s32[64]{0:T(128)} %param.18) | copy-start | bytes 772
  31.1 50.9 %copy-start.7 = (s32[64]{0:T(128)S(1)}, s32[64]{0:T(128)}, u32[]{:S(2)}) copy-start(s32[64]{0:T(128)} %offsets.3) | copy-start | bytes 772
  31.1 50.9 %copy-start.10 = (s32[64,2]{0,1:T(2,128)S(1)}, s32[64,2]{0,1:T(2,128)}, u32[]{:S(2)}) copy-start(s32[64,2]{0,1:T(2,128)} %param.16) | copy-start | bytes 1540
  31.1 54.4 %all-to-all-start = ((bf16[8,160,512]{2,1,0:T(8,128)(2,1)}), bf16[8,160,512]{2,1,0:T(8,128)(2,1)S(1)}, u32[]{:S(2)}, u32[]{:S(2)}) async-start(bf16[8,160,512]{2,1,0:T(8,128)(2,1)} %shard_map.92), calls=%async_computation | async-start | bytes 2621440 | tf_op jit(solution)/shard_map/all_to_all | solution.py:163
  75.8 9.7 %collective-permute-start.1 = (bf16[640,1280]{1,0:T(8,128)(2,1)}, bf16[640,1280]{1,0:T(8,128)(2,1)S(1)}, u32[]{:S(2)}, u32[]{:S(2)}) collective-permute-start(bf16[640,1280]{1,0:T(8,128)(2,1)} %all-gather.2.cloned.1.call-done.own_weight), channel_id=1, source_target_pairs={{0,1},{1,0},{2,3},{3,2},{4,5},{5,4},{6,7},{7,6},{8,9},{9,8},{10,11... | collective-permute-start | bytes 4915208 | tf_op jit(solution)/shard_map/ppermute | solution.py:22
  85.5 1.2 copy-start.8
  86.7 1.4 %copy-start.1 = (bf16[640,1280]{1,0:T(8,128)(2,1)S(1)}, bf16[640,1280]{1,0:T(8,128)(2,1)}, u32[]{:S(2)}) copy-start(bf16[640,1280]{1,0:T(8,128)(2,1)} %all-gather.2.cloned.1.call-done.own_weight) | copy-start | bytes 4915204
  95.7 20.0 %all-to-all-start.1 = ((bf16[64,2,160]{2,1,0:T(2,128)(2,1)}), bf16[64,2,160]{2,1,0:T(2,128)(2,1)S(1)}, u32[]{:S(2)}, u32[]{:S(2)}) async-start(bf16[64,2,160]{2,1,0:T(2,128)(2,1)} %reshape.62), calls=%async_computation.1 | async-start | bytes 131072 | tf_op jit(solution)/shard_map/all_to_all | solution.py:178
  116.8 14.9 %all-to-all-start.2 = ((bf16[64,4,160]{2,1,0:T(4,128)(2,1)}), bf16[64,4,160]{2,1,0:T(4,128)(2,1)S(1)}, u32[]{:S(2)}, u32[]{:S(2)}) async-start(bf16[64,4,160]{2,1,0:T(4,128)(2,1)} %reshape.64), calls=%async_computation.2 | async-start | bytes 262144 | tf_op jit(solution)/shard_map/all_to_all | solution.py:186
Sparse Core Ops, SparseCore 0:
  9.4 66.3 all-gather.1

commit v3 on v2

v3 whole, which is shorter than its diff:
```python
import math

import jax
import jax.numpy as jnp
from jax import lax
from jax.experimental import pallas as pl
from jax.experimental.pallas import tpu as pltpu
from jax.sharding import PartitionSpec as P

HEAD_DIM = 80
CAP = 248
WIDTH = 16
LANES = 128
RING = 8
SCALE = 1.0 / math.sqrt(HEAD_DIM)
MASKED = -1e30

VMEM = pl.BlockSpec(memory_space=pltpu.VMEM)
SMEM = pl.BlockSpec(memory_space=pltpu.SMEM)
HBM = pl.BlockSpec(memory_space=pltpu.HBM)


def partner(x, axis, apart):
    return lax.ppermute(x, axis, [(i, i ^ 1 << apart) for i in range(lax.axis_size(axis))])


def normalize(values):
    centered = values - jnp.mean(values, axis=-1, keepdims=True)
    variance = jnp.mean(centered * centered, axis=-1, keepdims=True)
    return centered * lax.rsqrt(variance + 1e-06)


def dot(left, right, dims):
    return lax.dot_general(left, right, (dims, ((), ())), preferred_element_type=jnp.float32)


def front_kernel(
    offsets,
    patches_hbm,
    row_hbm,
    col_hbm,
    weight_hbm,
    resid_hbm,
    queries,
    pairs,
    resid,
    patches,
    tables,
    weight,
    sems,
):
    rows = patches.shape[0]
    side = tables.shape[0] // 2
    copies = [
        pltpu.make_async_copy(row_hbm, tables.at[pl.ds(0, side), :], sems.at[0]),
        pltpu.make_async_copy(col_hbm, tables.at[pl.ds(side, side), :], sems.at[1]),
        pltpu.make_async_copy(patches_hbm, patches, sems.at[2]),
        pltpu.make_async_copy(weight_hbm, weight, sems.at[3]),
    ]
    for copy in copies:
        copy.start()
    place = lax.axis_index("tok")
    first = place // 2 * 2
    position = place * rows + lax.broadcasted_iota(jnp.int32, (rows, 2 * side), 0)
    start = jnp.where(position >= offsets[first + 1], offsets[first + 1], offsets[first])
    local = position - start
    window = local >> 2
    quarter = local & 3
    half = WIDTH // 2
    row = 2 * (window // half) + (quarter >> 1)
    col = 2 * (window % half) + (quarter & 1)
    lane = lax.broadcasted_iota(jnp.int32, (rows, 2 * side), 1)
    onehot = lane == jnp.where(lane < side, row, col + side)
    onehot = jnp.where(onehot, 1.0, 0.0).astype(jnp.bfloat16)
    copies[0].wait()
    copies[1].wait()
    embedded = dot(onehot, tables[...], ((1,), (0,)))
    copies[2].wait()
    values = patches[...].astype(jnp.float32) + embedded
    for tile in range(resid.shape[0]):
        resid[tile] = values[:, tile * LANES : (tile + 1) * LANES]
    resid_copy = pltpu.make_async_copy(resid, resid_hbm, sems.at[4])
    resid_copy.start()
    normed = normalize(values).astype(jnp.bfloat16)
    copies[3].wait()
    width = weight.shape[1]
    wide = weight[...].reshape(3 * width, weight.shape[2])
    out = dot(wide, normed, ((1,), (1,))).astype(jnp.bfloat16)
    queries[...] = out[:width]
    pairs[...] = out[width:]
    resid_copy.wait()


def attend_kernel(offsets, queries, near, far, out):
    rows = queries.shape[1]
    width = queries.shape[0]
    place = lax.axis_index("tok")
    core = place % 2
    border = offsets[place // 2 * 2 + 1]
    ahead = jnp.where(core == 0, rows, -rows)
    query_pos = place * rows + lax.broadcasted_iota(jnp.int32, (1, rows), 1)
    key_pos = place * rows + lax.broadcasted_iota(jnp.int32, (rows, 1), 0)
    query_side = jnp.where(query_pos >= border, 1, 0)
    near_side = jnp.where(key_pos >= border, 1, 0)
    far_side = jnp.where(key_pos + ahead >= border, 1, 0)
    for head in range(width // HEAD_DIM):
        own = slice(head * HEAD_DIM, (head + 1) * HEAD_DIM)
        value = slice(width + head * HEAD_DIM, width + (head + 1) * HEAD_DIM)
        query = queries[own, :]
        near_scores = dot(near[own, :], query, ((0,), (0,)))
        far_scores = dot(far[own, :], query, ((0,), (0,)))
        near_scores = jnp.where(near_side == query_side, near_scores * SCALE, MASKED)
        far_scores = jnp.where(far_side == query_side, far_scores * SCALE, MASKED)
        top = jnp.maximum(
            jnp.max(near_scores, axis=0, keepdims=True), jnp.max(far_scores, axis=0, keepdims=True)
        )
        near_expo = jnp.exp(near_scores - top)
        far_expo = jnp.exp(far_scores - top)
        total = jnp.sum(near_expo, axis=0, keepdims=True) + jnp.sum(far_expo, axis=0, keepdims=True)
        mixed = dot(near[value, :], near_expo.astype(jnp.bfloat16), ((1,), (0,)))
        mixed += dot(far[value, :], far_expo.astype(jnp.bfloat16), ((1,), (0,)))
        mixed = (mixed / total).astype(jnp.bfloat16)
        for copy in range(out.shape[0]):
            out[copy, own, :] = mixed


def merge_kernel(
    gathered,
    own_weight,
    other_hbm,
    resid_hbm,
    merge_hbm,
    out,
    other_weight,
    resid,
    merge_weight,
    total,
    sems,
):
    other_copy = pltpu.make_async_copy(other_hbm, other_weight, sems.at[0])
    resid_copy = pltpu.make_async_copy(resid_hbm, resid, sems.at[1])
    merge_copy = pltpu.make_async_copy(merge_hbm, merge_weight, sems.at[2])
    other_copy.start()
    resid_copy.start()
    merge_copy.start()
    core = lax.axis_index("tok") % 2
    group, depth, rows = gathered.shape
    attended = gathered[...].reshape(group * depth, rows)
    tiles = resid.shape[0]
    for weight, half in ((own_weight, core), (other_weight, 1 - core)):
        if weight is other_weight:
            other_copy.wait()
        part = dot(attended, weight[...], ((0,), (0,)))
        if weight is own_weight:
            resid_copy.wait()
        for tile in range(tiles // 2):
            place = half * (tiles // 2) + tile
            total[place] = resid[place] + part[:, tile * LANES : (tile + 1) * LANES]
    values = jnp.concatenate([total[tile] for tile in range(tiles)], axis=1)
    normed = normalize(values)
    for tile in range(tiles):
        total[tile] = normed[:, tile * LANES : (tile + 1) * LANES]
    width = tiles * LANES
    merge_copy.wait()
    projected = jnp.zeros(out.shape[1:], jnp.float32)
    for quarter in range(4):
        part = [total[tile, pl.ds(quarter, rows // 4, stride=4), :] for tile in range(tiles)]
        part = jnp.concatenate(part, axis=1).astype(jnp.bfloat16)
        weight = merge_weight[:, quarter * width : (quarter + 1) * width]
        projected += dot(weight, part, ((1,), (1,)))
    projected = projected.astype(out.dtype)
    for copy in range(out.shape[0]):
        out[copy] = projected


def pick_kernel(wanted, blocks, out):
    for slot in range(out.shape[0]):
        out[slot] = blocks[wanted[slot]]


def deliver_kernel(facts, blocks, out):
    source = 2 * facts[0]
    pair = jnp.concatenate([blocks[source], blocks[source + 1]], axis=1)
    shape = (pair.shape[1], out.shape[1])
    row = lax.broadcasted_iota(jnp.int32, shape, 0) - facts[1]
    slot = lax.broadcasted_iota(jnp.int32, shape, 1)
    chosen = row == jnp.where(slot < facts[2], slot, -shape[0])
    chosen = jnp.where(chosen, 1.0, 0.0).astype(jnp.bfloat16)
    out[...] = dot(pair, chosen, ((1,), (0,))).astype(out.dtype)


def on_device(
    patches,
    row_table,
    col_table,
    qkv_weight,
    out_weight,
    merge_weight,
    segment_ids,
    image_grids,
    image_offsets,
    owners,
):
    block_rows, width = patches.shape
    width_here = qkv_weight.shape[1]
    group = lax.axis_size("head")
    places = lax.axis_size("tok")
    place = lax.axis_index("tok")
    params = pltpu.CompilerParams(vmem_limit_bytes=24 * 2**20)
    at_hbm = lambda x: pltpu.with_memory_space_constraint(x, pltpu.HBM)

    sides = places // (RING * 2)
    tok_of = [[[(x * RING + y) * 2 + c for c in range(2)] for y in range(RING)] for x in range(sides)]
    rings_y = [[tok_of[x][y][c] for y in range(RING)] for x in range(sides) for c in range(2)]
    rings_x = [[tok_of[x][y][c] for x in range(sides)] for y in range(RING) for c in range(2)]
    planes = [[tok_of[x][y][c] for x in range(sides) for c in range(2)] for y in range(RING)]
    my_x = place // (2 * RING)
    my_y = place // 2 % RING
    core = place % 2

    depth, columns = width_here // sides, width // 2
    piece = lax.dynamic_slice(out_weight, (my_x * depth, core * columns), (depth, columns))
    pieces = jnp.broadcast_to(piece[None], (group, depth, columns))
    pieces = lax.all_to_all(pieces, "head", 0, 0, tiled=True)

    resid, queries, near = pl.pallas_call(
        front_kernel,
        out_shape=(
            pltpu.HBM((width // LANES, block_rows, LANES), jnp.float32),
            jax.ShapeDtypeStruct((width_here, block_rows), jnp.bfloat16),
            jax.ShapeDtypeStruct((2 * width_here, block_rows), jnp.bfloat16),
        ),
        in_specs=[SMEM, HBM, HBM, HBM, HBM],
        out_specs=(HBM, VMEM, VMEM),
        scratch_shapes=[
            pltpu.VMEM((width // LANES, block_rows, LANES), jnp.float32),
            pltpu.VMEM(patches.shape, jnp.bfloat16),
            pltpu.VMEM((2 * row_table.shape[0], width), jnp.bfloat16),
            pltpu.VMEM(qkv_weight.shape, jnp.bfloat16),
            pltpu.SemaphoreType.DMA((5,)),
        ],
        compiler_params=params,
        cost_estimate=pl.CostEstimate(
            flops=3 * 2 * block_rows * width * width_here, bytes_accessed=8 * 2**20, transcendentals=0
        ),
    )(image_offsets, *map(at_hbm, (patches, row_table, col_table, qkv_weight)))
    far = partner(near, "tok", 0)
    sent = pl.pallas_call(
        attend_kernel,
        out_shape=jax.ShapeDtypeStruct((group, width_here, block_rows), jnp.bfloat16),
        in_specs=[SMEM, VMEM, VMEM, VMEM],
        out_specs=VMEM,
        compiler_params=params,
    )(image_offsets, queries, near, far)
    pieces, sent = lax.optimization_barrier((pieces, sent))
    own_weight = lax.all_gather(pieces, "tok", axis=0, axis_index_groups=rings_x)
    own_weight = own_weight.transpose(1, 0, 2, 3).reshape(group * width_here, columns)
    other_weight = partner(own_weight, "tok", 0)

    gathered = lax.all_to_all(sent, "head", 0, 0, tiled=True)
    rows_here = block_rows // 4
    blocks_shape = jax.ShapeDtypeStruct((RING, width_here, rows_here), jnp.bfloat16)
    projected = pl.pallas_call(
        merge_kernel,
        out_shape=blocks_shape,
        in_specs=[VMEM, VMEM, HBM, HBM, HBM],
        out_specs=VMEM,
        scratch_shapes=[
            pltpu.VMEM(other_weight.shape, jnp.bfloat16),
            pltpu.VMEM((width // LANES, block_rows, LANES), jnp.float32),
            pltpu.VMEM(merge_weight.shape, jnp.bfloat16),
            pltpu.VMEM((width // LANES, block_rows, LANES), jnp.float32),
            pltpu.SemaphoreType.DMA((3,)),
        ],
        compiler_params=params,
    )(gathered, own_weight, *map(at_hbm, (other_weight, resid, merge_weight)))

    image_ids = jnp.arange(owners.shape[0], dtype=jnp.int32)
    place_ids = jnp.arange(places, dtype=jnp.int32)
    image_of = jnp.sum(jnp.where(owners[None, :] == place_ids[:, None], image_ids[None, :], 0), axis=1)
    pair_y = (image_of // 2 % RING).reshape(sides, RING, 2)
    wanted = jnp.sum(
        jnp.where((jnp.arange(RING) == my_y)[None, :, None], pair_y, 0), axis=1
    ).reshape(2 * sides)
    mine = owners == place
    tokens = image_grids[:, 0] * image_grids[:, 1]
    first_token = image_offsets - image_ids // 2 * (2 * block_rows)
    facts = jnp.stack([image_ids // 2 // RING, first_token // 4, tokens // 4])
    facts = jnp.sum(jnp.where(mine[None, :], facts, 0), axis=1)

    blocks = lax.all_to_all(projected, "tok", 0, 0, axis_index_groups=rings_y, tiled=True)
    blocks = pl.pallas_call(
        pick_kernel,
        out_shape=jax.ShapeDtypeStruct((2 * sides, width_here, rows_here), jnp.bfloat16),
        in_specs=[SMEM, VMEM],
        out_specs=VMEM,
        compiler_params=params,
    )(wanted, blocks)
    blocks = lax.all_to_all(blocks, "tok", 0, 0, axis_index_groups=planes, tiled=True)
    return pl.pallas_call(
        deliver_kernel,
        out_shape=jax.ShapeDtypeStruct((width_here, CAP), jnp.bfloat16),
        in_specs=[SMEM, VMEM],
        out_specs=VMEM,
        compiler_params=params,
    )(facts, blocks).T


def solution(mesh):
    placed = (
        P("tok", None),
        P(),
        P(),
        P(None, "head", None),
        P("head", None),
        P("head", None),
        P("tok"),
        P(),
        P(),
        P(),
    )
    return jax.shard_map(
        on_device, mesh=mesh, in_specs=placed, out_specs=P("tok", "head"), check_vma=False
    )
```

time: 140 us -> 124 us (0.89)
  between operations: 21.5 us -> 13.5 us
  local copies, waits for them, and re-layouts: 11.3 us -> 4.8 us
  Pallas kernels: 14.6 us -> 17.6 us
  waiting for transfers between devices: 56 us -> 53.6 us
    all_gather x1, waiting for transfers between devices: 39.9 us -> 26.9 us  [on_device(): lax.all_gather(pieces, 'tok', axis=0, axis_index_groups=rings_x)]
    ppermute x2, starting transfers between devices: 14.9 us -> 5.45 us  [partner(): lax.ppermute(x, axis, [(i, i ^ 1 << apart) for i in range(lax.axis_size(a...]
    all_to_all x2 -> x3, starting transfers between devices: 14.6 us -> 23.2 us  [the longest x1 10.9 us: on_device(): pieces = lax.all_to_all(pieces, 'head', 0, 0, tiled=True)]
    unnamed x22 -> x10, local copies, waits for them, and re-layouts: 8.74 us -> 1.42 us
    all_to_all x2 -> x3, waiting for transfers between devices: 14.8 us -> 21.8 us  [the longest x1 12.7 us: on_device(): lax.all_to_all(projected, 'tok', 0, 0, axis_index_groups=rings_y, tiled=T...]
    all_to_all x1, waiting for transfers between devices: 0.01 us -> 3.63 us  [on_device(): gathered = lax.all_to_all(sent, 'head', 0, 0, tiled=True)]
    pallas_call x2 -> x4, Pallas kernels: 10.8 us -> 13.8 us  [the longest x1 7.24 us: on_device(): pl.pallas_call(merge_kernel, out_shape=blocks_shape, in_specs=[VMEM, VMEM...]
    transpose x0 -> x1, local copies, waits for them, and re-layouts: none -> 1.58 us  [on_device(): own_weight.transpose(1, 0, 2, 3).reshape(group * width_here, columns)]
  transfers between devices with their start and end apart: 6 -> 7, of which waited for: 4 -> 6; matrix products, arithmetic and copies ran while one was open for 1% -> 2% of each run, Pallas kernels for 6% -> 6%
where the time goes in v3:
time: 124 us; the launch traced here: 123 us
  waiting for transfers between devices  53.6 us (43%)
  starting transfers between devices  33.4 us (27%)
  Pallas kernels  17.6 us (14%)
  between operations  13.5 us (11%)
  local copies, waits for them, and re-layouts  4.8 us (4%)
    all_gather x1, waiting for transfers between devices, on_device(): lax.all_gather(pieces, 'tok', axis=0, axis_index_groups=rings_x)  26.9 us
    all_to_all x1, waiting for transfers between devices, on_device(): lax.all_to_all(projected, 'tok', 0, 0, axis_index_groups=rings_y, tiled=T...  12.7 us
    all_to_all x1, starting transfers between devices, on_device(): pieces = lax.all_to_all(pieces, 'head', 0, 0, tiled=True)  10.9 us
    pallas_call x1, Pallas kernels, on_device(): pl.pallas_call(merge_kernel, out_shape=blocks_shape, in_specs=[VMEM, VMEM...  7.24 us
    all_to_all x1, waiting for transfers between devices, on_device(): lax.all_to_all(blocks, 'tok', 0, 0, axis_index_groups=planes, tiled=True)  6.98 us
    all_to_all x1, starting transfers between devices, on_device(): lax.all_to_all(projected, 'tok', 0, 0, axis_index_groups=rings_y, tiled=T...  6.84 us
    all_to_all x1, starting transfers between devices, on_device(): lax.all_to_all(blocks, 'tok', 0, 0, axis_index_groups=planes, tiled=True)  5.51 us
    ppermute x2, starting transfers between devices, partner(): lax.ppermute(x, axis, [(i, i ^ 1 << apart) for i in range(lax.axis_size(a...  5.45 us
  transfers between devices with their start and end apart: 7, of which 6 were waited for; matrix products, arithmetic and copies ran while one was open for 2% of the time, Pallas kernels for 6%

profile of v3, /device:TPU:1, one launch (start us, length us, event | category | flops | bytes accessed | tf_op | source)
XLA Modules:
  0.0 123.3 jit_solution(8234862040958597817)
XLA Ops:
  6.5 0.8 dynamic_slice.3
  7.3 0.8 broadcast_in_dim.50
  8.1 10.9 %all-to-all-start = ((bf16[8,40,640]{2,1,0:T(8,128)(2,1)}), bf16[8,40,640]{2,1,0:T(8,128)(2,1)S(1)}, u32[]{:S(2)}, u32[]{:S(2)}) async-start(bf16[8,40,640]{2,1,0:T(8,128)(2,1)} %broadcast_in_dim.50), calls=%async_computation | async-start | bytes 819200 | tf_op jit(solution)/shard_map/all_to_all | solution.py:224
  19.0 0.0 all-gather.3.cloned.1.call-start
  19.1 0.0 copy-start
  19.1 0.6 copy-done
  19.7 3.9 %shard_map.91 = (f32[10,512,128]{2,1,0:T(8,128)}, bf16[160,512]{1,0:T(8,128)(2,1)S(1)}, bf16[320,512]{1,0:T(8,128)(2,1)S(1)}) custom-call(s32[64]{0:T(128)S(1)} %copy-done, bf16[512,1280]{1,0:T(8,128)(2,1)} %patches_hbm.1, bf16[64,1280]{1,0:T(8,128)(2,1)} %row_hbm.1, bf16[64,1280]{1,0:T(8,128)(2,1)} %col_hbm.1, bf16[3,160,1280]{2,1,0:T(8,128)(2,1)} %weight_hbm.1), custom_call_target="tpu_custom_call" | custom-call | flops 629145600 | bytes 8388608 | tf_op jit(solution)/shard_map/pallas_call | solution.py:226
  23.6 2.9 %collective-permute-start = (bf16[320,512]{1,0:T(8,128)(2,1)S(1)}, bf16[320,512]{1,0:T(8,128)(2,1)S(1)}, u32[]{:S(2)}, u32[]{:S(2)}) collective-permute-start(bf16[320,512]{1,0:T(8,128)(2,1)S(1)} %get-tuple-element.11.near), channel_id=1, source_target_pairs={{0,1},{1,0},{2,3},{3,2},{4,5},{5,4},{6,7},{7,6},{8,9},{9,8},{10,11... | collective-permute-start | bytes 983048 | tf_op jit(solution)/shard_map/ppermute | solution.py:24
  26.5 1.2 %collective-permute-done.far = bf16[320,512]{1,0:T(8,128)(2,1)S(1)} collective-permute-done((bf16[320,512]{1,0:T(8,128)(2,1)S(1)}, bf16[320,512]{1,0:T(8,128)(2,1)S(1)}, u32[]{:S(2)}, u32[]{:S(2)}) %collective-permute-start) | collective-permute-done | bytes 327712 | tf_op jit(solution)/shard_map/ppermute | solution.py:24
  27.7 3.8 %shard_map.92 = bf16[8,160,512]{2,1,0:T(8,128)(2,1)} custom-call(s32[64]{0:T(128)S(1)} %copy-done, bf16[160,512]{1,0:T(8,128)(2,1)S(1)} %get-tuple-element.10.queries, bf16[320,512]{1,0:T(8,128)(2,1)S(1)} %get-tuple-element.11.near, bf16[320,512]{1,0:T(8,128)(2,1)S(1)} %collective-permute-done.far), custom_call_target="tpu_custom_call" | custom-call | tf_op jit(solution)/shard_map/pallas_call | solution.py:248
  31.6 2.2 %all-to-all-done = bf16[8,40,640]{2,1,0:T(8,128)(2,1)S(1)} async-done(((bf16[8,40,640]{2,1,0:T(8,128)(2,1)}), bf16[8,40,640]{2,1,0:T(8,128)(2,1)S(1)}, u32[]{:S(2)}, u32[]{:S(2)}) %all-to-all-start) | async-done | bytes 409632 | tf_op jit(solution)/shard_map/all_to_all | solution.py:224
  33.7 0.0 copy-start.2
  33.7 0.8 copy-done.2
  34.5 0.0 all-gather.3.cloned.1.call-update
  34.5 4.7 %all-to-all-start.1 = ((bf16[8,160,512]{2,1,0:T(8,128)(2,1)}), bf16[8,160,512]{2,1,0:T(8,128)(2,1)S(1)}, u32[]{:S(2)}, u32[]{:S(2)}) async-start(bf16[8,160,512]{2,1,0:T(8,128)(2,1)} %shard_map.92), calls=%async_computation.1 | async-start | bytes 2621440 | tf_op jit(solution)/shard_map/all_to_all | solution.py:260
  39.2 26.9 %all-gather.3.cloned.1.call-done = bf16[32,40,640]{2,1,0:T(8,128)(2,1)} async-done(((bf16[8,40,640]{2,1,0:T(8,128)(2,1)}), bf16[32,40,640]{2,1,0:T(8,128)(2,1)}) %all-gather.3.cloned.1.call-update) | async-done | bytes 1638416 | tf_op jit(solution)/shard_map/all_gather | solution.py:256
  66.1 0.0 copy-start.4
  66.1 1.6 %copy.12 = bf16[8,4,40,640]{3,2,1,0:T(8,128)(2,1)S(1)} copy(bf16[8,4,40,640]{3,2,0,1:T(8,128)(2,1)} %bitcast.17) | data formatting | bytes 3276800 | tf_op jit(solution)/shard_map/transpose | solution.py:257
  67.7 2.6 %collective-permute-start.1 = (bf16[1280,640]{1,0:T(8,128)(2,1)S(1)}, bf16[1280,640]{1,0:T(8,128)(2,1)}, u32[]{:S(2)}, u32[]{:S(2)}) collective-permute-start(bf16[1280,640]{1,0:T(8,128)(2,1)S(1)} %bitcast.15), channel_id=1, source_target_pairs={{0,1},{1,0},{2,3},{3,2},{4,5},{5,4},{6,7},{7,6},{8,9},{9,8},{10,11... | collective-permute-start | bytes 4915208 | tf_op jit(solution)/shard_map/ppermute | solution.py:24
  70.3 0.0 copy-done.4
  70.3 0.1 select_reduce_fusion
  70.4 3.6 %all-to-all-done.1.gathered = bf16[8,160,512]{2,1,0:T(8,128)(2,1)S(1)} async-done(((bf16[8,160,512]{2,1,0:T(8,128)(2,1)}), bf16[8,160,512]{2,1,0:T(8,128)(2,1)S(1)}, u32[]{:S(2)}, u32[]{:S(2)}) %all-to-all-start.1) | async-done | bytes 1310752 | tf_op jit(solution)/shard_map/all_to_all | solution.py:260
  74.1 0.0 collective-permute-done.1.other_hbm
  74.1 0.0 copy-start.3
  74.1 7.2 %shard_map.93 = bf16[8,160,128]{2,1,0:T(8,128)(2,1)} custom-call(bf16[8,160,512]{2,1,0:T(8,128)(2,1)S(1)} %all-to-all-done.1.gathered, bf16[1280,640]{1,0:T(8,128)(2,1)S(1)} %bitcast.16, bf16[1280,640]{1,0:T(8,128)(2,1)} %collective-permute-done.1.other_hbm, f32[10,512,128]{2,1,0:T(8,128)} %get-tuple-element.14.resid_hbm, bf16[160,5120]{1,0:T(8,128)(2,1)} %merge_hbm.1), custom_call_target="tpu_custom_call" | custom-call | tf_op jit(solution)/shard_map/pallas_call | solution.py:263
  81.3 0.0 copy-start.1
  81.3 6.8 %all-to-all-start.2 = ((bf16[8,160,128]{2,1,0:T(8,128)(2,1)}), bf16[8,160,128]{2,1,0:T(8,128)(2,1)S(1)}, u32[]{:S(2)}, u32[]{:S(2)}) async-start(bf16[8,160,128]{2,1,0:T(8,128)(2,1)} %shard_map.93), calls=%async_computation.2 | async-start | bytes 655360 | tf_op jit(solution)/shard_map/all_to_all | solution.py:291
  88.2 0.1 reduce_sum.31
  88.3 0.1 fusion.3
  88.4 0.1 reshape.157.wanted
  88.4 0.0 copy-done.3
  88.5 12.7 %all-to-all-done.2.blocks = bf16[8,160,128]{2,1,0:T(8,128)(2,1)S(1)} async-done(((bf16[8,160,128]{2,1,0:T(8,128)(2,1)}), bf16[8,160,128]{2,1,0:T(8,128)(2,1)S(1)}, u32[]{:S(2)}, u32[]{:S(2)}) %all-to-all-start.2) | async-done | bytes 327712 | tf_op jit(solution)/shard_map/all_to_all | solution.py:291
  101.2 1.3 %shard_map.94 = bf16[8,160,128]{2,1,0:T(8,128)(2,1)} custom-call(s32[8]{0:T(128)S(1)} %reshape.157.wanted, bf16[8,160,128]{2,1,0:T(8,128)(2,1)S(1)} %all-to-all-done.2.blocks), custom_call_target="tpu_custom_call" | custom-call | tf_op jit(solution)/shard_map/pallas_call | solution.py:292
  102.5 5.5 %all-to-all-start.3 = ((bf16[8,160,128]{2,1,0:T(8,128)(2,1)}), bf16[8,160,128]{2,1,0:T(8,128)(2,1)S(1)}, u32[]{:S(2)}, u32[]{:S(2)}) async-start(bf16[8,160,128]{2,1,0:T(8,128)(2,1)} %shard_map.94), calls=%async_computation.3 | async-start | bytes 655360 | tf_op jit(solution)/shard_map/all_to_all | solution.py:299
  108.0 0.0 copy-done.1
  108.0 0.1 fusion.5.facts
  108.1 7.0 %all-to-all-done.3.blocks = bf16[8,160,128]{2,1,0:T(8,128)(2,1)S(1)} async-done(((bf16[8,160,128]{2,1,0:T(8,128)(2,1)}), bf16[8,160,128]{2,1,0:T(8,128)(2,1)S(1)}, u32[]{:S(2)}, u32[]{:S(2)}) %all-to-all-start.3) | async-done | bytes 327712 | tf_op jit(solution)/shard_map/all_to_all | solution.py:299
  115.1 1.4 %shard_map.95 = bf16[160,248]{1,0:T(8,128)(2,1)} custom-call(s32[3]{0:T(128)S(1)} %fusion.5.facts, bf16[8,160,128]{2,1,0:T(8,128)(2,1)S(1)} %all-to-all-done.3.blocks), custom_call_target="tpu_custom_call" | custom-call | tf_op jit(solution)/shard_map/pallas_call | solution.py:300
  (4 shorter events, 0.0 us)
Async XLA Ops:
  8.1 25.6 %all-to-all-start = ((bf16[8,40,640]{2,1,0:T(8,128)(2,1)}), bf16[8,40,640]{2,1,0:T(8,128)(2,1)S(1)}, u32[]{:S(2)}, u32[]{:S(2)}) async-start(bf16[8,40,640]{2,1,0:T(8,128)(2,1)} %broadcast_in_dim.50), calls=%async_computation | async-start | bytes 819200 | tf_op jit(solution)/shard_map/all_to_all | solution.py:224
  19.0 47.1 %all-gather.3.cloned.1.call-start = ((), (), s32[]{:S(2)}) async-start(), calls=%async_computation.4 | async-start | bytes 2048000 | tf_op jit(solution)/shard_map/all_gather | solution.py:256
  19.1 0.7 copy-start
  23.6 4.1 %collective-permute-start = (bf16[320,512]{1,0:T(8,128)(2,1)S(1)}, bf16[320,512]{1,0:T(8,128)(2,1)S(1)}, u32[]{:S(2)}, u32[]{:S(2)}) collective-permute-start(bf16[320,512]{1,0:T(8,128)(2,1)S(1)} %get-tuple-element.11.near), channel_id=1, source_target_pairs={{0,1},{1,0},{2,3},{3,2},{4,5},{5,4},{6,7},{7,6},{8,9},{9,8},{10,11... | collective-permute-start | bytes 983048 | tf_op jit(solution)/shard_map/ppermute | solution.py:24
  33.7 0.8 copy-start.2
  34.5 39.5 %all-to-all-start.1 = ((bf16[8,160,512]{2,1,0:T(8,128)(2,1)}), bf16[8,160,512]{2,1,0:T(8,128)(2,1)S(1)}, u32[]{:S(2)}, u32[]{:S(2)}) async-start(bf16[8,160,512]{2,1,0:T(8,128)(2,1)} %shard_map.92), calls=%async_computation.1 | async-start | bytes 2621440 | tf_op jit(solution)/shard_map/all_to_all | solution.py:260
  66.1 4.2 %copy-start.4 = (s32[64]{0:T(128)S(1)}, s32[64]{0:T(128)}, u32[]{:S(2)}) copy-start(s32[64]{0:T(128)} %param.18) | copy-start | bytes 772
  67.7 6.4 %collective-permute-start.1 = (bf16[1280,640]{1,0:T(8,128)(2,1)S(1)}, bf16[1280,640]{1,0:T(8,128)(2,1)}, u32[]{:S(2)}, u32[]{:S(2)}) collective-permute-start(bf16[1280,640]{1,0:T(8,128)(2,1)S(1)} %bitcast.15), channel_id=1, source_target_pairs={{0,1},{1,0},{2,3},{3,2},{4,5},{5,4},{6,7},{7,6},{8,9},{9,8},{10,11... | collective-permute-start | bytes 4915208 | tf_op jit(solution)/shard_map/ppermute | solution.py:24
  74.1 14.4 %copy-start.3 = (s32[64,2]{0,1:T(2,128)S(1)}, s32[64,2]{0,1:T(2,128)}, u32[]{:S(2)}) copy-start(s32[64,2]{0,1:T(2,128)} %param.16) | copy-start | bytes 1540
  81.3 26.7 %copy-start.1 = (s32[64]{0:T(128)S(1)}, s32[64]{0:T(128)}, u32[]{:S(2)}) copy-start(s32[64]{0:T(128)} %offsets.3) | copy-start | bytes 772
  81.3 19.9 %all-to-all-start.2 = ((bf16[8,160,128]{2,1,0:T(8,128)(2,1)}), bf16[8,160,128]{2,1,0:T(8,128)(2,1)S(1)}, u32[]{:S(2)}, u32[]{:S(2)}) async-start(bf16[8,160,128]{2,1,0:T(8,128)(2,1)} %shard_map.93), calls=%async_computation.2 | async-start | bytes 655360 | tf_op jit(solution)/shard_map/all_to_all | solution.py:291
  102.5 12.6 %all-to-all-start.3 = ((bf16[8,160,128]{2,1,0:T(8,128)(2,1)}), bf16[8,160,128]{2,1,0:T(8,128)(2,1)S(1)}, u32[]{:S(2)}, u32[]{:S(2)}) async-start(bf16[8,160,128]{2,1,0:T(8,128)(2,1)} %shard_map.94), calls=%async_computation.3 | async-start | bytes 655360 | tf_op jit(solution)/shard_map/all_to_all | solution.py:299
Sparse Core Ops, SparseCore 0:
  34.6 31.4 all-gather.2

commit v4 on v3

--- a/solution.py
+++ b/solution.py
@@ -18,6 +18,7 @@
 VMEM = pl.BlockSpec(memory_space=pltpu.VMEM)
 SMEM = pl.BlockSpec(memory_space=pltpu.SMEM)
 HBM = pl.BlockSpec(memory_space=pltpu.HBM)
+ANY = pl.BlockSpec(memory_space=pl.ANY)
 
 
 def partner(x, axis, apart):
@@ -35,7 +36,7 @@
 
 
 def front_kernel(
-    offsets,
+    offsets_hbm,
     patches_hbm,
     row_hbm,
     col_hbm,
@@ -47,6 +48,7 @@
     patches,
     tables,
     weight,
+    offsets,
     sems,
 ):
     rows = patches.shape[0]
@@ -57,8 +59,11 @@
         pltpu.make_async_copy(patches_hbm, patches, sems.at[2]),
         pltpu.make_async_copy(weight_hbm, weight, sems.at[3]),
     ]
+    offsets_copy = pltpu.make_async_copy(offsets_hbm, offsets, sems.at[5])
+    offsets_copy.start()
     for copy in copies:
         copy.start()
+    offsets_copy.wait()
     place = lax.axis_index("tok")
     first = place // 2 * 2
     position = place * rows + lax.broadcasted_iota(jnp.int32, (rows, 2 * side), 0)
@@ -124,38 +129,53 @@
             out[copy, own, :] = mixed
 
 
-def merge_kernel(
-    gathered,
-    own_weight,
-    other_hbm,
-    resid_hbm,
-    merge_hbm,
-    out,
-    other_weight,
-    resid,
-    merge_weight,
-    total,
-    sems,
-):
-    other_copy = pltpu.make_async_copy(other_hbm, other_weight, sems.at[0])
-    resid_copy = pltpu.make_async_copy(resid_hbm, resid, sems.at[1])
-    merge_copy = pltpu.make_async_copy(merge_hbm, merge_weight, sems.at[2])
-    other_copy.start()
+def piece_kernel(weight, out, sems):
+    depth, columns = out.shape[1:]
+    place = lax.axis_index("tok")
+    row = pl.multiple_of(place // (2 * RING) * depth, 8)
+    column = pl.multiple_of(place % 2 * columns, LANES)
+    copies = [
+        pltpu.make_async_copy(
+            weight.at[pl.ds(row, depth), pl.ds(column, columns)], out.at[copy], sems.at[copy]
+        )
+        for copy in range(out.shape[0])
+    ]
+    for copy in copies:
+        copy.start()
+    for copy in copies:
+        copy.wait()
+
+
+def project_kernel(gathered, weight, resid_hbm, attended, partial, resid, sem):
+    resid_copy = pltpu.make_async_copy(resid_hbm, resid, sem)
     resid_copy.start()
+    core = lax.axis_index("tok") % 2
+    group, depth, rows = gathered.shape
+    whole = gathered[...].reshape(group * depth, rows)
+    tiles = resid.shape[0]
+    for tile in range(tiles):
+        part = slice(tile * LANES, (tile + 1) * LANES)
+        attended[:, part] = whole[part, :].T
+    part = dot(attended[...], weight[...], ((1,), (0,)))
+    resid_copy.wait()
+    for tile in range(tiles // 2):
+        place = core * (tiles // 2) + tile
+        partial[place] = resid[place] + part[:, tile * LANES : (tile + 1) * LANES]
+        place = (1 - core) * (tiles // 2) + tile
+        partial[place] = resid[place]
+
+
+def merge_kernel(attended, weight, partial, merge_hbm, out, merge_weight, total, sem):
+    merge_copy = pltpu.make_async_copy(merge_hbm, merge_weight, sem)
     merge_copy.start()
     core = lax.axis_index("tok") % 2
-    group, depth, rows = gathered.shape
-    attended = gathered[...].reshape(group * depth, rows)
-    tiles = resid.shape[0]
-    for weight, half in ((own_weight, core), (other_weight, 1 - core)):
-        if weight is other_weight:
-            other_copy.wait()
-        part = dot(attended, weight[...], ((0,), (0,)))
-        if weight is own_weight:
-            resid_copy.wait()
-        for tile in range(tiles // 2):
-            place = half * (tiles // 2) + tile
-            total[place] = resid[place] + part[:, tile * LANES : (tile + 1) * LANES]
+    tiles, rows = partial.shape[:2]
+    part = dot(attended[...], weight[...], ((1,), (0,)))
+    for tile in range(tiles // 2):
+        place = core * (tiles // 2) + tile
+        total[place] = partial[place]
+        place = (1 - core) * (tiles // 2) + tile
+        total[place] = partial[place] + part[:, tile * LANES : (tile + 1) * LANES]
     values = jnp.concatenate([total[tile] for tile in range(tiles)], axis=1)
     normed = normalize(values)
     for tile in range(tiles):
@@ -173,9 +193,15 @@
         out[copy] = projected
 
 
-def pick_kernel(wanted, blocks, out):
-    for slot in range(out.shape[0]):
-        out[slot] = blocks[wanted[slot]]
+def pick_kernel(wanted, blocks, out, sems):
+    copies = [
+        pltpu.make_async_copy(blocks.at[wanted[slot]], out.at[slot], sems.at[slot])
+        for slot in range(out.shape[0])
+    ]
+    for copy in copies:
+        copy.start()
+    for copy in copies:
+        copy.wait()
 
 
 def deliver_kernel(facts, blocks, out):
@@ -219,8 +245,14 @@
     core = place % 2
 
     depth, columns = width_here // sides, width // 2
-    piece = lax.dynamic_slice(out_weight, (my_x * depth, core * columns), (depth, columns))
-    pieces = jnp.broadcast_to(piece[None], (group, depth, columns))
+    pieces = pl.pallas_call(
+        piece_kernel,
+        out_shape=pltpu.HBM((group, depth, columns), jnp.bfloat16),
+        in_specs=[HBM],
+        out_specs=HBM,
+        scratch_shapes=[pltpu.SemaphoreType.DMA((group,))],
+        compiler_params=params,
+    )(at_hbm(out_weight))
     pieces = lax.all_to_all(pieces, "head", 0, 0, tiled=True)
 
     resid, queries, near = pl.pallas_call(
@@ -230,20 +262,21 @@
             jax.ShapeDtypeStruct((width_here, block_rows), jnp.bfloat16),
             jax.ShapeDtypeStruct((2 * width_here, block_rows), jnp.bfloat16),
         ),
-        in_specs=[SMEM, HBM, HBM, HBM, HBM],
+        in_specs=[HBM] * 5,
         out_specs=(HBM, VMEM, VMEM),
         scratch_shapes=[
             pltpu.VMEM((width // LANES, block_rows, LANES), jnp.float32),
             pltpu.VMEM(patches.shape, jnp.bfloat16),
             pltpu.VMEM((2 * row_table.shape[0], width), jnp.bfloat16),
             pltpu.VMEM(qkv_weight.shape, jnp.bfloat16),
-            pltpu.SemaphoreType.DMA((5,)),
+            pltpu.SMEM(image_offsets.shape, jnp.int32),
+            pltpu.SemaphoreType.DMA((6,)),
         ],
         compiler_params=params,
         cost_estimate=pl.CostEstimate(
             flops=3 * 2 * block_rows * width * width_here, bytes_accessed=8 * 2**20, transcendentals=0
         ),
-    )(image_offsets, *map(at_hbm, (patches, row_table, col_table, qkv_weight)))
+    )(*map(at_hbm, (image_offsets, patches, row_table, col_table, qkv_weight)))
     far = partner(near, "tok", 0)
     sent = pl.pallas_call(
         attend_kernel,
@@ -260,20 +293,37 @@
     gathered = lax.all_to_all(sent, "head", 0, 0, tiled=True)
     rows_here = block_rows // 4
     blocks_shape = jax.ShapeDtypeStruct((RING, width_here, rows_here), jnp.bfloat16)
+    tiles = width // LANES
+    half_flops = 2 * block_rows * width * columns
+    attended, partial = pl.pallas_call(
+        project_kernel,
+        out_shape=(
+            jax.ShapeDtypeStruct((block_rows, width), jnp.bfloat16),
+            jax.ShapeDtypeStruct((tiles, block_rows, LANES), jnp.float32),
+        ),
+        in_specs=[VMEM, VMEM, HBM],
+        out_specs=(VMEM, VMEM),
+        scratch_shapes=[
+            pltpu.VMEM((tiles, block_rows, LANES), jnp.float32),
+            pltpu.SemaphoreType.DMA,
+        ],
+        compiler_params=params,
+        cost_estimate=pl.CostEstimate(
+            flops=half_flops, bytes_accessed=8 * 2**20, transcendentals=0
+        ),
+    )(gathered, own_weight, at_hbm(resid))
     projected = pl.pallas_call(
         merge_kernel,
         out_shape=blocks_shape,
-        in_specs=[VMEM, VMEM, HBM, HBM, HBM],
+        in_specs=[VMEM, VMEM, VMEM, HBM],
         out_specs=VMEM,
         scratch_shapes=[
-            pltpu.VMEM(other_weight.shape, jnp.bfloat16),
-            pltpu.VMEM((width // LANES, block_rows, LANES), jnp.float32),
             pltpu.VMEM(merge_weight.shape, jnp.bfloat16),
-            pltpu.VMEM((width // LANES, block_rows, LANES), jnp.float32),
-            pltpu.SemaphoreType.DMA((3,)),
+            pltpu.VMEM((tiles, block_rows, LANES), jnp.float32),
+            pltpu.SemaphoreType.DMA,
         ],
         compiler_params=params,
-    )(gathered, own_weight, *map(at_hbm, (other_weight, resid, merge_weight)))
+    )(attended, other_weight, partial, at_hbm(merge_weight))
 
     image_ids = jnp.arange(owners.shape[0], dtype=jnp.int32)
     place_ids = jnp.arange(places, dtype=jnp.int32)
@@ -291,9 +341,10 @@
     blocks = lax.all_to_all(projected, "tok", 0, 0, axis_index_groups=rings_y, tiled=True)
     blocks = pl.pallas_call(
         pick_kernel,
-        out_shape=jax.ShapeDtypeStruct((2 * sides, width_here, rows_here), jnp.bfloat16),
-        in_specs=[SMEM, VMEM],
-        out_specs=VMEM,
+        out_shape=pltpu.HBM((2 * sides, width_here, rows_here), jnp.bfloat16),
+        in_specs=[SMEM, ANY],
+        out_specs=HBM,
+        scratch_shapes=[pltpu.SemaphoreType.DMA((2 * sides,))],
         compiler_params=params,
     )(wanted, blocks)
     blocks = lax.all_to_all(blocks, "tok", 0, 0, axis_index_groups=planes, tiled=True)

time: 124 us -> 137 us (1.10)
  Pallas kernels: 17.6 us -> 33 us
  local copies, waits for them, and re-layouts: 4.8 us -> 2.53 us
    pallas_call x1 -> x3, Pallas kernels: 1.29 us -> 18 us  [the longest x1 13.6 us: on_device(): pl.pallas_call(piece_kernel, out_shape=pltpu.HBM((group, depth, columns),...]
    all_gather x0 -> x1, local copies, waits for them, and re-layouts: none -> 1.58 us  [on_device(): lax.all_gather(pieces, 'tok', axis=0, axis_index_groups=rings_x)]
    transpose x1 -> x0, local copies, waits for them, and re-layouts: 1.58 us -> none  [on_device(): own_weight.transpose(1, 0, 2, 3).reshape(group * width_here, columns)]
  transfers between devices with their start and end apart: 7 -> 7, of which waited for: 6 -> 6; matrix products, arithmetic and copies ran while one was open for 2% -> 2% of each run, Pallas kernels for 6% -> 8%
where the time goes in v4:
time: 137 us
  waiting for transfers between devices  54.7 us (40%)
  Pallas kernels  33 us (24%)
  starting transfers between devices  32.5 us (24%)
  between operations  13.5 us (10%)
  local copies, waits for them, and re-layouts  2.53 us (2%)
    all_gather x1, waiting for transfers between devices, on_device(): lax.all_gather(pieces, 'tok', axis=0, axis_index_groups=rings_x)  26.9 us
    pallas_call x1, Pallas kernels, on_device(): pl.pallas_call(piece_kernel, out_shape=pltpu.HBM((group, depth, columns),...  13.6 us
    all_to_all x1, waiting for transfers between devices, on_device(): lax.all_to_all(projected, 'tok', 0, 0, axis_index_groups=rings_y, tiled=T...  12.7 us
    all_to_all x1, starting transfers between devices, on_device(): pieces = lax.all_to_all(pieces, 'head', 0, 0, tiled=True)  10.9 us
    all_to_all x1, waiting for transfers between devices, on_device(): lax.all_to_all(blocks, 'tok', 0, 0, axis_index_groups=planes, tiled=True)  6.98 us
    all_to_all x1, starting transfers between devices, on_device(): lax.all_to_all(projected, 'tok', 0, 0, axis_index_groups=rings_y, tiled=T...  6.83 us
    pallas_call x1, Pallas kernels, on_device(): pl.pallas_call(merge_kernel, out_shape=blocks_shape, in_specs=[VMEM, VMEM...  6.34 us
    all_to_all x1, starting transfers between devices, on_device(): lax.all_to_all(blocks, 'tok', 0, 0, axis_index_groups=planes, tiled=True)  5.54 us
  transfers between devices with their start and end apart: 7, of which 6 were waited for; matrix products, arithmetic and copies ran while one was open for 2% of the time, Pallas kernels for 8%

profile of v4, /device:TPU:1, one launch (start us, length us, event | category | flops | bytes accessed | tf_op | source)
XLA Modules:
  0.0 136.7 jit_solution(16430398380792236987)
XLA Ops:
  6.5 13.6 %shard_map.91 = bf16[8,40,640]{2,1,0:T(8,128)(2,1)} custom-call(bf16[160,1280]{1,0:T(8,128)(2,1)} %weight.1), custom_call_target="tpu_custom_call" | custom-call | tf_op jit(solution)/shard_map/pallas_call | solution.py:248
  20.1 10.9 %all-to-all-start = ((bf16[8,40,640]{2,1,0:T(8,128)(2,1)}), bf16[8,40,640]{2,1,0:T(8,128)(2,1)S(1)}, u32[]{:S(2)}, u32[]{:S(2)}) async-start(bf16[8,40,640]{2,1,0:T(8,128)(2,1)} %shard_map.91), calls=%async_computation | async-start | bytes 819200 | tf_op jit(solution)/shard_map/all_to_all | solution.py:256
  31.0 0.0 copy-start
  31.0 0.0 all-gather.3.cloned.1.call-start
  31.1 3.5 %shard_map.92 = (f32[10,512,128]{2,1,0:T(8,128)}, bf16[160,512]{1,0:T(8,128)(2,1)S(1)}, bf16[320,512]{1,0:T(8,128)(2,1)S(1)}) custom-call(s32[64]{0:T(128)} %offsets.1, bf16[512,1280]{1,0:T(8,128)(2,1)} %patches_hbm.1, bf16[64,1280]{1,0:T(8,128)(2,1)} %row_hbm.1, bf16[64,1280]{1,0:T(8,128)(2,1)} %col_hbm.1, bf16[3,160,1280]{2,1,0:T(8,128)(2,1)} %weight_hbm.1), custom_call_target="tpu_custom_call" | custom-call | flops 629145600 | bytes 8388608 | tf_op jit(solution)/shard_map/pallas_call | solution.py:258
  34.6 2.9 %collective-permute-start = (bf16[320,512]{1,0:T(8,128)(2,1)S(1)}, bf16[320,512]{1,0:T(8,128)(2,1)S(1)}, u32[]{:S(2)}, u32[]{:S(2)}) collective-permute-start(bf16[320,512]{1,0:T(8,128)(2,1)S(1)} %get-tuple-element.13.near), channel_id=1, source_target_pairs={{0,1},{1,0},{2,3},{3,2},{4,5},{5,4},{6,7},{7,6},{8,9},{9,8},{10,11... | collective-permute-start | bytes 983048 | tf_op jit(solution)/shard_map/ppermute | solution.py:25
  37.4 1.2 collective-permute-done.far
  38.7 0.0 copy-done
  38.7 3.8 %shard_map.93 = bf16[8,160,512]{2,1,0:T(8,128)(2,1)} custom-call(s32[64]{0:T(128)S(1)} %copy-done, bf16[160,512]{1,0:T(8,128)(2,1)S(1)} %get-tuple-element.12.queries, bf16[320,512]{1,0:T(8,128)(2,1)S(1)} %get-tuple-element.13.near, bf16[320,512]{1,0:T(8,128)(2,1)S(1)} %collective-permute-done.far), custom_call_target="tpu_custom_call" | custom-call | tf_op jit(solution)/shard_map/pallas_call | solution.py:281
  42.5 3.2 %all-to-all-done = bf16[8,40,640]{2,1,0:T(8,128)(2,1)S(1)} async-done(((bf16[8,40,640]{2,1,0:T(8,128)(2,1)}), bf16[8,40,640]{2,1,0:T(8,128)(2,1)S(1)}, u32[]{:S(2)}, u32[]{:S(2)}) %all-to-all-start) | async-done | bytes 409632 | tf_op jit(solution)/shard_map/all_to_all | solution.py:256
  45.7 0.0 copy-start.1
  45.7 0.8 copy-done.1
  46.5 0.0 all-gather.3.cloned.1.call-update
  46.5 3.8 %all-to-all-start.1 = ((bf16[8,160,512]{2,1,0:T(8,128)(2,1)}), bf16[8,160,512]{2,1,0:T(8,128)(2,1)S(1)}, u32[]{:S(2)}, u32[]{:S(2)}) async-start(bf16[8,160,512]{2,1,0:T(8,128)(2,1)} %shard_map.93), calls=%async_computation.1 | async-start | bytes 2621440 | tf_op jit(solution)/shard_map/all_to_all | solution.py:293
  50.3 26.9 %all-gather.3.cloned.1.call-done = bf16[32,40,640]{2,1,0:T(8,128)(2,1)} async-done(((bf16[8,40,640]{2,1,0:T(8,128)(2,1)}), bf16[32,40,640]{2,1,0:T(8,128)(2,1)}) %all-gather.3.cloned.1.call-update) | async-done | bytes 1638416 | tf_op jit(solution)/shard_map/all_gather | solution.py:289
  77.1 0.0 copy-start.3
  77.1 1.6 %copy.13 = bf16[4,8,40,640]{3,2,0,1:T(8,128)(2,1)S(1)} copy(bf16[4,8,40,640]{3,2,1,0:T(8,128)(2,1)} %bitcast.17) | data formatting | bytes 3276800 | tf_op jit(solution)/shard_map/all_gather | solution.py:289
  78.7 2.6 %collective-permute-start.1 = (bf16[1280,640]{1,0:T(8,128)(2,1)S(1)}, bf16[1280,640]{1,0:T(8,128)(2,1)}, u32[]{:S(2)}, u32[]{:S(2)}) collective-permute-start(bf16[1280,640]{1,0:T(8,128)(2,1)S(1)} %bitcast.15), channel_id=1, source_target_pairs={{0,1},{1,0},{2,3},{3,2},{4,5},{5,4},{6,7},{7,6},{8,9},{9,8},{10,11... | collective-permute-start | bytes 4915208 | tf_op jit(solution)/shard_map/ppermute | solution.py:25
  81.3 0.0 copy-done.3
  81.4 0.1 select_reduce_fusion
  81.5 3.7 %all-to-all-done.1.gathered = bf16[8,160,512]{2,1,0:T(8,128)(2,1)S(1)} async-done(((bf16[8,160,512]{2,1,0:T(8,128)(2,1)}), bf16[8,160,512]{2,1,0:T(8,128)(2,1)S(1)}, u32[]{:S(2)}, u32[]{:S(2)}) %all-to-all-start.1) | async-done | bytes 1310752 | tf_op jit(solution)/shard_map/all_to_all | solution.py:293
  85.2 3.1 %shard_map.94 = (bf16[512,1280]{1,0:T(8,128)(2,1)S(1)}, f32[10,512,128]{2,1,0:T(8,128)S(1)}) custom-call(bf16[8,160,512]{2,1,0:T(8,128)(2,1)S(1)} %all-to-all-done.1.gathered, bf16[1280,640]{1,0:T(8,128)(2,1)S(1)} %bitcast.16, f32[10,512,128]{2,1,0:T(8,128)} %get-tuple-element.16.resid_hbm), custom_call_target="tpu_custom_call" | custom-call | flops 838860800 | bytes 8388608 | tf_op jit(solution)/shard_map/pallas_call | solution.py:298
  88.3 0.0 collective-permute-done.1.weight
  88.3 0.0 copy-start.2
  88.3 6.3 %shard_map.95 = bf16[8,160,128]{2,1,0:T(8,128)(2,1)} custom-call(bf16[512,1280]{1,0:T(8,128)(2,1)S(1)} %get-tuple-element.17.attended, bf16[1280,640]{1,0:T(8,128)(2,1)} %collective-permute-done.1.weight, f32[10,512,128]{2,1,0:T(8,128)S(1)} %get-tuple-element.18.partial, bf16[160,5120]{1,0:T(8,128)(2,1)} %merge_hbm.1), custom_call_target="tpu_custom_call" | custom-call | tf_op jit(solution)/shard_map/pallas_call | solution.py:315
  94.6 6.8 %all-to-all-start.2 = ((bf16[8,160,128]{2,1,0:T(8,128)(2,1)}), bf16[8,160,128]{2,1,0:T(8,128)(2,1)S(1)}, u32[]{:S(2)}, u32[]{:S(2)}) async-start(bf16[8,160,128]{2,1,0:T(8,128)(2,1)} %shard_map.95), calls=%async_computation.2 | async-start | bytes 655360 | tf_op jit(solution)/shard_map/all_to_all | solution.py:341
  101.5 0.1 reduce_sum.31
  101.6 0.1 fusion.3
  101.7 0.1 reshape.156.wanted
  101.7 0.0 copy-done.2
  101.8 12.7 %all-to-all-done.2.blocks = bf16[8,160,128]{2,1,0:T(8,128)(2,1)S(1)} async-done(((bf16[8,160,128]{2,1,0:T(8,128)(2,1)}), bf16[8,160,128]{2,1,0:T(8,128)(2,1)S(1)}, u32[]{:S(2)}, u32[]{:S(2)}) %all-to-all-start.2) | async-done | bytes 327712 | tf_op jit(solution)/shard_map/all_to_all | solution.py:341
  114.5 1.3 shard_map.96
  115.8 5.5 %all-to-all-start.3 = ((bf16[8,160,128]{2,1,0:T(8,128)(2,1)}), bf16[8,160,128]{2,1,0:T(8,128)(2,1)S(1)}, u32[]{:S(2)}, u32[]{:S(2)}) async-start(bf16[8,160,128]{2,1,0:T(8,128)(2,1)} %shard_map.96), calls=%async_computation.3 | async-start | bytes 655360 | tf_op jit(solution)/shard_map/all_to_all | solution.py:350
  121.4 0.1 fusion.5.facts
  121.5 7.0 %all-to-all-done.3.blocks = bf16[8,160,128]{2,1,0:T(8,128)(2,1)S(1)} async-done(((bf16[8,160,128]{2,1,0:T(8,128)(2,1)}), bf16[8,160,128]{2,1,0:T(8,128)(2,1)S(1)}, u32[]{:S(2)}, u32[]{:S(2)}) %all-to-all-start.3) | async-done | bytes 327712 | tf_op jit(solution)/shard_map/all_to_all | solution.py:350
  128.5 1.4 shard_map.97
  (4 shorter events, 0.0 us)
Async XLA Ops:
  20.1 25.6 %all-to-all-start = ((bf16[8,40,640]{2,1,0:T(8,128)(2,1)}), bf16[8,40,640]{2,1,0:T(8,128)(2,1)S(1)}, u32[]{:S(2)}, u32[]{:S(2)}) async-start(bf16[8,40,640]{2,1,0:T(8,128)(2,1)} %shard_map.91), calls=%async_computation | async-start | bytes 819200 | tf_op jit(solution)/shard_map/all_to_all | solution.py:256
  31.0 7.7 %copy-start = (s32[64]{0:T(128)S(1)}, s32[64]{0:T(128)}, u32[]{:S(2)}) copy-start(s32[64]{0:T(128)} %offsets.1) | copy-start | bytes 772
  31.0 46.1 %all-gather.3.cloned.1.call-start = ((), (), s32[]{:S(2)}) async-start(), calls=%async_computation.4 | async-start | bytes 2048000 | tf_op jit(solution)/shard_map/all_gather | solution.py:289
  34.6 4.1 %collective-permute-start = (bf16[320,512]{1,0:T(8,128)(2,1)S(1)}, bf16[320,512]{1,0:T(8,128)(2,1)S(1)}, u32[]{:S(2)}, u32[]{:S(2)}) collective-permute-start(bf16[320,512]{1,0:T(8,128)(2,1)S(1)} %get-tuple-element.13.near), channel_id=1, source_target_pairs={{0,1},{1,0},{2,3},{3,2},{4,5},{5,4},{6,7},{7,6},{8,9},{9,8},{10,11... | collective-permute-start | bytes 983048 | tf_op jit(solution)/shard_map/ppermute | solution.py:25
  45.7 0.8 copy-start.1
  46.5 38.7 %all-to-all-start.1 = ((bf16[8,160,512]{2,1,0:T(8,128)(2,1)}), bf16[8,160,512]{2,1,0:T(8,128)(2,1)S(1)}, u32[]{:S(2)}, u32[]{:S(2)}) async-start(bf16[8,160,512]{2,1,0:T(8,128)(2,1)} %shard_map.93), calls=%async_computation.1 | async-start | bytes 2621440 | tf_op jit(solution)/shard_map/all_to_all | solution.py:293
  77.1 4.2 %copy-start.3 = (s32[64]{0:T(128)S(1)}, s32[64]{0:T(128)}, u32[]{:S(2)}) copy-start(s32[64]{0:T(128)} %param.18) | copy-start | bytes 772
  78.7 9.5 %collective-permute-start.1 = (bf16[1280,640]{1,0:T(8,128)(2,1)S(1)}, bf16[1280,640]{1,0:T(8,128)(2,1)}, u32[]{:S(2)}, u32[]{:S(2)}) collective-permute-start(bf16[1280,640]{1,0:T(8,128)(2,1)S(1)} %bitcast.15), channel_id=1, source_target_pairs={{0,1},{1,0},{2,3},{3,2},{4,5},{5,4},{6,7},{7,6},{8,9},{9,8},{10,11... | collective-permute-start | bytes 4915208 | tf_op jit(solution)/shard_map/ppermute | solution.py:25
  88.3 13.5 %copy-start.2 = (s32[64,2]{0,1:T(2,128)S(1)}, s32[64,2]{0,1:T(2,128)}, u32[]{:S(2)}) copy-start(s32[64,2]{0,1:T(2,128)} %param.16) | copy-start | bytes 1540
  94.6 19.8 %all-to-all-start.2 = ((bf16[8,160,128]{2,1,0:T(8,128)(2,1)}), bf16[8,160,128]{2,1,0:T(8,128)(2,1)S(1)}, u32[]{:S(2)}, u32[]{:S(2)}) async-start(bf16[8,160,128]{2,1,0:T(8,128)(2,1)} %shard_map.95), calls=%async_computation.2 | async-start | bytes 655360 | tf_op jit(solution)/shard_map/all_to_all | solution.py:341
  115.8 12.7 %all-to-all-start.3 = ((bf16[8,160,128]{2,1,0:T(8,128)(2,1)}), bf16[8,160,128]{2,1,0:T(8,128)(2,1)S(1)}, u32[]{:S(2)}, u32[]{:S(2)}) async-start(bf16[8,160,128]{2,1,0:T(8,128)(2,1)} %shard_map.96), calls=%async_computation.3 | async-start | bytes 655360 | tf_op jit(solution)/shard_map/all_to_all | solution.py:350
Sparse Core Ops, SparseCore 0:
  46.6 30.4 all-gather.2

commit v5 on v4

--- a/solution.py
+++ b/solution.py
@@ -129,26 +129,13 @@
             out[copy, own, :] = mixed
 
 
-def piece_kernel(weight, out, sems):
-    depth, columns = out.shape[1:]
-    place = lax.axis_index("tok")
-    row = pl.multiple_of(place // (2 * RING) * depth, 8)
-    column = pl.multiple_of(place % 2 * columns, LANES)
-    copies = [
-        pltpu.make_async_copy(
-            weight.at[pl.ds(row, depth), pl.ds(column, columns)], out.at[copy], sems.at[copy]
-        )
-        for copy in range(out.shape[0])
-    ]
-    for copy in copies:
-        copy.start()
-    for copy in copies:
-        copy.wait()
-
-
-def project_kernel(gathered, weight, resid_hbm, attended, partial, resid, sem):
-    resid_copy = pltpu.make_async_copy(resid_hbm, resid, sem)
+def project_kernel(
+    gathered, weight, resid_hbm, merge_hbm, attended, partial, merge_weight, resid, sems
+):
+    resid_copy = pltpu.make_async_copy(resid_hbm, resid, sems.at[0])
     resid_copy.start()
+    merge_copy = pltpu.make_async_copy(merge_hbm, merge_weight, sems.at[1])
+    merge_copy.start()
     core = lax.axis_index("tok") % 2
     group, depth, rows = gathered.shape
     whole = gathered[...].reshape(group * depth, rows)
@@ -163,11 +150,10 @@
         partial[place] = resid[place] + part[:, tile * LANES : (tile + 1) * LANES]
         place = (1 - core) * (tiles // 2) + tile
         partial[place] = resid[place]
-
-
-def merge_kernel(attended, weight, partial, merge_hbm, out, merge_weight, total, sem):
-    merge_copy = pltpu.make_async_copy(merge_hbm, merge_weight, sem)
-    merge_copy.start()
+    merge_copy.wait()
+
+
+def merge_kernel(attended, weight, partial, merge_weight, out, total):
     core = lax.axis_index("tok") % 2
     tiles, rows = partial.shape[:2]
     part = dot(attended[...], weight[...], ((1,), (0,)))
@@ -181,7 +167,6 @@
     for tile in range(tiles):
         total[tile] = normed[:, tile * LANES : (tile + 1) * LANES]
     width = tiles * LANES
-    merge_copy.wait()
     projected = jnp.zeros(out.shape[1:], jnp.float32)
     for quarter in range(4):
         part = [total[tile, pl.ds(quarter, rows // 4, stride=4), :] for tile in range(tiles)]
@@ -245,14 +230,8 @@
     core = place % 2
 
     depth, columns = width_here // sides, width // 2
-    pieces = pl.pallas_call(
-        piece_kernel,
-        out_shape=pltpu.HBM((group, depth, columns), jnp.bfloat16),
-        in_specs=[HBM],
-        out_specs=HBM,
-        scratch_shapes=[pltpu.SemaphoreType.DMA((group,))],
-        compiler_params=params,
-    )(at_hbm(out_weight))
+    piece = lax.dynamic_slice(out_weight, (my_x * depth, core * columns), (depth, columns))
+    pieces = jnp.broadcast_to(piece[None], (group, depth, columns))
     pieces = lax.all_to_all(pieces, "head", 0, 0, tiled=True)
 
     resid, queries, near = pl.pallas_call(
@@ -295,35 +274,32 @@
     blocks_shape = jax.ShapeDtypeStruct((RING, width_here, rows_here), jnp.bfloat16)
     tiles = width // LANES
     half_flops = 2 * block_rows * width * columns
-    attended, partial = pl.pallas_call(
+    attended, partial, merge_here = pl.pallas_call(
         project_kernel,
         out_shape=(
             jax.ShapeDtypeStruct((block_rows, width), jnp.bfloat16),
             jax.ShapeDtypeStruct((tiles, block_rows, LANES), jnp.float32),
+            jax.ShapeDtypeStruct(merge_weight.shape, jnp.bfloat16),
         ),
-        in_specs=[VMEM, VMEM, HBM],
-        out_specs=(VMEM, VMEM),
+        in_specs=[VMEM, VMEM, HBM, HBM],
+        out_specs=(VMEM, VMEM, VMEM),
         scratch_shapes=[
             pltpu.VMEM((tiles, block_rows, LANES), jnp.float32),
-            pltpu.SemaphoreType.DMA,
+            pltpu.SemaphoreType.DMA((2,)),
         ],
         compiler_params=params,
         cost_estimate=pl.CostEstimate(
             flops=half_flops, bytes_accessed=8 * 2**20, transcendentals=0
         ),
-    )(gathered, own_weight, at_hbm(resid))
+    )(gathered, own_weight, at_hbm(resid), at_hbm(merge_weight))
     projected = pl.pallas_call(
         merge_kernel,
         out_shape=blocks_shape,
-        in_specs=[VMEM, VMEM, VMEM, HBM],
+        in_specs=[VMEM, VMEM, VMEM, VMEM],
         out_specs=VMEM,
-        scratch_shapes=[
-            pltpu.VMEM(merge_weight.shape, jnp.bfloat16),
-            pltpu.VMEM((tiles, block_rows, LANES), jnp.float32),
-            pltpu.SemaphoreType.DMA,
-        ],
-        compiler_params=params,
-    )(attended, other_weight, partial, at_hbm(merge_weight))
+        scratch_shapes=[pltpu.VMEM((tiles, block_rows, LANES), jnp.float32)],
+        compiler_params=params,
+    )(attended, other_weight, partial, merge_here)
 
     image_ids = jnp.arange(owners.shape[0], dtype=jnp.int32)
     place_ids = jnp.arange(places, dtype=jnp.int32)

time: 137 us -> 125 us (0.912)
  Pallas kernels: 33 us -> 18.8 us
  local copies, waits for them, and re-layouts: 2.53 us -> 4.14 us
    pallas_call x1 -> x0, Pallas kernels: 13.6 us -> none  [on_device(): pl.pallas_call(piece_kernel, out_shape=pltpu.HBM((group, depth, columns),...]
    all_gather x1 -> x0, local copies, waits for them, and re-layouts: 1.58 us -> none  [on_device(): lax.all_gather(pieces, 'tok', axis=0, axis_index_groups=rings_x)]
    transpose x0 -> x1, local copies, waits for them, and re-layouts: none -> 1.58 us  [on_device(): own_weight.transpose(1, 0, 2, 3).reshape(group * width_here, columns)]
  transfers between devices with their start and end apart: 7 -> 7, of which waited for: 6 -> 6; matrix products, arithmetic and copies ran while one was open for 2% -> 2% of each run, Pallas kernels for 8% -> 9%
where the time goes in v5:
time: 125 us; the launch traced here: 124 us
  waiting for transfers between devices  54.7 us (44%)
  starting transfers between devices  32.5 us (26%)
  Pallas kernels  18.8 us (15%)
  between operations  13.5 us (11%)
  local copies, waits for them, and re-layouts  4.14 us (3%)
    all_gather x1, waiting for transfers between devices, on_device(): lax.all_gather(pieces, 'tok', axis=0, axis_index_groups=rings_x)  26.9 us
    all_to_all x1, waiting for transfers between devices, on_device(): lax.all_to_all(projected, 'tok', 0, 0, axis_index_groups=rings_y, tiled=T...  12.7 us
    all_to_all x1, starting transfers between devices, on_device(): pieces = lax.all_to_all(pieces, 'head', 0, 0, tiled=True)  10.9 us
    all_to_all x1, waiting for transfers between devices, on_device(): lax.all_to_all(blocks, 'tok', 0, 0, axis_index_groups=planes, tiled=True)  6.98 us
    all_to_all x1, starting transfers between devices, on_device(): lax.all_to_all(projected, 'tok', 0, 0, axis_index_groups=rings_y, tiled=T...  6.92 us
    ppermute x2, starting transfers between devices, partner(): lax.ppermute(x, axis, [(i, i ^ 1 << apart) for i in range(lax.axis_size(a...  5.44 us
    all_to_all x1, starting transfers between devices, on_device(): lax.all_to_all(blocks, 'tok', 0, 0, axis_index_groups=planes, tiled=True)  5.44 us
    pallas_call x1, Pallas kernels, on_device(): pl.pallas_call(merge_kernel, out_shape=blocks_shape, in_specs=[VMEM, VMEM...  5.39 us
  transfers between devices with their start and end apart: 7, of which 6 were waited for; matrix products, arithmetic and copies ran while one was open for 2% of the time, Pallas kernels for 9%

profile of v5, /device:TPU:1, one launch (start us, length us, event | category | flops | bytes accessed | tf_op | source)
XLA Modules:
  0.0 123.9 jit_solution(16782253318345756765)
XLA Ops:
  6.5 0.8 dynamic_slice.3
  7.3 0.8 broadcast_in_dim.50
  8.1 10.9 %all-to-all-start = ((bf16[8,40,640]{2,1,0:T(8,128)(2,1)}), bf16[8,40,640]{2,1,0:T(8,128)(2,1)S(1)}, u32[]{:S(2)}, u32[]{:S(2)}) async-start(bf16[8,40,640]{2,1,0:T(8,128)(2,1)} %broadcast_in_dim.50), calls=%async_computation | async-start | bytes 819200 | tf_op jit(solution)/shard_map/all_to_all | solution.py:235
  19.0 0.0 copy-start
  19.0 0.0 all-gather.3.cloned.1.call-start
  19.1 3.5 %shard_map.91 = (f32[10,512,128]{2,1,0:T(8,128)}, bf16[160,512]{1,0:T(8,128)(2,1)S(1)}, bf16[320,512]{1,0:T(8,128)(2,1)S(1)}) custom-call(s32[64]{0:T(128)} %offsets.1, bf16[512,1280]{1,0:T(8,128)(2,1)} %patches_hbm.1, bf16[64,1280]{1,0:T(8,128)(2,1)} %row_hbm.1, bf16[64,1280]{1,0:T(8,128)(2,1)} %col_hbm.1, bf16[3,160,1280]{2,1,0:T(8,128)(2,1)} %weight_hbm.1), custom_call_target="tpu_custom_call" | custom-call | flops 629145600 | bytes 8388608 | tf_op jit(solution)/shard_map/pallas_call | solution.py:237
  22.6 2.9 %collective-permute-start = (bf16[320,512]{1,0:T(8,128)(2,1)S(1)}, bf16[320,512]{1,0:T(8,128)(2,1)S(1)}, u32[]{:S(2)}, u32[]{:S(2)}) collective-permute-start(bf16[320,512]{1,0:T(8,128)(2,1)S(1)} %get-tuple-element.14.near), channel_id=1, source_target_pairs={{0,1},{1,0},{2,3},{3,2},{4,5},{5,4},{6,7},{7,6},{8,9},{9,8},{10,11... | collective-permute-start | bytes 983048 | tf_op jit(solution)/shard_map/ppermute | solution.py:25
  25.4 1.2 collective-permute-done.far
  26.7 0.0 copy-done
  26.7 3.8 %shard_map.92 = bf16[8,160,512]{2,1,0:T(8,128)(2,1)} custom-call(s32[64]{0:T(128)S(1)} %copy-done, bf16[160,512]{1,0:T(8,128)(2,1)S(1)} %get-tuple-element.13.queries, bf16[320,512]{1,0:T(8,128)(2,1)S(1)} %get-tuple-element.14.near, bf16[320,512]{1,0:T(8,128)(2,1)S(1)} %collective-permute-done.far), custom_call_target="tpu_custom_call" | custom-call | tf_op jit(solution)/shard_map/pallas_call | solution.py:260
  30.5 3.2 %all-to-all-done = bf16[8,40,640]{2,1,0:T(8,128)(2,1)S(1)} async-done(((bf16[8,40,640]{2,1,0:T(8,128)(2,1)}), bf16[8,40,640]{2,1,0:T(8,128)(2,1)S(1)}, u32[]{:S(2)}, u32[]{:S(2)}) %all-to-all-start) | async-done | bytes 409632 | tf_op jit(solution)/shard_map/all_to_all | solution.py:235
  33.7 0.0 copy-start.1
  33.7 0.8 copy-done.1
  34.5 0.0 all-gather.3.cloned.1.call-update
  34.5 3.8 %all-to-all-start.1 = ((bf16[8,160,512]{2,1,0:T(8,128)(2,1)}), bf16[8,160,512]{2,1,0:T(8,128)(2,1)S(1)}, u32[]{:S(2)}, u32[]{:S(2)}) async-start(bf16[8,160,512]{2,1,0:T(8,128)(2,1)} %shard_map.92), calls=%async_computation.1 | async-start | bytes 2621440 | tf_op jit(solution)/shard_map/all_to_all | solution.py:272
  38.3 26.9 %all-gather.3.cloned.1.call-done = bf16[32,40,640]{2,1,0:T(8,128)(2,1)} async-done(((bf16[8,40,640]{2,1,0:T(8,128)(2,1)}), bf16[32,40,640]{2,1,0:T(8,128)(2,1)}) %all-gather.3.cloned.1.call-update) | async-done | bytes 1638416 | tf_op jit(solution)/shard_map/all_gather | solution.py:268
  65.1 0.0 copy-start.3
  65.1 1.6 %copy.12 = bf16[8,4,40,640]{3,2,1,0:T(8,128)(2,1)S(1)} copy(bf16[8,4,40,640]{3,2,0,1:T(8,128)(2,1)} %bitcast.17) | data formatting | bytes 3276800 | tf_op jit(solution)/shard_map/transpose | solution.py:269
  66.7 2.6 %collective-permute-start.1 = (bf16[1280,640]{1,0:T(8,128)(2,1)S(1)}, bf16[1280,640]{1,0:T(8,128)(2,1)}, u32[]{:S(2)}, u32[]{:S(2)}) collective-permute-start(bf16[1280,640]{1,0:T(8,128)(2,1)S(1)} %bitcast.15), channel_id=1, source_target_pairs={{0,1},{1,0},{2,3},{3,2},{4,5},{5,4},{6,7},{7,6},{8,9},{9,8},{10,11... | collective-permute-start | bytes 4915208 | tf_op jit(solution)/shard_map/ppermute | solution.py:25
  69.3 0.0 copy-done.3
  69.3 0.1 select_reduce_fusion
  69.5 3.6 %all-to-all-done.1.gathered = bf16[8,160,512]{2,1,0:T(8,128)(2,1)S(1)} async-done(((bf16[8,160,512]{2,1,0:T(8,128)(2,1)}), bf16[8,160,512]{2,1,0:T(8,128)(2,1)S(1)}, u32[]{:S(2)}, u32[]{:S(2)}) %all-to-all-start.1) | async-done | bytes 1310752 | tf_op jit(solution)/shard_map/all_to_all | solution.py:272
  73.1 3.4 %shard_map.93 = (bf16[512,1280]{1,0:T(8,128)(2,1)S(1)}, f32[10,512,128]{2,1,0:T(8,128)S(1)}, bf16[160,5120]{1,0:T(8,128)(2,1)S(1)}) custom-call(bf16[8,160,512]{2,1,0:T(8,128)(2,1)S(1)} %all-to-all-done.1.gathered, bf16[1280,640]{1,0:T(8,128)(2,1)S(1)} %bitcast.16, f32[10,512,128]{2,1,0:T(8,128)} %get-tuple-element.17.resid_hbm, bf16[160,5120]{1,0:T(8,128)(2,1)} %merge_hbm.1), custom_call_target="tpu_custom_call" | custom-call | flops 838860800 | bytes 8388608 | tf_op jit(solution)/shard_map/pallas_call | solution.py:277
  76.5 0.0 collective-permute-done.1.weight
  76.5 0.0 copy-start.2
  76.5 5.4 %shard_map.94 = bf16[8,160,128]{2,1,0:T(8,128)(2,1)} custom-call(bf16[512,1280]{1,0:T(8,128)(2,1)S(1)} %get-tuple-element.18.attended, bf16[1280,640]{1,0:T(8,128)(2,1)} %collective-permute-done.1.weight, f32[10,512,128]{2,1,0:T(8,128)S(1)} %get-tuple-element.19.partial, bf16[160,5120]{1,0:T(8,128)(2,1)S(1)} %get-tuple-element.20.merge_weight), custom_call_target="tpu_custom_call" | custom-call | tf_op jit(solution)/shard_map/pallas_call | solution.py:295
  81.9 6.9 %all-to-all-start.2 = ((bf16[8,160,128]{2,1,0:T(8,128)(2,1)}), bf16[8,160,128]{2,1,0:T(8,128)(2,1)S(1)}, u32[]{:S(2)}, u32[]{:S(2)}) async-start(bf16[8,160,128]{2,1,0:T(8,128)(2,1)} %shard_map.94), calls=%async_computation.2 | async-start | bytes 655360 | tf_op jit(solution)/shard_map/all_to_all | solution.py:317
  88.8 0.1 reduce_sum.31
  88.9 0.1 fusion.3
  89.0 0.1 reshape.157.wanted
  89.1 0.0 copy-done.2
  89.1 12.7 %all-to-all-done.2.blocks = bf16[8,160,128]{2,1,0:T(8,128)(2,1)S(1)} async-done(((bf16[8,160,128]{2,1,0:T(8,128)(2,1)}), bf16[8,160,128]{2,1,0:T(8,128)(2,1)S(1)}, u32[]{:S(2)}, u32[]{:S(2)}) %all-to-all-start.2) | async-done | bytes 327712 | tf_op jit(solution)/shard_map/all_to_all | solution.py:317
  101.8 1.3 %shard_map.95 = bf16[8,160,128]{2,1,0:T(8,128)(2,1)} custom-call(s32[8]{0:T(128)S(1)} %reshape.157.wanted, bf16[8,160,128]{2,1,0:T(8,128)(2,1)S(1)} %all-to-all-done.2.blocks), custom_call_target="tpu_custom_call" | custom-call | tf_op jit(solution)/shard_map/pallas_call | solution.py:318
  103.1 5.4 %all-to-all-start.3 = ((bf16[8,160,128]{2,1,0:T(8,128)(2,1)}), bf16[8,160,128]{2,1,0:T(8,128)(2,1)S(1)}, u32[]{:S(2)}, u32[]{:S(2)}) async-start(bf16[8,160,128]{2,1,0:T(8,128)(2,1)} %shard_map.95), calls=%async_computation.3 | async-start | bytes 655360 | tf_op jit(solution)/shard_map/all_to_all | solution.py:326
  108.6 0.1 fusion.5.facts
  108.7 7.0 %all-to-all-done.3.blocks = bf16[8,160,128]{2,1,0:T(8,128)(2,1)S(1)} async-done(((bf16[8,160,128]{2,1,0:T(8,128)(2,1)}), bf16[8,160,128]{2,1,0:T(8,128)(2,1)S(1)}, u32[]{:S(2)}, u32[]{:S(2)}) %all-to-all-start.3) | async-done | bytes 327712 | tf_op jit(solution)/shard_map/all_to_all | solution.py:326
  115.7 1.4 %shard_map.96 = bf16[160,248]{1,0:T(8,128)(2,1)} custom-call(s32[3]{0:T(128)S(1)} %fusion.5.facts, bf16[8,160,128]{2,1,0:T(8,128)(2,1)S(1)} %all-to-all-done.3.blocks), custom_call_target="tpu_custom_call" | custom-call | tf_op jit(solution)/shard_map/pallas_call | solution.py:327
  (4 shorter events, 0.0 us)
Async XLA Ops:
  8.1 25.6 %all-to-all-start = ((bf16[8,40,640]{2,1,0:T(8,128)(2,1)}), bf16[8,40,640]{2,1,0:T(8,128)(2,1)S(1)}, u32[]{:S(2)}, u32[]{:S(2)}) async-start(bf16[8,40,640]{2,1,0:T(8,128)(2,1)} %broadcast_in_dim.50), calls=%async_computation | async-start | bytes 819200 | tf_op jit(solution)/shard_map/all_to_all | solution.py:235
  19.0 7.7 %copy-start = (s32[64]{0:T(128)S(1)}, s32[64]{0:T(128)}, u32[]{:S(2)}) copy-start(s32[64]{0:T(128)} %offsets.1) | copy-start | bytes 772
  19.0 46.1 %all-gather.3.cloned.1.call-start = ((), (), s32[]{:S(2)}) async-start(), calls=%async_computation.4 | async-start | bytes 2048000 | tf_op jit(solution)/shard_map/all_gather | solution.py:268
  22.6 4.1 %collective-permute-start = (bf16[320,512]{1,0:T(8,128)(2,1)S(1)}, bf16[320,512]{1,0:T(8,128)(2,1)S(1)}, u32[]{:S(2)}, u32[]{:S(2)}) collective-permute-start(bf16[320,512]{1,0:T(8,128)(2,1)S(1)} %get-tuple-element.14.near), channel_id=1, source_target_pairs={{0,1},{1,0},{2,3},{3,2},{4,5},{5,4},{6,7},{7,6},{8,9},{9,8},{10,11... | collective-permute-start | bytes 983048 | tf_op jit(solution)/shard_map/ppermute | solution.py:25
  33.7 0.8 copy-start.1
  34.5 38.6 %all-to-all-start.1 = ((bf16[8,160,512]{2,1,0:T(8,128)(2,1)}), bf16[8,160,512]{2,1,0:T(8,128)(2,1)S(1)}, u32[]{:S(2)}, u32[]{:S(2)}) async-start(bf16[8,160,512]{2,1,0:T(8,128)(2,1)} %shard_map.92), calls=%async_computation.1 | async-start | bytes 2621440 | tf_op jit(solution)/shard_map/all_to_all | solution.py:272
  65.1 4.2 %copy-start.3 = (s32[64]{0:T(128)S(1)}, s32[64]{0:T(128)}, u32[]{:S(2)}) copy-start(s32[64]{0:T(128)} %param.18) | copy-start | bytes 772
  66.7 9.7 %collective-permute-start.1 = (bf16[1280,640]{1,0:T(8,128)(2,1)S(1)}, bf16[1280,640]{1,0:T(8,128)(2,1)}, u32[]{:S(2)}, u32[]{:S(2)}) collective-permute-start(bf16[1280,640]{1,0:T(8,128)(2,1)S(1)} %bitcast.15), channel_id=1, source_target_pairs={{0,1},{1,0},{2,3},{3,2},{4,5},{5,4},{6,7},{7,6},{8,9},{9,8},{10,11... | collective-permute-start | bytes 4915208 | tf_op jit(solution)/shard_map/ppermute | solution.py:25
  76.5 12.6 %copy-start.2 = (s32[64,2]{0,1:T(2,128)S(1)}, s32[64,2]{0,1:T(2,128)}, u32[]{:S(2)}) copy-start(s32[64,2]{0,1:T(2,128)} %param.16) | copy-start | bytes 1540
  81.9 19.9 %all-to-all-start.2 = ((bf16[8,160,128]{2,1,0:T(8,128)(2,1)}), bf16[8,160,128]{2,1,0:T(8,128)(2,1)S(1)}, u32[]{:S(2)}, u32[]{:S(2)}) async-start(bf16[8,160,128]{2,1,0:T(8,128)(2,1)} %shard_map.94), calls=%async_computation.2 | async-start | bytes 655360 | tf_op jit(solution)/shard_map/all_to_all | solution.py:317
  103.1 12.6 %all-to-all-start.3 = ((bf16[8,160,128]{2,1,0:T(8,128)(2,1)}), bf16[8,160,128]{2,1,0:T(8,128)(2,1)S(1)}, u32[]{:S(2)}, u32[]{:S(2)}) async-start(bf16[8,160,128]{2,1,0:T(8,128)(2,1)} %shard_map.95), calls=%async_computation.3 | async-start | bytes 655360 | tf_op jit(solution)/shard_map/all_to_all | solution.py:326
Sparse Core Ops, SparseCore 0:
  34.6 30.4 all-gather.2

commit v6 on v5

--- a/solution.py
+++ b/solution.py
@@ -37,7 +37,7 @@
 
 def front_kernel(
     offsets_hbm,
-    patches_hbm,
+    patches,
     row_hbm,
     col_hbm,
     weight_hbm,
@@ -45,7 +45,6 @@
     queries,
     pairs,
     resid,
-    patches,
     tables,
     weight,
     offsets,
@@ -56,10 +55,9 @@
     copies = [
         pltpu.make_async_copy(row_hbm, tables.at[pl.ds(0, side), :], sems.at[0]),
         pltpu.make_async_copy(col_hbm, tables.at[pl.ds(side, side), :], sems.at[1]),
-        pltpu.make_async_copy(patches_hbm, patches, sems.at[2]),
-        pltpu.make_async_copy(weight_hbm, weight, sems.at[3]),
+        pltpu.make_async_copy(weight_hbm, weight, sems.at[2]),
     ]
-    offsets_copy = pltpu.make_async_copy(offsets_hbm, offsets, sems.at[5])
+    offsets_copy = pltpu.make_async_copy(offsets_hbm, offsets, sems.at[4])
     offsets_copy.start()
     for copy in copies:
         copy.start()
@@ -80,14 +78,13 @@
     copies[0].wait()
     copies[1].wait()
     embedded = dot(onehot, tables[...], ((1,), (0,)))
-    copies[2].wait()
     values = patches[...].astype(jnp.float32) + embedded
     for tile in range(resid.shape[0]):
         resid[tile] = values[:, tile * LANES : (tile + 1) * LANES]
-    resid_copy = pltpu.make_async_copy(resid, resid_hbm, sems.at[4])
+    resid_copy = pltpu.make_async_copy(resid, resid_hbm, sems.at[3])
     resid_copy.start()
     normed = normalize(values).astype(jnp.bfloat16)
-    copies[3].wait()
+    copies[2].wait()
     width = weight.shape[1]
     wide = weight[...].reshape(3 * width, weight.shape[2])
     out = dot(wide, normed, ((1,), (1,))).astype(jnp.bfloat16)
@@ -96,37 +93,58 @@
     resid_copy.wait()
 
 
-def attend_kernel(offsets, queries, near, far, out):
-    rows = queries.shape[1]
+def block_scores(offsets, block, query, other):
+    rows = query.shape[1]
+    place = lax.axis_index("tok")
+    border = offsets[place // 2 * 2 + 1]
+    key_place = jnp.where(place % 2 == 0, place + 1, place - 1) if other else place
+    query_pos = place * rows + lax.broadcasted_iota(jnp.int32, (1, rows), 1)
+    key_pos = key_place * rows + lax.broadcasted_iota(jnp.int32, (rows, 1), 0)
+    query_side = jnp.where(query_pos >= border, 1, 0)
+    key_side = jnp.where(key_pos >= border, 1, 0)
+    scores = dot(block, query, ((0,), (0,))) * SCALE
+    return jnp.where(key_side == query_side, scores, MASKED)
+
+
+def near_kernel(offsets, queries, near, mixed, stats):
     width = queries.shape[0]
-    place = lax.axis_index("tok")
-    core = place % 2
-    border = offsets[place // 2 * 2 + 1]
-    ahead = jnp.where(core == 0, rows, -rows)
-    query_pos = place * rows + lax.broadcasted_iota(jnp.int32, (1, rows), 1)
-    key_pos = place * rows + lax.broadcasted_iota(jnp.int32, (rows, 1), 0)
-    query_side = jnp.where(query_pos >= border, 1, 0)
-    near_side = jnp.where(key_pos >= border, 1, 0)
-    far_side = jnp.where(key_pos + ahead >= border, 1, 0)
     for head in range(width // HEAD_DIM):
         own = slice(head * HEAD_DIM, (head + 1) * HEAD_DIM)
         value = slice(width + head * HEAD_DIM, width + (head + 1) * HEAD_DIM)
-        query = queries[own, :]
-        near_scores = dot(near[own, :], query, ((0,), (0,)))
-        far_scores = dot(far[own, :], query, ((0,), (0,)))
-        near_scores = jnp.where(near_side == query_side, near_scores * SCALE, MASKED)
-        far_scores = jnp.where(far_side == query_side, far_scores * SCALE, MASKED)
-        top = jnp.maximum(
-            jnp.max(near_scores, axis=0, keepdims=True), jnp.max(far_scores, axis=0, keepdims=True)
-        )
-        near_expo = jnp.exp(near_scores - top)
-        far_expo = jnp.exp(far_scores - top)
-        total = jnp.sum(near_expo, axis=0, keepdims=True) + jnp.sum(far_expo, axis=0, keepdims=True)
-        mixed = dot(near[value, :], near_expo.astype(jnp.bfloat16), ((1,), (0,)))
-        mixed += dot(far[value, :], far_expo.astype(jnp.bfloat16), ((1,), (0,)))
-        mixed = (mixed / total).astype(jnp.bfloat16)
+        scores = block_scores(offsets, near[own, :], queries[own, :], False)
+        top = jnp.max(scores, axis=0, keepdims=True)
+        expo = jnp.exp(scores - top)
+        stats[2 * head : 2 * head + 1, :] = top
+        stats[2 * head + 1 : 2 * head + 2, :] = jnp.sum(expo, axis=0, keepdims=True)
+        mixed[own, :] = dot(near[value, :], expo.astype(jnp.bfloat16), ((1,), (0,)))
+
+
+def far_kernel(offsets, queries, far, near_mixed, stats, out, attended, sems):
+    width = queries.shape[0]
+    copies = []
+    for head in range(width // HEAD_DIM):
+        own = slice(head * HEAD_DIM, (head + 1) * HEAD_DIM)
+        value = slice(width + head * HEAD_DIM, width + (head + 1) * HEAD_DIM)
+        scores = block_scores(offsets, far[own, :], queries[own, :], True)
+        near_top = stats[2 * head : 2 * head + 1, :]
+        top = jnp.maximum(near_top, jnp.max(scores, axis=0, keepdims=True))
+        expo = jnp.exp(scores - top)
+        scale = jnp.exp(near_top - top)
+        total = stats[2 * head + 1 : 2 * head + 2, :] * scale
+        total += jnp.sum(expo, axis=0, keepdims=True)
+        mixed = near_mixed[own, :] * scale
+        mixed += dot(far[value, :], expo.astype(jnp.bfloat16), ((1,), (0,)))
+        attended[own, :] = (mixed / total).astype(jnp.bfloat16)
+        part = pl.ds(head * HEAD_DIM, HEAD_DIM)
         for copy in range(out.shape[0]):
-            out[copy, own, :] = mixed
+            copies.append(
+                pltpu.make_async_copy(
+                    attended.at[part, :], out.at[copy, part, :], sems.at[head, copy]
+                )
+            )
+            copies[-1].start()
+    for copy in copies:
+        copy.wait()
 
 
 def project_kernel(
@@ -153,29 +171,50 @@
     merge_copy.wait()
 
 
-def merge_kernel(attended, weight, partial, merge_weight, out, total):
+def merge_kernel(
+    attended, weight_hbm, partial, merge_weight, out, weight, total, block, weight_sems, sems
+):
+    chunks = [(start, min(256, weight.shape[1] - start)) for start in range(0, weight.shape[1], 256)]
+    loads = [
+        pltpu.make_async_copy(
+            weight_hbm.at[:, pl.ds(start, size)],
+            weight.at[:, pl.ds(start, size)],
+            weight_sems.at[chunk],
+        )
+        for chunk, (start, size) in enumerate(chunks)
+    ]
+    for load in loads:
+        load.start()
     core = lax.axis_index("tok") % 2
     tiles, rows = partial.shape[:2]
-    part = dot(attended[...], weight[...], ((1,), (0,)))
     for tile in range(tiles // 2):
         place = core * (tiles // 2) + tile
         total[place] = partial[place]
-        place = (1 - core) * (tiles // 2) + tile
-        total[place] = partial[place] + part[:, tile * LANES : (tile + 1) * LANES]
+    for load, (start, size) in zip(loads, chunks):
+        load.wait()
+        part = dot(attended[...], weight[:, start : start + size], ((1,), (0,)))
+        for tile in range(size // LANES):
+            place = (1 - core) * (tiles // 2) + start // LANES + tile
+            total[place] = partial[place] + part[:, tile * LANES : (tile + 1) * LANES]
     values = jnp.concatenate([total[tile] for tile in range(tiles)], axis=1)
     normed = normalize(values)
     for tile in range(tiles):
         total[tile] = normed[:, tile * LANES : (tile + 1) * LANES]
     width = tiles * LANES
-    projected = jnp.zeros(out.shape[1:], jnp.float32)
+    projected = jnp.zeros(block.shape, jnp.float32)
     for quarter in range(4):
         part = [total[tile, pl.ds(quarter, rows // 4, stride=4), :] for tile in range(tiles)]
         part = jnp.concatenate(part, axis=1).astype(jnp.bfloat16)
         weight = merge_weight[:, quarter * width : (quarter + 1) * width]
         projected += dot(weight, part, ((1,), (1,)))
-    projected = projected.astype(out.dtype)
-    for copy in range(out.shape[0]):
-        out[copy] = projected
+    block[...] = projected.astype(block.dtype)
+    copies = [
+        pltpu.make_async_copy(block, out.at[copy], sems.at[copy]) for copy in range(out.shape[0])
+    ]
+    for copy in copies:
+        copy.start()
+    for copy in copies:
+        copy.wait()
 
 
 def pick_kernel(wanted, blocks, out, sems):
@@ -241,29 +280,47 @@
             jax.ShapeDtypeStruct((width_here, block_rows), jnp.bfloat16),
             jax.ShapeDtypeStruct((2 * width_here, block_rows), jnp.bfloat16),
         ),
-        in_specs=[HBM] * 5,
+        in_specs=[HBM, VMEM, HBM, HBM, HBM],
         out_specs=(HBM, VMEM, VMEM),
         scratch_shapes=[
             pltpu.VMEM((width // LANES, block_rows, LANES), jnp.float32),
-            pltpu.VMEM(patches.shape, jnp.bfloat16),
             pltpu.VMEM((2 * row_table.shape[0], width), jnp.bfloat16),
             pltpu.VMEM(qkv_weight.shape, jnp.bfloat16),
             pltpu.SMEM(image_offsets.shape, jnp.int32),
-            pltpu.SemaphoreType.DMA((6,)),
+            pltpu.SemaphoreType.DMA((5,)),
         ],
         compiler_params=params,
         cost_estimate=pl.CostEstimate(
             flops=3 * 2 * block_rows * width * width_here, bytes_accessed=8 * 2**20, transcendentals=0
         ),
-    )(*map(at_hbm, (image_offsets, patches, row_table, col_table, qkv_weight)))
+    )(at_hbm(image_offsets), patches, *map(at_hbm, (row_table, col_table, qkv_weight)))
     far = partner(near, "tok", 0)
+    mixed, stats = pl.pallas_call(
+        near_kernel,
+        out_shape=(
+            jax.ShapeDtypeStruct((width_here, block_rows), jnp.float32),
+            jax.ShapeDtypeStruct((2 * width_here // HEAD_DIM, block_rows), jnp.float32),
+        ),
+        in_specs=[SMEM, VMEM, VMEM],
+        out_specs=(VMEM, VMEM),
+        compiler_params=params,
+        cost_estimate=pl.CostEstimate(
+            flops=4 * block_rows * block_rows * width_here,
+            bytes_accessed=2**21,
+            transcendentals=block_rows * block_rows * 2,
+        ),
+    )(image_offsets, queries, near)
     sent = pl.pallas_call(
-        attend_kernel,
-        out_shape=jax.ShapeDtypeStruct((group, width_here, block_rows), jnp.bfloat16),
-        in_specs=[SMEM, VMEM, VMEM, VMEM],
-        out_specs=VMEM,
-        compiler_params=params,
-    )(image_offsets, queries, near, far)
+        far_kernel,
+        out_shape=pltpu.HBM((group, width_here, block_rows), jnp.bfloat16),
+        in_specs=[SMEM, VMEM, VMEM, VMEM, VMEM],
+        out_specs=HBM,
+        scratch_shapes=[
+            pltpu.VMEM((width_here, block_rows), jnp.bfloat16),
+            pltpu.SemaphoreType.DMA((width_here // HEAD_DIM, group)),
+        ],
+        compiler_params=params,
+    )(image_offsets, queries, far, mixed, stats)
     pieces, sent = lax.optimization_barrier((pieces, sent))
     own_weight = lax.all_gather(pieces, "tok", axis=0, axis_index_groups=rings_x)
     own_weight = own_weight.transpose(1, 0, 2, 3).reshape(group * width_here, columns)
@@ -271,7 +328,7 @@
 
     gathered = lax.all_to_all(sent, "head", 0, 0, tiled=True)
     rows_here = block_rows // 4
-    blocks_shape = jax.ShapeDtypeStruct((RING, width_here, rows_here), jnp.bfloat16)
+    blocks_shape = pltpu.HBM((RING, width_here, rows_here), jnp.bfloat16)
     tiles = width // LANES
     half_flops = 2 * block_rows * width * columns
     attended, partial, merge_here = pl.pallas_call(
@@ -295,11 +352,17 @@
     projected = pl.pallas_call(
         merge_kernel,
         out_shape=blocks_shape,
-        in_specs=[VMEM, VMEM, VMEM, VMEM],
-        out_specs=VMEM,
-        scratch_shapes=[pltpu.VMEM((tiles, block_rows, LANES), jnp.float32)],
-        compiler_params=params,
-    )(attended, other_weight, partial, merge_here)
+        in_specs=[VMEM, HBM, VMEM, VMEM],
+        out_specs=HBM,
+        scratch_shapes=[
+            pltpu.VMEM(other_weight.shape, jnp.bfloat16),
+            pltpu.VMEM((tiles, block_rows, LANES), jnp.float32),
+            pltpu.VMEM((width_here, rows_here), jnp.bfloat16),
+            pltpu.SemaphoreType.DMA((columns // 256 + 1,)),
+            pltpu.SemaphoreType.DMA((RING,)),
+        ],
+        compiler_params=params,
+    )(attended, at_hbm(other_weight), partial, merge_here)
 
     image_ids = jnp.arange(owners.shape[0], dtype=jnp.int32)
     place_ids = jnp.arange(places, dtype=jnp.int32)

time: 125 us -> 124 us (level)
    pallas_call x2 -> x3, Pallas kernels: 9.21 us -> 10 us  [the longest x1 5.49 us: on_device(): pl.pallas_call(merge_kernel, out_shape=blocks_shape, in_specs=[VMEM, HBM,...]
  transfers between devices with their start and end apart: 7 -> 7, of which waited for: 6 -> 5; matrix products, arithmetic and copies ran while one was open for 2% -> 2% of each run, Pallas kernels for 9% -> 9%
where the time goes in v6:
time: 124 us
  waiting for transfers between devices  53.9 us (43%)
  starting transfers between devices  32.4 us (26%)
  Pallas kernels  19.3 us (16%)
  between operations  13.6 us (11%)
  local copies, waits for them, and re-layouts  4.25 us (3%)
    all_gather x1, waiting for transfers between devices, on_device(): lax.all_gather(pieces, 'tok', axis=0, axis_index_groups=rings_x)  26.1 us
    all_to_all x1, waiting for transfers between devices, on_device(): lax.all_to_all(projected, 'tok', 0, 0, axis_index_groups=rings_y, tiled=T...  12.6 us
    all_to_all x1, starting transfers between devices, on_device(): pieces = lax.all_to_all(pieces, 'head', 0, 0, tiled=True)  10.9 us
    all_to_all x1, waiting for transfers between devices, on_device(): lax.all_to_all(blocks, 'tok', 0, 0, axis_index_groups=planes, tiled=True)  6.98 us
    all_to_all x1, starting transfers between devices, on_device(): lax.all_to_all(projected, 'tok', 0, 0, axis_index_groups=rings_y, tiled=T...  6.84 us
    all_to_all x1, starting transfers between devices, on_device(): lax.all_to_all(blocks, 'tok', 0, 0, axis_index_groups=planes, tiled=True)  5.67 us
    pallas_call x1, Pallas kernels, on_device(): pl.pallas_call(merge_kernel, out_shape=blocks_shape, in_specs=[VMEM, HBM,...  5.49 us
    ppermute x2, starting transfers between devices, partner(): lax.ppermute(x, axis, [(i, i ^ 1 << apart) for i in range(lax.axis_size(a...  5.45 us
  transfers between devices with their start and end apart: 7, of which 5 were waited for; matrix products, arithmetic and copies ran while one was open for 2% of the time, Pallas kernels for 9%

profile of v6, /device:TPU:1, one launch (start us, length us, event | category | flops | bytes accessed | tf_op | source)
XLA Modules:
  0.0 123.9 jit_solution(5235802662775496311)
XLA Ops:
  6.5 0.0 copy-start
  6.5 0.9 dynamic_slice.3
  7.4 0.8 broadcast_in_dim.50
  8.3 10.9 %all-to-all-start = ((bf16[8,40,640]{2,1,0:T(8,128)(2,1)}), bf16[8,40,640]{2,1,0:T(8,128)(2,1)S(1)}, u32[]{:S(2)}, u32[]{:S(2)}) async-start(bf16[8,40,640]{2,1,0:T(8,128)(2,1)} %broadcast_in_dim.50), calls=%async_computation | async-start | bytes 819200 | tf_op jit(solution)/shard_map/all_to_all | solution.py:274
  19.1 0.0 copy-start.1
  19.1 0.0 all-gather.3.cloned.1.call-start
  19.2 0.0 copy-done
  19.2 3.3 %shard_map.91 = (f32[10,512,128]{2,1,0:T(8,128)}, bf16[160,512]{1,0:T(8,128)(2,1)S(1)}, bf16[320,512]{1,0:T(8,128)(2,1)S(1)}) custom-call(s32[64]{0:T(128)} %offsets.3, bf16[512,1280]{1,0:T(8,128)(2,1)S(1)} %copy-done, bf16[64,1280]{1,0:T(8,128)(2,1)} %row_hbm.1, bf16[64,1280]{1,0:T(8,128)(2,1)} %col_hbm.1, bf16[3,160,1280]{2,1,0:T(8,128)(2,1)} %weight_hbm.1), custom_call_target="tpu_custom_call" | custom-call | flops 629145600 | bytes 8388608 | tf_op jit(solution)/shard_map/pallas_call | solution.py:276
  22.5 2.9 %collective-permute-start = (bf16[320,512]{1,0:T(8,128)(2,1)S(1)}, bf16[320,512]{1,0:T(8,128)(2,1)S(1)}, u32[]{:S(2)}, u32[]{:S(2)}) collective-permute-start(bf16[320,512]{1,0:T(8,128)(2,1)S(1)} %get-tuple-element.16.near), channel_id=1, source_target_pairs={{0,1},{1,0},{2,3},{3,2},{4,5},{5,4},{6,7},{7,6},{8,9},{9,8},{10,11... | collective-permute-start | bytes 983048 | tf_op jit(solution)/shard_map/ppermute | solution.py:25
  25.3 0.0 copy-done.1
  25.4 1.7 %shard_map.92 = (f32[160,512]{1,0:T(8,128)S(1)}, f32[4,512]{1,0:T(4,128)S(1)}) custom-call(s32[64]{0:T(128)S(1)} %copy-done.1, bf16[160,512]{1,0:T(8,128)(2,1)S(1)} %get-tuple-element.15.queries, bf16[320,512]{1,0:T(8,128)(2,1)S(1)} %get-tuple-element.16.near), custom_call_target="tpu_custom_call" | custom-call | flops 167772160 | bytes 2097152 | tf_op jit(solution)/shard_map/pallas_call | solution.py:298
  27.1 0.0 collective-permute-done.far
  27.1 2.8 %shard_map.93 = bf16[8,160,512]{2,1,0:T(8,128)(2,1)} custom-call(s32[64]{0:T(128)S(1)} %copy-done.1, bf16[160,512]{1,0:T(8,128)(2,1)S(1)} %get-tuple-element.15.queries, bf16[320,512]{1,0:T(8,128)(2,1)S(1)} %collective-permute-done.far, f32[160,512]{1,0:T(8,128)S(1)} %get-tuple-element.17.near_mixed, f32[4,512]{1,0:T(4,128)S(1)} %get-tuple-element.18.stats), custom_call_target="tpu_custom_call" | custom-call | tf_op jit(solution)/shard_map/pallas_call | solution.py:313
  29.9 3.9 %all-to-all-done = bf16[8,40,640]{2,1,0:T(8,128)(2,1)S(1)} async-done(((bf16[8,40,640]{2,1,0:T(8,128)(2,1)}), bf16[8,40,640]{2,1,0:T(8,128)(2,1)S(1)}, u32[]{:S(2)}, u32[]{:S(2)}) %all-to-all-start) | async-done | bytes 409632 | tf_op jit(solution)/shard_map/all_to_all | solution.py:274
  33.8 0.0 copy-start.2
  33.8 0.8 copy-done.2
  34.6 0.0 all-gather.3.cloned.1.call-update
  34.6 3.6 %all-to-all-start.1 = ((bf16[8,160,512]{2,1,0:T(8,128)(2,1)}), bf16[8,160,512]{2,1,0:T(8,128)(2,1)S(1)}, u32[]{:S(2)}, u32[]{:S(2)}) async-start(bf16[8,160,512]{2,1,0:T(8,128)(2,1)} %shard_map.93), calls=%async_computation.1 | async-start | bytes 2621440 | tf_op jit(solution)/shard_map/all_to_all | solution.py:329
  38.2 26.1 %all-gather.3.cloned.1.call-done = bf16[32,40,640]{2,1,0:T(8,128)(2,1)} async-done(((bf16[8,40,640]{2,1,0:T(8,128)(2,1)}), bf16[32,40,640]{2,1,0:T(8,128)(2,1)}) %all-gather.3.cloned.1.call-update) | async-done | bytes 1638416 | tf_op jit(solution)/shard_map/all_gather | solution.py:325
  64.3 0.0 copy-start.4
  64.3 1.6 %copy.12 = bf16[8,4,40,640]{3,2,1,0:T(8,128)(2,1)S(1)} copy(bf16[8,4,40,640]{3,2,0,1:T(8,128)(2,1)} %bitcast.17) | data formatting | bytes 3276800 | tf_op jit(solution)/shard_map/transpose | solution.py:326
  65.9 2.6 %collective-permute-start.1 = (bf16[1280,640]{1,0:T(8,128)(2,1)S(1)}, bf16[1280,640]{1,0:T(8,128)(2,1)}, u32[]{:S(2)}, u32[]{:S(2)}) collective-permute-start(bf16[1280,640]{1,0:T(8,128)(2,1)S(1)} %bitcast.15), channel_id=1, source_target_pairs={{0,1},{1,0},{2,3},{3,2},{4,5},{5,4},{6,7},{7,6},{8,9},{9,8},{10,11... | collective-permute-start | bytes 4915208 | tf_op jit(solution)/shard_map/ppermute | solution.py:25
  68.5 0.0 copy-done.4
  68.5 0.1 select_reduce_fusion
  68.6 4.3 %all-to-all-done.1.gathered = bf16[8,160,512]{2,1,0:T(8,128)(2,1)S(1)} async-done(((bf16[8,160,512]{2,1,0:T(8,128)(2,1)}), bf16[8,160,512]{2,1,0:T(8,128)(2,1)S(1)}, u32[]{:S(2)}, u32[]{:S(2)}) %all-to-all-start.1) | async-done | bytes 1310752 | tf_op jit(solution)/shard_map/all_to_all | solution.py:329
  72.9 3.4 %shard_map.94 = (bf16[512,1280]{1,0:T(8,128)(2,1)S(1)}, f32[10,512,128]{2,1,0:T(8,128)S(1)}, bf16[160,5120]{1,0:T(8,128)(2,1)S(1)}) custom-call(bf16[8,160,512]{2,1,0:T(8,128)(2,1)S(1)} %all-to-all-done.1.gathered, bf16[1280,640]{1,0:T(8,128)(2,1)S(1)} %bitcast.16, f32[10,512,128]{2,1,0:T(8,128)} %get-tuple-element.21.resid_hbm, bf16[160,5120]{1,0:T(8,128)(2,1)} %merge_hbm.1), custom_call_target="tpu_custom_call" | custom-call | flops 838860800 | bytes 8388608 | tf_op jit(solution)/shard_map/pallas_call | solution.py:334
  76.3 0.0 collective-permute-done.1.weight_hbm
  76.3 0.0 copy-start.3
  76.3 5.5 %shard_map.95 = bf16[8,160,128]{2,1,0:T(8,128)(2,1)} custom-call(bf16[512,1280]{1,0:T(8,128)(2,1)S(1)} %get-tuple-element.22.attended, bf16[1280,640]{1,0:T(8,128)(2,1)} %collective-permute-done.1.weight_hbm, f32[10,512,128]{2,1,0:T(8,128)S(1)} %get-tuple-element.23.partial, bf16[160,5120]{1,0:T(8,128)(2,1)S(1)} %get-tuple-element.24.merge_weight), custom_call_target="tpu_custom_call" | custom-call | tf_op jit(solution)/shard_map/pallas_call | solution.py:352
  81.8 6.8 %all-to-all-start.2 = ((bf16[8,160,128]{2,1,0:T(8,128)(2,1)}), bf16[8,160,128]{2,1,0:T(8,128)(2,1)S(1)}, u32[]{:S(2)}, u32[]{:S(2)}) async-start(bf16[8,160,128]{2,1,0:T(8,128)(2,1)} %shard_map.95), calls=%async_computation.2 | async-start | bytes 655360 | tf_op jit(solution)/shard_map/all_to_all | solution.py:380
  88.7 0.1 reduce_sum.31
  88.8 0.1 fusion.3
  88.9 0.1 reshape.157.wanted
  89.0 0.0 copy-done.3
  89.0 12.6 %all-to-all-done.2.blocks = bf16[8,160,128]{2,1,0:T(8,128)(2,1)S(1)} async-done(((bf16[8,160,128]{2,1,0:T(8,128)(2,1)}), bf16[8,160,128]{2,1,0:T(8,128)(2,1)S(1)}, u32[]{:S(2)}, u32[]{:S(2)}) %all-to-all-start.2) | async-done | bytes 327712 | tf_op jit(solution)/shard_map/all_to_all | solution.py:380
  101.5 1.3 %shard_map.96 = bf16[8,160,128]{2,1,0:T(8,128)(2,1)} custom-call(s32[8]{0:T(128)S(1)} %reshape.157.wanted, bf16[8,160,128]{2,1,0:T(8,128)(2,1)S(1)} %all-to-all-done.2.blocks), custom_call_target="tpu_custom_call" | custom-call | tf_op jit(solution)/shard_map/pallas_call | solution.py:381
  102.9 5.7 %all-to-all-start.3 = ((bf16[8,160,128]{2,1,0:T(8,128)(2,1)}), bf16[8,160,128]{2,1,0:T(8,128)(2,1)S(1)}, u32[]{:S(2)}, u32[]{:S(2)}) async-start(bf16[8,160,128]{2,1,0:T(8,128)(2,1)} %shard_map.96), calls=%async_computation.3 | async-start | bytes 655360 | tf_op jit(solution)/shard_map/all_to_all | solution.py:389
  108.6 0.1 fusion.5.facts
  108.7 7.0 %all-to-all-done.3.blocks = bf16[8,160,128]{2,1,0:T(8,128)(2,1)S(1)} async-done(((bf16[8,160,128]{2,1,0:T(8,128)(2,1)}), bf16[8,160,128]{2,1,0:T(8,128)(2,1)S(1)}, u32[]{:S(2)}, u32[]{:S(2)}) %all-to-all-start.3) | async-done | bytes 327712 | tf_op jit(solution)/shard_map/all_to_all | solution.py:389
  115.7 1.4 %shard_map.97 = bf16[160,248]{1,0:T(8,128)(2,1)} custom-call(s32[3]{0:T(128)S(1)} %fusion.5.facts, bf16[8,160,128]{2,1,0:T(8,128)(2,1)S(1)} %all-to-all-done.3.blocks), custom_call_target="tpu_custom_call" | custom-call | tf_op jit(solution)/shard_map/pallas_call | solution.py:390
  (4 shorter events, 0.0 us)
Async XLA Ops:
  6.5 12.6 %copy-start = (bf16[512,1280]{1,0:T(8,128)(2,1)S(1)}, bf16[512,1280]{1,0:T(8,128)(2,1)}, u32[]{:S(2)}) copy-start(bf16[512,1280]{1,0:T(8,128)(2,1)} %patches.1) | copy-start | bytes 3932164
  8.3 25.6 %all-to-all-start = ((bf16[8,40,640]{2,1,0:T(8,128)(2,1)}), bf16[8,40,640]{2,1,0:T(8,128)(2,1)S(1)}, u32[]{:S(2)}, u32[]{:S(2)}) async-start(bf16[8,40,640]{2,1,0:T(8,128)(2,1)} %broadcast_in_dim.50), calls=%async_computation | async-start | bytes 819200 | tf_op jit(solution)/shard_map/all_to_all | solution.py:274
  19.1 6.2 %copy-start.1 = (s32[64]{0:T(128)S(1)}, s32[64]{0:T(128)}, u32[]{:S(2)}) copy-start(s32[64]{0:T(128)} %offsets.3) | copy-start | bytes 772
  19.1 45.2 %all-gather.3.cloned.1.call-start = ((), (), s32[]{:S(2)}) async-start(), calls=%async_computation.4 | async-start | bytes 2048000 | tf_op jit(solution)/shard_map/all_gather | solution.py:325
  22.5 4.6 %collective-permute-start = (bf16[320,512]{1,0:T(8,128)(2,1)S(1)}, bf16[320,512]{1,0:T(8,128)(2,1)S(1)}, u32[]{:S(2)}, u32[]{:S(2)}) collective-permute-start(bf16[320,512]{1,0:T(8,128)(2,1)S(1)} %get-tuple-element.16.near), channel_id=1, source_target_pairs={{0,1},{1,0},{2,3},{3,2},{4,5},{5,4},{6,7},{7,6},{8,9},{9,8},{10,11... | collective-permute-start | bytes 983048 | tf_op jit(solution)/shard_map/ppermute | solution.py:25
  33.8 0.8 copy-start.2
  34.6 38.3 %all-to-all-start.1 = ((bf16[8,160,512]{2,1,0:T(8,128)(2,1)}), bf16[8,160,512]{2,1,0:T(8,128)(2,1)S(1)}, u32[]{:S(2)}, u32[]{:S(2)}) async-start(bf16[8,160,512]{2,1,0:T(8,128)(2,1)} %shard_map.93), calls=%async_computation.1 | async-start | bytes 2621440 | tf_op jit(solution)/shard_map/all_to_all | solution.py:329
  64.3 4.2 %copy-start.4 = (s32[64]{0:T(128)S(1)}, s32[64]{0:T(128)}, u32[]{:S(2)}) copy-start(s32[64]{0:T(128)} %param.18) | copy-start | bytes 772
  65.9 10.4 %collective-permute-start.1 = (bf16[1280,640]{1,0:T(8,128)(2,1)S(1)}, bf16[1280,640]{1,0:T(8,128)(2,1)}, u32[]{:S(2)}, u32[]{:S(2)}) collective-permute-start(bf16[1280,640]{1,0:T(8,128)(2,1)S(1)} %bitcast.15), channel_id=1, source_target_pairs={{0,1},{1,0},{2,3},{3,2},{4,5},{5,4},{6,7},{7,6},{8,9},{9,8},{10,11... | collective-permute-start | bytes 4915208 | tf_op jit(solution)/shard_map/ppermute | solution.py:25
  76.3 12.6 %copy-start.3 = (s32[64,2]{0,1:T(2,128)S(1)}, s32[64,2]{0,1:T(2,128)}, u32[]{:S(2)}) copy-start(s32[64,2]{0,1:T(2,128)} %param.16) | copy-start | bytes 1540
  81.8 19.7 %all-to-all-start.2 = ((bf16[8,160,128]{2,1,0:T(8,128)(2,1)}), bf16[8,160,128]{2,1,0:T(8,128)(2,1)S(1)}, u32[]{:S(2)}, u32[]{:S(2)}) async-start(bf16[8,160,128]{2,1,0:T(8,128)(2,1)} %shard_map.95), calls=%async_computation.2 | async-start | bytes 655360 | tf_op jit(solution)/shard_map/all_to_all | solution.py:380
  102.9 12.8 %all-to-all-start.3 = ((bf16[8,160,128]{2,1,0:T(8,128)(2,1)}), bf16[8,160,128]{2,1,0:T(8,128)(2,1)S(1)}, u32[]{:S(2)}, u32[]{:S(2)}) async-start(bf16[8,160,128]{2,1,0:T(8,128)(2,1)} %shard_map.96), calls=%async_computation.3 | async-start | bytes 655360 | tf_op jit(solution)/shard_map/all_to_all | solution.py:389
Sparse Core Ops, SparseCore 0:
  34.7 29.4 all-gather.2

commit v7 on v6

--- a/solution.py
+++ b/solution.py
@@ -322,8 +322,12 @@
         compiler_params=params,
     )(image_offsets, queries, far, mixed, stats)
     pieces, sent = lax.optimization_barrier((pieces, sent))
-    own_weight = lax.all_gather(pieces, "tok", axis=0, axis_index_groups=rings_x)
-    own_weight = own_weight.transpose(1, 0, 2, 3).reshape(group * width_here, columns)
+    own_weight = [
+        lax.all_gather(part, "tok", axis=0, axis_index_groups=rings_x)
+        for part in jnp.split(pieces, 2)
+    ]
+    own_weight = jnp.concatenate([part.transpose(1, 0, 2, 3) for part in own_weight], axis=0)
+    own_weight = own_weight.reshape(group * width_here, columns)
     other_weight = partner(own_weight, "tok", 0)
 
     gathered = lax.all_to_all(sent, "head", 0, 0, tiled=True)

time: 124 us -> 110 us (0.89)
  waiting for transfers between devices: 53.9 us -> 26.7 us
  blocking collectives: 0 us -> 24.1 us
  between operations: 13.6 us -> 0.21 us
  starting transfers between devices: 32.4 us -> 36.6 us
  local copies, waits for them, and re-layouts: 4.25 us -> 2.1 us
    all_gather x1 -> x0, waiting for transfers between devices: 26.1 us -> none  [on_device(): lax.all_gather(pieces, 'tok', axis=0, axis_index_groups=rings_x)]
    all_gather x0 -> x2, blocking collectives: none -> 24.1 us  [on_device(): lax.all_gather(part, 'tok', axis=0, axis_index_groups=rings_x)]
    ppermute x2, starting transfers between devices: 5.45 us -> 9.66 us  [partner(): lax.ppermute(x, axis, [(i, i ^ 1 << apart) for i in range(lax.axis_size(a...]
    transpose x1 -> x0, local copies, waits for them, and re-layouts: 1.58 us -> none  [on_device(): own_weight.transpose(1, 0, 2, 3).reshape(group * width_here, columns)]
  transfers between devices with their start and end apart: 7 -> 6, of which waited for: 5 -> 4; matrix products, arithmetic and copies ran while one was open for 2% -> 1% of each run, Pallas kernels for 9% -> 10%
where the time goes in v7:
time: 110 us
  starting transfers between devices  36.6 us (33%)
  waiting for transfers between devices  26.7 us (24%)
  blocking collectives  24.1 us (22%)
  Pallas kernels  19.5 us (18%)
  local copies, waits for them, and re-layouts  2.1 us (2%)
    all_gather x2, blocking collectives, on_device(): lax.all_gather(part, 'tok', axis=0, axis_index_groups=rings_x)  24.1 us
    all_to_all x1, waiting for transfers between devices, on_device(): lax.all_to_all(projected, 'tok', 0, 0, axis_index_groups=rings_y, tiled=T...  12.6 us
    all_to_all x1, starting transfers between devices, on_device(): pieces = lax.all_to_all(pieces, 'head', 0, 0, tiled=True)  10.9 us
    ppermute x2, starting transfers between devices, partner(): lax.ppermute(x, axis, [(i, i ^ 1 << apart) for i in range(lax.axis_size(a...  9.66 us
    all_to_all x1, waiting for transfers between devices, on_device(): lax.all_to_all(blocks, 'tok', 0, 0, axis_index_groups=planes, tiled=True)  6.98 us
    all_to_all x1, starting transfers between devices, on_device(): lax.all_to_all(projected, 'tok', 0, 0, axis_index_groups=rings_y, tiled=T...  6.84 us
    all_to_all x1, starting transfers between devices, on_device(): lax.all_to_all(blocks, 'tok', 0, 0, axis_index_groups=planes, tiled=True)  5.67 us
    pallas_call x1, Pallas kernels, on_device(): pl.pallas_call(merge_kernel, out_shape=blocks_shape, in_specs=[VMEM, HBM,...  5.47 us
  transfers between devices with their start and end apart: 6, of which 4 were waited for; matrix products, arithmetic and copies ran while one was open for 1% of the time, Pallas kernels for 10%

profile of v7, /device:TPU:1, one launch (start us, length us, event | category | flops | bytes accessed | tf_op | source)
XLA Modules:
  0.0 109.7 jit_solution(14314457394966390080)
XLA Ops:
  0.0 0.0 copy-start
  0.0 0.9 dynamic_slice.3
  0.9 0.8 broadcast_in_dim.50
  1.7 10.9 %all-to-all-start = ((bf16[8,40,640]{2,1,0:T(8,128)(2,1)}), bf16[8,40,640]{2,1,0:T(8,128)(2,1)S(1)}, u32[]{:S(2)}, u32[]{:S(2)}) async-start(bf16[8,40,640]{2,1,0:T(8,128)(2,1)} %broadcast_in_dim.50), calls=%async_computation | async-start | bytes 819200 | tf_op jit(solution)/shard_map/all_to_all | solution.py:274
  12.6 0.0 copy-done
  12.6 0.0 copy-start.1
  12.6 3.4 %shard_map.91 = (f32[10,512,128]{2,1,0:T(8,128)}, bf16[160,512]{1,0:T(8,128)(2,1)S(1)}, bf16[320,512]{1,0:T(8,128)(2,1)S(1)}) custom-call(s32[64]{0:T(128)} %offsets.3, bf16[512,1280]{1,0:T(8,128)(2,1)S(1)} %copy-done, bf16[64,1280]{1,0:T(8,128)(2,1)} %row_hbm.1, bf16[64,1280]{1,0:T(8,128)(2,1)} %col_hbm.1, bf16[3,160,1280]{2,1,0:T(8,128)(2,1)} %weight_hbm.1), custom_call_target="tpu_custom_call" | custom-call | flops 629145600 | bytes 8388608 | tf_op jit(solution)/shard_map/pallas_call | solution.py:276
  16.0 2.9 %collective-permute-start = (bf16[320,512]{1,0:T(8,128)(2,1)S(1)}, bf16[320,512]{1,0:T(8,128)(2,1)S(1)}, u32[]{:S(2)}, u32[]{:S(2)}) collective-permute-start(bf16[320,512]{1,0:T(8,128)(2,1)S(1)} %get-tuple-element.16.near), channel_id=1, source_target_pairs={{0,1},{1,0},{2,3},{3,2},{4,5},{5,4},{6,7},{7,6},{8,9},{9,8},{10,11... | collective-permute-start | bytes 983048 | tf_op jit(solution)/shard_map/ppermute | solution.py:25
  18.9 0.0 copy-done.1
  18.9 1.7 %shard_map.92 = (f32[160,512]{1,0:T(8,128)S(1)}, f32[4,512]{1,0:T(4,128)S(1)}) custom-call(s32[64]{0:T(128)S(1)} %copy-done.1, bf16[160,512]{1,0:T(8,128)(2,1)S(1)} %get-tuple-element.15.queries, bf16[320,512]{1,0:T(8,128)(2,1)S(1)} %get-tuple-element.16.near), custom_call_target="tpu_custom_call" | custom-call | flops 167772160 | bytes 2097152 | tf_op jit(solution)/shard_map/pallas_call | solution.py:298
  20.7 0.0 collective-permute-done.far
  20.7 2.8 %shard_map.93 = bf16[8,160,512]{2,1,0:T(8,128)(2,1)} custom-call(s32[64]{0:T(128)S(1)} %copy-done.1, bf16[160,512]{1,0:T(8,128)(2,1)S(1)} %get-tuple-element.15.queries, bf16[320,512]{1,0:T(8,128)(2,1)S(1)} %collective-permute-done.far, f32[160,512]{1,0:T(8,128)S(1)} %get-tuple-element.17.near_mixed, f32[4,512]{1,0:T(4,128)S(1)} %get-tuple-element.18.stats), custom_call_target="tpu_custom_call" | custom-call | tf_op jit(solution)/shard_map/pallas_call | solution.py:313
  23.5 3.9 %all-to-all-done = bf16[8,40,640]{2,1,0:T(8,128)(2,1)S(1)} async-done(((bf16[8,40,640]{2,1,0:T(8,128)(2,1)}), bf16[8,40,640]{2,1,0:T(8,128)(2,1)S(1)}, u32[]{:S(2)}, u32[]{:S(2)}) %all-to-all-start) | async-done | bytes 409632 | tf_op jit(solution)/shard_map/all_to_all | solution.py:274
  27.3 3.6 %all-to-all-start.1 = ((bf16[8,160,512]{2,1,0:T(8,128)(2,1)}), bf16[8,160,512]{2,1,0:T(8,128)(2,1)S(1)}, u32[]{:S(2)}, u32[]{:S(2)}) async-start(bf16[8,160,512]{2,1,0:T(8,128)(2,1)} %shard_map.93), calls=%async_computation.1 | async-start | bytes 2621440 | tf_op jit(solution)/shard_map/all_to_all | solution.py:333
  30.9 12.7 %all-gather = bf16[16,40,640]{2,1,0:T(8,128)(2,1)S(1)} all-gather(bf16[4,40,640]{2,1,0:T(8,128)(2,1)S(1)} %get-tuple-element.25), channel_id=2, replica_groups={{0,16,32,48},{1,17,33,49},{2,18,34,50},{3,19,35,51},{4,20,36,52},{5,21,..., dimensions={0}, use_global_device_ids=true | all-gather | bytes 1024000 | tf_op jit(solution)/shard_map/all_gather | solution.py:326
  43.7 11.4 %all-gather.1 = bf16[16,40,640]{2,1,0:T(8,128)(2,1)S(1)} all-gather(bf16[4,40,640]{2,1,0:T(8,128)(2,1)S(1)} %get-tuple-element.26), channel_id=3, replica_groups={{0,16,32,48},{1,17,33,49},{2,18,34,50},{3,19,35,51},{4,20,36,52},{5,21,..., dimensions={0}, use_global_device_ids=true | all-gather | bytes 1024000 | tf_op jit(solution)/shard_map/all_gather | solution.py:326
  55.0 0.2 pad_maximum_fusion
  55.2 0.0 copy-start.3
  55.2 0.1 copy.12
  55.4 6.8 %collective-permute-start.1 = (bf16[1280,640]{1,0:T(8,128)(2,1)S(1)}, bf16[1280,640]{1,0:T(8,128)(2,1)}, u32[]{:S(2)}, u32[]{:S(2)}) collective-permute-start(bf16[1280,640]{1,0:T(8,128)(2,1)S(1)} %bitcast.18), channel_id=1, source_target_pairs={{0,1},{1,0},{2,3},{3,2},{4,5},{5,4},{6,7},{7,6},{8,9},{9,8},{10,11... | collective-permute-start | bytes 4915208 | tf_op jit(solution)/shard_map/ppermute | solution.py:25
  62.2 0.0 copy-done.3
  62.2 0.1 select_reduce_fusion
  62.3 3.3 %all-to-all-done.1.gathered = bf16[8,160,512]{2,1,0:T(8,128)(2,1)S(1)} async-done(((bf16[8,160,512]{2,1,0:T(8,128)(2,1)}), bf16[8,160,512]{2,1,0:T(8,128)(2,1)S(1)}, u32[]{:S(2)}, u32[]{:S(2)}) %all-to-all-start.1) | async-done | bytes 1310752 | tf_op jit(solution)/shard_map/all_to_all | solution.py:333
  65.6 3.4 %shard_map.94 = (bf16[512,1280]{1,0:T(8,128)(2,1)S(1)}, f32[10,512,128]{2,1,0:T(8,128)S(1)}, bf16[160,5120]{1,0:T(8,128)(2,1)S(1)}) custom-call(bf16[8,160,512]{2,1,0:T(8,128)(2,1)S(1)} %all-to-all-done.1.gathered, bf16[1280,640]{1,0:T(8,128)(2,1)S(1)} %bitcast.19, f32[10,512,128]{2,1,0:T(8,128)} %get-tuple-element.21.resid_hbm, bf16[160,5120]{1,0:T(8,128)(2,1)} %merge_hbm.1), custom_call_target="tpu_custom_call" | custom-call | flops 838860800 | bytes 8388608 | tf_op jit(solution)/shard_map/pallas_call | solution.py:338
  69.0 0.0 collective-permute-done.1.weight_hbm
  69.0 0.0 copy-start.2
  69.0 5.5 %shard_map.95 = bf16[8,160,128]{2,1,0:T(8,128)(2,1)} custom-call(bf16[512,1280]{1,0:T(8,128)(2,1)S(1)} %get-tuple-element.22.attended, bf16[1280,640]{1,0:T(8,128)(2,1)} %collective-permute-done.1.weight_hbm, f32[10,512,128]{2,1,0:T(8,128)S(1)} %get-tuple-element.23.partial, bf16[160,5120]{1,0:T(8,128)(2,1)S(1)} %get-tuple-element.24.merge_weight), custom_call_target="tpu_custom_call" | custom-call | tf_op jit(solution)/shard_map/pallas_call | solution.py:356
  74.5 6.8 %all-to-all-start.2 = ((bf16[8,160,128]{2,1,0:T(8,128)(2,1)}), bf16[8,160,128]{2,1,0:T(8,128)(2,1)S(1)}, u32[]{:S(2)}, u32[]{:S(2)}) async-start(bf16[8,160,128]{2,1,0:T(8,128)(2,1)} %shard_map.95), calls=%async_computation.2 | async-start | bytes 655360 | tf_op jit(solution)/shard_map/all_to_all | solution.py:384
  81.3 0.1 reduce_sum.31
  81.4 0.1 fusion.3
  81.5 0.1 reshape.157.wanted
  81.6 0.0 copy-done.2
  81.6 12.6 %all-to-all-done.2.blocks = bf16[8,160,128]{2,1,0:T(8,128)(2,1)S(1)} async-done(((bf16[8,160,128]{2,1,0:T(8,128)(2,1)}), bf16[8,160,128]{2,1,0:T(8,128)(2,1)S(1)}, u32[]{:S(2)}, u32[]{:S(2)}) %all-to-all-start.2) | async-done | bytes 327712 | tf_op jit(solution)/shard_map/all_to_all | solution.py:384
  94.2 1.3 %shard_map.96 = bf16[8,160,128]{2,1,0:T(8,128)(2,1)} custom-call(s32[8]{0:T(128)S(1)} %reshape.157.wanted, bf16[8,160,128]{2,1,0:T(8,128)(2,1)S(1)} %all-to-all-done.2.blocks), custom_call_target="tpu_custom_call" | custom-call | tf_op jit(solution)/shard_map/pallas_call | solution.py:385
  95.6 5.7 %all-to-all-start.3 = ((bf16[8,160,128]{2,1,0:T(8,128)(2,1)}), bf16[8,160,128]{2,1,0:T(8,128)(2,1)S(1)}, u32[]{:S(2)}, u32[]{:S(2)}) async-start(bf16[8,160,128]{2,1,0:T(8,128)(2,1)} %shard_map.96), calls=%async_computation.3 | async-start | bytes 655360 | tf_op jit(solution)/shard_map/all_to_all | solution.py:393
  101.2 0.1 fusion.5.facts
  101.4 7.0 %all-to-all-done.3.blocks = bf16[8,160,128]{2,1,0:T(8,128)(2,1)S(1)} async-done(((bf16[8,160,128]{2,1,0:T(8,128)(2,1)}), bf16[8,160,128]{2,1,0:T(8,128)(2,1)S(1)}, u32[]{:S(2)}, u32[]{:S(2)}) %all-to-all-start.3) | async-done | bytes 327712 | tf_op jit(solution)/shard_map/all_to_all | solution.py:393
  108.3 1.4 %shard_map.97 = bf16[160,248]{1,0:T(8,128)(2,1)} custom-call(s32[3]{0:T(128)S(1)} %fusion.5.facts, bf16[8,160,128]{2,1,0:T(8,128)(2,1)S(1)} %all-to-all-done.3.blocks), custom_call_target="tpu_custom_call" | custom-call | tf_op jit(solution)/shard_map/pallas_call | solution.py:394
  (5 shorter events, 0.1 us)
Async XLA Ops:
  0.0 12.6 %copy-start = (bf16[512,1280]{1,0:T(8,128)(2,1)S(1)}, bf16[512,1280]{1,0:T(8,128)(2,1)}, u32[]{:S(2)}) copy-start(bf16[512,1280]{1,0:T(8,128)(2,1)} %patches.1) | copy-start | bytes 3932164
  1.7 25.6 %all-to-all-start = ((bf16[8,40,640]{2,1,0:T(8,128)(2,1)}), bf16[8,40,640]{2,1,0:T(8,128)(2,1)S(1)}, u32[]{:S(2)}, u32[]{:S(2)}) async-start(bf16[8,40,640]{2,1,0:T(8,128)(2,1)} %broadcast_in_dim.50), calls=%async_computation | async-start | bytes 819200 | tf_op jit(solution)/shard_map/all_to_all | solution.py:274
  12.6 6.3 %copy-start.1 = (s32[64]{0:T(128)S(1)}, s32[64]{0:T(128)}, u32[]{:S(2)}) copy-start(s32[64]{0:T(128)} %offsets.3) | copy-start | bytes 772
  16.0 4.6 %collective-permute-start = (bf16[320,512]{1,0:T(8,128)(2,1)S(1)}, bf16[320,512]{1,0:T(8,128)(2,1)S(1)}, u32[]{:S(2)}, u32[]{:S(2)}) collective-permute-start(bf16[320,512]{1,0:T(8,128)(2,1)S(1)} %get-tuple-element.16.near), channel_id=1, source_target_pairs={{0,1},{1,0},{2,3},{3,2},{4,5},{5,4},{6,7},{7,6},{8,9},{9,8},{10,11... | collective-permute-start | bytes 983048 | tf_op jit(solution)/shard_map/ppermute | solution.py:25
  27.3 38.3 %all-to-all-start.1 = ((bf16[8,160,512]{2,1,0:T(8,128)(2,1)}), bf16[8,160,512]{2,1,0:T(8,128)(2,1)S(1)}, u32[]{:S(2)}, u32[]{:S(2)}) async-start(bf16[8,160,512]{2,1,0:T(8,128)(2,1)} %shard_map.93), calls=%async_computation.1 | async-start | bytes 2621440 | tf_op jit(solution)/shard_map/all_to_all | solution.py:333
  55.2 7.0 %copy-start.3 = (s32[64]{0:T(128)S(1)}, s32[64]{0:T(128)}, u32[]{:S(2)}) copy-start(s32[64]{0:T(128)} %param.18) | copy-start | bytes 772
  55.4 13.6 %collective-permute-start.1 = (bf16[1280,640]{1,0:T(8,128)(2,1)S(1)}, bf16[1280,640]{1,0:T(8,128)(2,1)}, u32[]{:S(2)}, u32[]{:S(2)}) collective-permute-start(bf16[1280,640]{1,0:T(8,128)(2,1)S(1)} %bitcast.18), channel_id=1, source_target_pairs={{0,1},{1,0},{2,3},{3,2},{4,5},{5,4},{6,7},{7,6},{8,9},{9,8},{10,11... | collective-permute-start | bytes 4915208 | tf_op jit(solution)/shard_map/ppermute | solution.py:25
  69.0 12.6 %copy-start.2 = (s32[64,2]{0,1:T(2,128)S(1)}, s32[64,2]{0,1:T(2,128)}, u32[]{:S(2)}) copy-start(s32[64,2]{0,1:T(2,128)} %param.16) | copy-start | bytes 1540
  74.5 19.7 %all-to-all-start.2 = ((bf16[8,160,128]{2,1,0:T(8,128)(2,1)}), bf16[8,160,128]{2,1,0:T(8,128)(2,1)S(1)}, u32[]{:S(2)}, u32[]{:S(2)}) async-start(bf16[8,160,128]{2,1,0:T(8,128)(2,1)} %shard_map.95), calls=%async_computation.2 | async-start | bytes 655360 | tf_op jit(solution)/shard_map/all_to_all | solution.py:384
  95.6 12.8 %all-to-all-start.3 = ((bf16[8,160,128]{2,1,0:T(8,128)(2,1)}), bf16[8,160,128]{2,1,0:T(8,128)(2,1)S(1)}, u32[]{:S(2)}, u32[]{:S(2)}) async-start(bf16[8,160,128]{2,1,0:T(8,128)(2,1)} %shard_map.96), calls=%async_computation.3 | async-start | bytes 655360 | tf_op jit(solution)/shard_map/all_to_all | solution.py:393

commit v8 on v7

--- a/solution.py
+++ b/solution.py
@@ -49,17 +49,22 @@
     weight,
     offsets,
     sems,
+    weight_sems,
+    resid_sems,
 ):
     rows = patches.shape[0]
     side = tables.shape[0] // 2
     copies = [
         pltpu.make_async_copy(row_hbm, tables.at[pl.ds(0, side), :], sems.at[0]),
         pltpu.make_async_copy(col_hbm, tables.at[pl.ds(side, side), :], sems.at[1]),
-        pltpu.make_async_copy(weight_hbm, weight, sems.at[2]),
-    ]
-    offsets_copy = pltpu.make_async_copy(offsets_hbm, offsets, sems.at[4])
+    ]
+    weight_copies = [
+        pltpu.make_async_copy(weight_hbm.at[part], weight.at[part], weight_sems.at[part])
+        for part in range(weight.shape[0])
+    ]
+    offsets_copy = pltpu.make_async_copy(offsets_hbm, offsets, sems.at[2])
     offsets_copy.start()
-    for copy in copies:
+    for copy in copies + weight_copies:
         copy.start()
     offsets_copy.wait()
     place = lax.axis_index("tok")
@@ -79,18 +84,23 @@
     copies[1].wait()
     embedded = dot(onehot, tables[...], ((1,), (0,)))
     values = patches[...].astype(jnp.float32) + embedded
+    resid_copies = []
     for tile in range(resid.shape[0]):
         resid[tile] = values[:, tile * LANES : (tile + 1) * LANES]
-    resid_copy = pltpu.make_async_copy(resid, resid_hbm, sems.at[3])
-    resid_copy.start()
+        resid_copies.append(
+            pltpu.make_async_copy(resid.at[tile], resid_hbm.at[tile], resid_sems.at[tile])
+        )
+        resid_copies[-1].start()
     normed = normalize(values).astype(jnp.bfloat16)
-    copies[2].wait()
+    for copy in weight_copies:
+        copy.wait()
     width = weight.shape[1]
     wide = weight[...].reshape(3 * width, weight.shape[2])
     out = dot(wide, normed, ((1,), (1,))).astype(jnp.bfloat16)
     queries[...] = out[:width]
     pairs[...] = out[width:]
-    resid_copy.wait()
+    for copy in resid_copies:
+        copy.wait()
 
 
 def block_scores(offsets, block, query, other):
@@ -148,12 +158,32 @@
 
 
 def project_kernel(
-    gathered, weight, resid_hbm, merge_hbm, attended, partial, merge_weight, resid, sems
+    gathered,
+    weight,
+    resid_hbm,
+    merge_hbm,
+    attended,
+    partial,
+    merge_weight,
+    resid,
+    resid_sems,
+    merge_sems,
 ):
-    resid_copy = pltpu.make_async_copy(resid_hbm, resid, sems.at[0])
-    resid_copy.start()
-    merge_copy = pltpu.make_async_copy(merge_hbm, merge_weight, sems.at[1])
-    merge_copy.start()
+    resid_copies = [
+        pltpu.make_async_copy(resid_hbm.at[tile], resid.at[tile], resid_sems.at[tile])
+        for tile in range(resid.shape[0])
+    ]
+    depth = merge_weight.shape[0] // 4
+    merge_copies = [
+        pltpu.make_async_copy(
+            merge_hbm.at[pl.ds(i * depth, depth), :],
+            merge_weight.at[pl.ds(i * depth, depth), :],
+            merge_sems.at[i],
+        )
+        for i in range(4)
+    ]
+    for copy in resid_copies + merge_copies:
+        copy.start()
     core = lax.axis_index("tok") % 2
     group, depth, rows = gathered.shape
     whole = gathered[...].reshape(group * depth, rows)
@@ -162,13 +192,15 @@
         part = slice(tile * LANES, (tile + 1) * LANES)
         attended[:, part] = whole[part, :].T
     part = dot(attended[...], weight[...], ((1,), (0,)))
-    resid_copy.wait()
+    for copy in resid_copies:
+        copy.wait()
     for tile in range(tiles // 2):
         place = core * (tiles // 2) + tile
         partial[place] = resid[place] + part[:, tile * LANES : (tile + 1) * LANES]
         place = (1 - core) * (tiles // 2) + tile
         partial[place] = resid[place]
-    merge_copy.wait()
+    for copy in merge_copies:
+        copy.wait()
 
 
 def merge_kernel(
@@ -287,7 +319,9 @@
             pltpu.VMEM((2 * row_table.shape[0], width), jnp.bfloat16),
             pltpu.VMEM(qkv_weight.shape, jnp.bfloat16),
             pltpu.SMEM(image_offsets.shape, jnp.int32),
-            pltpu.SemaphoreType.DMA((5,)),
+            pltpu.SemaphoreType.DMA((3,)),
+            pltpu.SemaphoreType.DMA((qkv_weight.shape[0],)),
+            pltpu.SemaphoreType.DMA((width // LANES,)),
         ],
         compiler_params=params,
         cost_estimate=pl.CostEstimate(
@@ -323,11 +357,10 @@
     )(image_offsets, queries, far, mixed, stats)
     pieces, sent = lax.optimization_barrier((pieces, sent))
     own_weight = [
-        lax.all_gather(part, "tok", axis=0, axis_index_groups=rings_x)
+        lax.all_gather(part, "tok", axis=1, axis_index_groups=rings_x, tiled=True)
         for part in jnp.split(pieces, 2)
     ]
-    own_weight = jnp.concatenate([part.transpose(1, 0, 2, 3) for part in own_weight], axis=0)
-    own_weight = own_weight.reshape(group * width_here, columns)
+    own_weight = jnp.concatenate(own_weight, axis=0).reshape(group * width_here, columns)
     other_weight = partner(own_weight, "tok", 0)
 
     gathered = lax.all_to_all(sent, "head", 0, 0, tiled=True)
@@ -346,7 +379,8 @@
         out_specs=(VMEM, VMEM, VMEM),
         scratch_shapes=[
             pltpu.VMEM((tiles, block_rows, LANES), jnp.float32),
-            pltpu.SemaphoreType.DMA((2,)),
+            pltpu.SemaphoreType.DMA((tiles,)),
+            pltpu.SemaphoreType.DMA((4,)),
         ],
         compiler_params=params,
         cost_estimate=pl.CostEstimate(

time: 110 us -> 110 us (level)
  no operation moved by 1% of the time
where the time goes in v8:
time: 110 us
  starting transfers between devices  36.5 us (33%)
  waiting for transfers between devices  26.8 us (24%)
  blocking collectives  24.2 us (22%)
  Pallas kernels  19.5 us (18%)
  local copies, waits for them, and re-layouts  1.96 us (2%)
    all_gather x2, blocking collectives, on_device(): lax.all_gather(part, 'tok', axis=1, axis_index_groups=rings_x, tiled=True)  24.2 us
    all_to_all x1, waiting for transfers between devices, on_device(): lax.all_to_all(projected, 'tok', 0, 0, axis_index_groups=rings_y, tiled=T...  12.6 us
    all_to_all x1, starting transfers between devices, on_device(): pieces = lax.all_to_all(pieces, 'head', 0, 0, tiled=True)  10.9 us
    ppermute x2, starting transfers between devices, partner(): lax.ppermute(x, axis, [(i, i ^ 1 << apart) for i in range(lax.axis_size(a...  9.58 us
    all_to_all x1, waiting for transfers between devices, on_device(): lax.all_to_all(blocks, 'tok', 0, 0, axis_index_groups=planes, tiled=True)  6.98 us
    all_to_all x1, starting transfers between devices, on_device(): lax.all_to_all(projected, 'tok', 0, 0, axis_index_groups=rings_y, tiled=T...  6.84 us
    all_to_all x1, starting transfers between devices, on_device(): lax.all_to_all(blocks, 'tok', 0, 0, axis_index_groups=planes, tiled=True)  5.67 us
    pallas_call x1, Pallas kernels, on_device(): pl.pallas_call(merge_kernel, out_shape=blocks_shape, in_specs=[VMEM, HBM,...  5.47 us
  transfers between devices with their start and end apart: 6, of which 4 were waited for; matrix products, arithmetic and copies ran while one was open for 1% of the time, Pallas kernels for 10%

profile of v8, /device:TPU:1, one launch (start us, length us, event | category | flops | bytes accessed | tf_op | source)
XLA Modules:
  0.0 109.7 jit_solution(6391947650238815829)
XLA Ops:
  0.0 0.0 copy-start
  0.0 0.9 dynamic_slice.3
  0.9 0.8 broadcast_in_dim.50
  1.7 10.9 %all-to-all-start = ((bf16[8,40,640]{2,1,0:T(8,128)(2,1)}), bf16[8,40,640]{2,1,0:T(8,128)(2,1)S(1)}, u32[]{:S(2)}, u32[]{:S(2)}) async-start(bf16[8,40,640]{2,1,0:T(8,128)(2,1)} %broadcast_in_dim.50), calls=%async_computation | async-start | bytes 819200 | tf_op jit(solution)/shard_map/all_to_all | solution.py:306
  12.6 0.0 copy-done
  12.6 0.0 copy-start.1
  12.6 3.5 %shard_map.91 = (f32[10,512,128]{2,1,0:T(8,128)}, bf16[160,512]{1,0:T(8,128)(2,1)S(1)}, bf16[320,512]{1,0:T(8,128)(2,1)S(1)}) custom-call(s32[64]{0:T(128)} %offsets.3, bf16[512,1280]{1,0:T(8,128)(2,1)S(1)} %copy-done, bf16[64,1280]{1,0:T(8,128)(2,1)} %row_hbm.1, bf16[64,1280]{1,0:T(8,128)(2,1)} %col_hbm.1, bf16[3,160,1280]{2,1,0:T(8,128)(2,1)} %weight_hbm.1), custom_call_target="tpu_custom_call" | custom-call | flops 629145600 | bytes 8388608 | tf_op jit(solution)/shard_map/pallas_call | solution.py:308
  16.1 2.9 %collective-permute-start = (bf16[320,512]{1,0:T(8,128)(2,1)S(1)}, bf16[320,512]{1,0:T(8,128)(2,1)S(1)}, u32[]{:S(2)}, u32[]{:S(2)}) collective-permute-start(bf16[320,512]{1,0:T(8,128)(2,1)S(1)} %get-tuple-element.16.near), channel_id=1, source_target_pairs={{0,1},{1,0},{2,3},{3,2},{4,5},{5,4},{6,7},{7,6},{8,9},{9,8},{10,11... | collective-permute-start | bytes 983048 | tf_op jit(solution)/shard_map/ppermute | solution.py:25
  18.9 0.0 copy-done.1
  19.0 1.7 %shard_map.92 = (f32[160,512]{1,0:T(8,128)S(1)}, f32[4,512]{1,0:T(4,128)S(1)}) custom-call(s32[64]{0:T(128)S(1)} %copy-done.1, bf16[160,512]{1,0:T(8,128)(2,1)S(1)} %get-tuple-element.15.queries, bf16[320,512]{1,0:T(8,128)(2,1)S(1)} %get-tuple-element.16.near), custom_call_target="tpu_custom_call" | custom-call | flops 167772160 | bytes 2097152 | tf_op jit(solution)/shard_map/pallas_call | solution.py:332
  20.7 0.0 collective-permute-done.far
  20.7 2.8 %shard_map.93 = bf16[8,160,512]{2,1,0:T(8,128)(2,1)} custom-call(s32[64]{0:T(128)S(1)} %copy-done.1, bf16[160,512]{1,0:T(8,128)(2,1)S(1)} %get-tuple-element.15.queries, bf16[320,512]{1,0:T(8,128)(2,1)S(1)} %collective-permute-done.far, f32[160,512]{1,0:T(8,128)S(1)} %get-tuple-element.17.near_mixed, f32[4,512]{1,0:T(4,128)S(1)} %get-tuple-element.18.stats), custom_call_target="tpu_custom_call" | custom-call | tf_op jit(solution)/shard_map/pallas_call | solution.py:347
  23.5 3.8 %all-to-all-done = bf16[8,40,640]{2,1,0:T(8,128)(2,1)S(1)} async-done(((bf16[8,40,640]{2,1,0:T(8,128)(2,1)}), bf16[8,40,640]{2,1,0:T(8,128)(2,1)S(1)}, u32[]{:S(2)}, u32[]{:S(2)}) %all-to-all-start) | async-done | bytes 409632 | tf_op jit(solution)/shard_map/all_to_all | solution.py:306
  27.3 3.6 %all-to-all-start.1 = ((bf16[8,160,512]{2,1,0:T(8,128)(2,1)}), bf16[8,160,512]{2,1,0:T(8,128)(2,1)S(1)}, u32[]{:S(2)}, u32[]{:S(2)}) async-start(bf16[8,160,512]{2,1,0:T(8,128)(2,1)} %shard_map.93), calls=%async_computation.1 | async-start | bytes 2621440 | tf_op jit(solution)/shard_map/all_to_all | solution.py:366
  30.9 12.8 %all_gather.6 = bf16[4,160,640]{2,1,0:T(8,128)(2,1)S(1)} all-gather(bf16[4,40,640]{2,1,0:T(8,128)(2,1)S(1)} %get-tuple-element.25), channel_id=1, replica_groups={{0,16,32,48},{1,17,33,49},{2,18,34,50},{3,19,35,51},{4,20,36,52},{5,21,..., dimensions={1}, use_global_device_ids=true | all-gather | bytes 1024000 | tf_op jit(solution)/shard_map/all_gather | solution.py:360
  43.7 11.4 %all_gather.7 = bf16[4,160,640]{2,1,0:T(8,128)(2,1)S(1)} all-gather(bf16[4,40,640]{2,1,0:T(8,128)(2,1)S(1)} %get-tuple-element.26), channel_id=1, replica_groups={{0,16,32,48},{1,17,33,49},{2,18,34,50},{3,19,35,51},{4,20,36,52},{5,21,..., dimensions={1}, use_global_device_ids=true | all-gather | bytes 1024000 | tf_op jit(solution)/shard_map/all_gather | solution.py:360
  55.1 0.0 copy-start.3
  55.2 0.2 pad_maximum_fusion
  55.3 6.7 %collective-permute-start.1 = (bf16[1280,640]{1,0:T(8,128)(2,1)S(1)}, bf16[1280,640]{1,0:T(8,128)(2,1)}, u32[]{:S(2)}, u32[]{:S(2)}) collective-permute-start(bf16[1280,640]{1,0:T(8,128)(2,1)S(1)} %bitcast.12), channel_id=1, source_target_pairs={{0,1},{1,0},{2,3},{3,2},{4,5},{5,4},{6,7},{7,6},{8,9},{9,8},{10,11... | collective-permute-start | bytes 4915208 | tf_op jit(solution)/shard_map/ppermute | solution.py:25
  62.1 0.0 copy-done.3
  62.1 0.1 select_reduce_fusion
  62.2 3.4 %all-to-all-done.1.gathered = bf16[8,160,512]{2,1,0:T(8,128)(2,1)S(1)} async-done(((bf16[8,160,512]{2,1,0:T(8,128)(2,1)}), bf16[8,160,512]{2,1,0:T(8,128)(2,1)S(1)}, u32[]{:S(2)}, u32[]{:S(2)}) %all-to-all-start.1) | async-done | bytes 1310752 | tf_op jit(solution)/shard_map/all_to_all | solution.py:366
  65.6 3.4 %shard_map.94 = (bf16[512,1280]{1,0:T(8,128)(2,1)S(1)}, f32[10,512,128]{2,1,0:T(8,128)S(1)}, bf16[160,5120]{1,0:T(8,128)(2,1)S(1)}) custom-call(bf16[8,160,512]{2,1,0:T(8,128)(2,1)S(1)} %all-to-all-done.1.gathered, bf16[1280,640]{1,0:T(8,128)(2,1)S(1)} %bitcast.13, f32[10,512,128]{2,1,0:T(8,128)} %get-tuple-element.21.resid_hbm, bf16[160,5120]{1,0:T(8,128)(2,1)} %merge_hbm.1), custom_call_target="tpu_custom_call" | custom-call | flops 838860800 | bytes 8388608 | tf_op jit(solution)/shard_map/pallas_call | solution.py:371
  69.0 0.0 collective-permute-done.1.weight_hbm
  69.0 0.0 copy-start.2
  69.0 5.5 %shard_map.95 = bf16[8,160,128]{2,1,0:T(8,128)(2,1)} custom-call(bf16[512,1280]{1,0:T(8,128)(2,1)S(1)} %get-tuple-element.22.attended, bf16[1280,640]{1,0:T(8,128)(2,1)} %collective-permute-done.1.weight_hbm, f32[10,512,128]{2,1,0:T(8,128)S(1)} %get-tuple-element.23.partial, bf16[160,5120]{1,0:T(8,128)(2,1)S(1)} %get-tuple-element.24.merge_weight), custom_call_target="tpu_custom_call" | custom-call | tf_op jit(solution)/shard_map/pallas_call | solution.py:390
  74.5 6.8 %all-to-all-start.2 = ((bf16[8,160,128]{2,1,0:T(8,128)(2,1)}), bf16[8,160,128]{2,1,0:T(8,128)(2,1)S(1)}, u32[]{:S(2)}, u32[]{:S(2)}) async-start(bf16[8,160,128]{2,1,0:T(8,128)(2,1)} %shard_map.95), calls=%async_computation.2 | async-start | bytes 655360 | tf_op jit(solution)/shard_map/all_to_all | solution.py:418
  81.3 0.1 reduce_sum.31
  81.4 0.1 fusion.3
  81.5 0.1 reshape.157.wanted
  81.6 0.0 copy-done.2
  81.7 12.6 %all-to-all-done.2.blocks = bf16[8,160,128]{2,1,0:T(8,128)(2,1)S(1)} async-done(((bf16[8,160,128]{2,1,0:T(8,128)(2,1)}), bf16[8,160,128]{2,1,0:T(8,128)(2,1)S(1)}, u32[]{:S(2)}, u32[]{:S(2)}) %all-to-all-start.2) | async-done | bytes 327712 | tf_op jit(solution)/shard_map/all_to_all | solution.py:418
  94.2 1.3 %shard_map.96 = bf16[8,160,128]{2,1,0:T(8,128)(2,1)} custom-call(s32[8]{0:T(128)S(1)} %reshape.157.wanted, bf16[8,160,128]{2,1,0:T(8,128)(2,1)S(1)} %all-to-all-done.2.blocks), custom_call_target="tpu_custom_call" | custom-call | tf_op jit(solution)/shard_map/pallas_call | solution.py:419
  95.6 5.7 %all-to-all-start.3 = ((bf16[8,160,128]{2,1,0:T(8,128)(2,1)}), bf16[8,160,128]{2,1,0:T(8,128)(2,1)S(1)}, u32[]{:S(2)}, u32[]{:S(2)}) async-start(bf16[8,160,128]{2,1,0:T(8,128)(2,1)} %shard_map.96), calls=%async_computation.3 | async-start | bytes 655360 | tf_op jit(solution)/shard_map/all_to_all | solution.py:427
  101.2 0.1 fusion.5.facts
  101.4 7.0 %all-to-all-done.3.blocks = bf16[8,160,128]{2,1,0:T(8,128)(2,1)S(1)} async-done(((bf16[8,160,128]{2,1,0:T(8,128)(2,1)}), bf16[8,160,128]{2,1,0:T(8,128)(2,1)S(1)}, u32[]{:S(2)}, u32[]{:S(2)}) %all-to-all-start.3) | async-done | bytes 327712 | tf_op jit(solution)/shard_map/all_to_all | solution.py:427
  108.3 1.4 %shard_map.97 = bf16[160,248]{1,0:T(8,128)(2,1)} custom-call(s32[3]{0:T(128)S(1)} %fusion.5.facts, bf16[8,160,128]{2,1,0:T(8,128)(2,1)S(1)} %all-to-all-done.3.blocks), custom_call_target="tpu_custom_call" | custom-call | tf_op jit(solution)/shard_map/pallas_call | solution.py:428
  (5 shorter events, 0.1 us)
Async XLA Ops:
  0.0 12.6 %copy-start = (bf16[512,1280]{1,0:T(8,128)(2,1)S(1)}, bf16[512,1280]{1,0:T(8,128)(2,1)}, u32[]{:S(2)}) copy-start(bf16[512,1280]{1,0:T(8,128)(2,1)} %patches.1) | copy-start | bytes 3932164
  1.7 25.6 %all-to-all-start = ((bf16[8,40,640]{2,1,0:T(8,128)(2,1)}), bf16[8,40,640]{2,1,0:T(8,128)(2,1)S(1)}, u32[]{:S(2)}, u32[]{:S(2)}) async-start(bf16[8,40,640]{2,1,0:T(8,128)(2,1)} %broadcast_in_dim.50), calls=%async_computation | async-start | bytes 819200 | tf_op jit(solution)/shard_map/all_to_all | solution.py:306
  12.6 6.3 %copy-start.1 = (s32[64]{0:T(128)S(1)}, s32[64]{0:T(128)}, u32[]{:S(2)}) copy-start(s32[64]{0:T(128)} %offsets.3) | copy-start | bytes 772
  16.1 4.6 %collective-permute-start = (bf16[320,512]{1,0:T(8,128)(2,1)S(1)}, bf16[320,512]{1,0:T(8,128)(2,1)S(1)}, u32[]{:S(2)}, u32[]{:S(2)}) collective-permute-start(bf16[320,512]{1,0:T(8,128)(2,1)S(1)} %get-tuple-element.16.near), channel_id=1, source_target_pairs={{0,1},{1,0},{2,3},{3,2},{4,5},{5,4},{6,7},{7,6},{8,9},{9,8},{10,11... | collective-permute-start | bytes 983048 | tf_op jit(solution)/shard_map/ppermute | solution.py:25
  27.3 38.3 %all-to-all-start.1 = ((bf16[8,160,512]{2,1,0:T(8,128)(2,1)}), bf16[8,160,512]{2,1,0:T(8,128)(2,1)S(1)}, u32[]{:S(2)}, u32[]{:S(2)}) async-start(bf16[8,160,512]{2,1,0:T(8,128)(2,1)} %shard_map.93), calls=%async_computation.1 | async-start | bytes 2621440 | tf_op jit(solution)/shard_map/all_to_all | solution.py:366
  55.1 6.9 %copy-start.3 = (s32[64]{0:T(128)S(1)}, s32[64]{0:T(128)}, u32[]{:S(2)}) copy-start(s32[64]{0:T(128)} %param.18) | copy-start | bytes 772
  55.3 13.7 %collective-permute-start.1 = (bf16[1280,640]{1,0:T(8,128)(2,1)S(1)}, bf16[1280,640]{1,0:T(8,128)(2,1)}, u32[]{:S(2)}, u32[]{:S(2)}) collective-permute-start(bf16[1280,640]{1,0:T(8,128)(2,1)S(1)} %bitcast.12), channel_id=1, source_target_pairs={{0,1},{1,0},{2,3},{3,2},{4,5},{5,4},{6,7},{7,6},{8,9},{9,8},{10,11... | collective-permute-start | bytes 4915208 | tf_op jit(solution)/shard_map/ppermute | solution.py:25
  69.0 12.6 %copy-start.2 = (s32[64,2]{0,1:T(2,128)S(1)}, s32[64,2]{0,1:T(2,128)}, u32[]{:S(2)}) copy-start(s32[64,2]{0,1:T(2,128)} %param.16) | copy-start | bytes 1540
  74.5 19.7 %all-to-all-start.2 = ((bf16[8,160,128]{2,1,0:T(8,128)(2,1)}), bf16[8,160,128]{2,1,0:T(8,128)(2,1)S(1)}, u32[]{:S(2)}, u32[]{:S(2)}) async-start(bf16[8,160,128]{2,1,0:T(8,128)(2,1)} %shard_map.95), calls=%async_computation.2 | async-start | bytes 655360 | tf_op jit(solution)/shard_map/all_to_all | solution.py:418
  95.6 12.8 %all-to-all-start.3 = ((bf16[8,160,128]{2,1,0:T(8,128)(2,1)}), bf16[8,160,128]{2,1,0:T(8,128)(2,1)S(1)}, u32[]{:S(2)}, u32[]{:S(2)}) async-start(bf16[8,160,128]{2,1,0:T(8,128)(2,1)} %shard_map.96), calls=%async_computation.3 | async-start | bytes 655360 | tf_op jit(solution)/shard_map/all_to_all | solution.py:427

commit v9 on v8

--- a/solution.py
+++ b/solution.py
@@ -35,54 +35,71 @@
     return lax.dot_general(left, right, (dims, ((), ())), preferred_element_type=jnp.float32)
 
 
-def front_kernel(
-    offsets_hbm,
-    patches,
+def load_kernel(
+    out_weight,
     row_hbm,
     col_hbm,
-    weight_hbm,
-    resid_hbm,
-    queries,
-    pairs,
-    resid,
+    qkv_hbm,
+    offsets_hbm,
+    pieces,
     tables,
-    weight,
+    qkv_weight,
+    onehot,
+    piece,
     offsets,
     sems,
-    weight_sems,
-    resid_sems,
+    piece_sems,
 ):
-    rows = patches.shape[0]
-    side = tables.shape[0] // 2
+    depth, columns = piece.shape
+    side = row_hbm.shape[0]
+    place = lax.axis_index("tok")
+    row = pl.multiple_of(place // (2 * RING) * depth, 8)
+    column = pl.multiple_of(place % 2 * columns, LANES)
+    first = pltpu.make_async_copy(
+        out_weight.at[pl.ds(row, depth), pl.ds(column, columns)], piece, sems.at[0]
+    )
+    first.start()
+    offsets_copy = pltpu.make_async_copy(offsets_hbm, offsets, piece_sems.at[pieces.shape[0]])
+    offsets_copy.start()
+    loads = [
+        pltpu.make_async_copy(row_hbm, tables.at[pl.ds(0, side), :], sems.at[1]),
+        pltpu.make_async_copy(col_hbm, tables.at[pl.ds(side, side), :], sems.at[2]),
+    ]
+    for part in range(qkv_hbm.shape[0]):
+        loads.append(
+            pltpu.make_async_copy(qkv_hbm.at[part], qkv_weight.at[part], sems.at[3 + part])
+        )
+    for load in loads:
+        load.start()
+    first.wait()
     copies = [
-        pltpu.make_async_copy(row_hbm, tables.at[pl.ds(0, side), :], sems.at[0]),
-        pltpu.make_async_copy(col_hbm, tables.at[pl.ds(side, side), :], sems.at[1]),
-    ]
-    weight_copies = [
-        pltpu.make_async_copy(weight_hbm.at[part], weight.at[part], weight_sems.at[part])
-        for part in range(weight.shape[0])
-    ]
-    offsets_copy = pltpu.make_async_copy(offsets_hbm, offsets, sems.at[2])
-    offsets_copy.start()
-    for copy in copies + weight_copies:
+        pltpu.make_async_copy(piece, pieces.at[copy], piece_sems.at[copy])
+        for copy in range(pieces.shape[0])
+    ]
+    for copy in copies:
         copy.start()
     offsets_copy.wait()
-    place = lax.axis_index("tok")
-    first = place // 2 * 2
-    position = place * rows + lax.broadcasted_iota(jnp.int32, (rows, 2 * side), 0)
-    start = jnp.where(position >= offsets[first + 1], offsets[first + 1], offsets[first])
+    rows = onehot.shape[0]
+    pair = place // 2 * 2
+    position = place * rows + lax.broadcasted_iota(jnp.int32, onehot.shape, 0)
+    start = jnp.where(position >= offsets[pair + 1], offsets[pair + 1], offsets[pair])
     local = position - start
     window = local >> 2
     quarter = local & 3
     half = WIDTH // 2
-    row = 2 * (window // half) + (quarter >> 1)
-    col = 2 * (window % half) + (quarter & 1)
-    lane = lax.broadcasted_iota(jnp.int32, (rows, 2 * side), 1)
-    onehot = lane == jnp.where(lane < side, row, col + side)
-    onehot = jnp.where(onehot, 1.0, 0.0).astype(jnp.bfloat16)
-    copies[0].wait()
-    copies[1].wait()
-    embedded = dot(onehot, tables[...], ((1,), (0,)))
+    token_row = 2 * (window // half) + (quarter >> 1)
+    token_col = 2 * (window % half) + (quarter & 1)
+    lane = lax.broadcasted_iota(jnp.int32, onehot.shape, 1)
+    chosen = lane == jnp.where(lane < side, token_row, token_col + side)
+    onehot[...] = jnp.where(chosen, 1.0, 0.0).astype(jnp.bfloat16)
+    for copy in copies + loads:
+        copy.wait()
+
+
+def front_kernel(
+    onehot, patches, tables, weight, resid_hbm, queries, pairs, resid, resid_sems
+):
+    embedded = dot(onehot[...], tables[...], ((1,), (0,)))
     values = patches[...].astype(jnp.float32) + embedded
     resid_copies = []
     for tile in range(resid.shape[0]):
@@ -92,8 +109,6 @@
         )
         resid_copies[-1].start()
     normed = normalize(values).astype(jnp.bfloat16)
-    for copy in weight_copies:
-        copy.wait()
     width = weight.shape[1]
     wide = weight[...].reshape(3 * width, weight.shape[2])
     out = dot(wide, normed, ((1,), (1,))).astype(jnp.bfloat16)
@@ -301,8 +316,25 @@
     core = place % 2
 
     depth, columns = width_here // sides, width // 2
-    piece = lax.dynamic_slice(out_weight, (my_x * depth, core * columns), (depth, columns))
-    pieces = jnp.broadcast_to(piece[None], (group, depth, columns))
+    tables_shape = (2 * row_table.shape[0], width)
+    pieces, tables, qkv_here, onehot = pl.pallas_call(
+        load_kernel,
+        out_shape=(
+            pltpu.HBM((group, depth, columns), jnp.bfloat16),
+            jax.ShapeDtypeStruct(tables_shape, jnp.bfloat16),
+            jax.ShapeDtypeStruct(qkv_weight.shape, jnp.bfloat16),
+            jax.ShapeDtypeStruct((block_rows, 2 * row_table.shape[0]), jnp.bfloat16),
+        ),
+        in_specs=[HBM] * 5,
+        out_specs=(HBM, VMEM, VMEM, VMEM),
+        scratch_shapes=[
+            pltpu.VMEM((depth, columns), jnp.bfloat16),
+            pltpu.SMEM(image_offsets.shape, jnp.int32),
+            pltpu.SemaphoreType.DMA((3 + qkv_weight.shape[0],)),
+            pltpu.SemaphoreType.DMA((group + 1,)),
+        ],
+        compiler_params=params,
+    )(*map(at_hbm, (out_weight, row_table, col_table, qkv_weight, image_offsets)))
     pieces = lax.all_to_all(pieces, "head", 0, 0, tiled=True)
 
     resid, queries, near = pl.pallas_call(
@@ -312,22 +344,17 @@
             jax.ShapeDtypeStruct((width_here, block_rows), jnp.bfloat16),
             jax.ShapeDtypeStruct((2 * width_here, block_rows), jnp.bfloat16),
         ),
-        in_specs=[HBM, VMEM, HBM, HBM, HBM],
+        in_specs=[VMEM, VMEM, VMEM, VMEM],
         out_specs=(HBM, VMEM, VMEM),
         scratch_shapes=[
             pltpu.VMEM((width // LANES, block_rows, LANES), jnp.float32),
-            pltpu.VMEM((2 * row_table.shape[0], width), jnp.bfloat16),
-            pltpu.VMEM(qkv_weight.shape, jnp.bfloat16),
-            pltpu.SMEM(image_offsets.shape, jnp.int32),
-            pltpu.SemaphoreType.DMA((3,)),
-            pltpu.SemaphoreType.DMA((qkv_weight.shape[0],)),
             pltpu.SemaphoreType.DMA((width // LANES,)),
         ],
         compiler_params=params,
         cost_estimate=pl.CostEstimate(
             flops=3 * 2 * block_rows * width * width_here, bytes_accessed=8 * 2**20, transcendentals=0
         ),
-    )(at_hbm(image_offsets), patches, *map(at_hbm, (row_table, col_table, qkv_weight)))
+    )(onehot, patches, tables, qkv_here)
     far = partner(near, "tok", 0)
     mixed, stats = pl.pallas_call(
         near_kernel,

time: 110 us -> 110 us (level)
  local copies, waits for them, and re-layouts: 1.96 us -> 0.23 us
  waiting for transfers between devices: 26.8 us -> 28.1 us
    pallas_call x0 -> x1, Pallas kernels: none -> 1.82 us  [on_device(): pl.pallas_call(load_kernel, out_shape=(pltpu.HBM((group, depth, columns),...]
    pallas_call x1, Pallas kernels: 3.46 us -> 2.08 us  [on_device(): pl.pallas_call(front_kernel, out_shape=(pltpu.HBM((width // LANES, block_...]
    all_to_all x1, waiting for transfers between devices: 3.82 us -> 5.14 us  [on_device(): pieces = lax.all_to_all(pieces, 'head', 0, 0, tiled=True)]
  transfers between devices with their start and end apart: 6 -> 6, of which waited for: 4 -> 4; matrix products, arithmetic and copies ran while one was open for 1% -> 1% of each run, Pallas kernels for 10% -> 9%
where the time goes in v9:
time: 110 us
  starting transfers between devices  36.6 us (33%)
  waiting for transfers between devices  28.1 us (26%)
  blocking collectives  24.2 us (22%)
  Pallas kernels  20 us (18%)
    all_gather x2, blocking collectives, on_device(): lax.all_gather(part, 'tok', axis=1, axis_index_groups=rings_x, tiled=True)  24.2 us
    all_to_all x1, waiting for transfers between devices, on_device(): lax.all_to_all(projected, 'tok', 0, 0, axis_index_groups=rings_y, tiled=T...  12.6 us
    all_to_all x1, starting transfers between devices, on_device(): pieces = lax.all_to_all(pieces, 'head', 0, 0, tiled=True)  10.9 us
    ppermute x2, starting transfers between devices, partner(): lax.ppermute(x, axis, [(i, i ^ 1 << apart) for i in range(lax.axis_size(a...  9.59 us
    all_to_all x1, waiting for transfers between devices, on_device(): lax.all_to_all(blocks, 'tok', 0, 0, axis_index_groups=planes, tiled=True)  6.98 us
    all_to_all x1, starting transfers between devices, on_device(): lax.all_to_all(projected, 'tok', 0, 0, axis_index_groups=rings_y, tiled=T...  6.83 us
    all_to_all x1, starting transfers between devices, on_device(): lax.all_to_all(blocks, 'tok', 0, 0, axis_index_groups=planes, tiled=True)  5.67 us
    pallas_call x1, Pallas kernels, on_device(): pl.pallas_call(merge_kernel, out_shape=blocks_shape, in_specs=[VMEM, HBM,...  5.51 us
  transfers between devices with their start and end apart: 6, of which 4 were waited for; matrix products, arithmetic and copies ran while one was open for 1% of the time, Pallas kernels for 9%

profile of v9, /device:TPU:1, one launch (start us, length us, event | category | flops | bytes accessed | tf_op | source)
XLA Modules:
  0.0 109.9 jit_solution(13199162677527749035)
XLA Ops:
  0.0 0.0 copy-start
  0.0 1.8 %shard_map.91 = (bf16[8,40,640]{2,1,0:T(8,128)(2,1)}, bf16[128,1280]{1,0:T(8,128)(2,1)S(1)}, bf16[3,160,1280]{2,1,0:T(8,128)(2,1)S(1)}, bf16[512,128]{1,0:T(8,128)(2,1)S(1)}) custom-call(bf16[160,1280]{1,0:T(8,128)(2,1)} %out_weight.1, bf16[64,1280]{1,0:T(8,128)(2,1)} %row_hbm.1, bf16[64,1280]{1,0:T(8,128)(2,1)} %col_hbm.1, bf16[3,160,1280]{2,1,0:T(8,128)(2,1)} %qkv_hbm.1, ...), custom_call_target="tpu_custom_call" | custom-call | tf_op jit(solution)/shard_map/pallas_call | solution.py:320
  1.8 10.9 %all-to-all-start = ((bf16[8,40,640]{2,1,0:T(8,128)(2,1)}), bf16[8,40,640]{2,1,0:T(8,128)(2,1)S(1)}, u32[]{:S(2)}, u32[]{:S(2)}) async-start(bf16[8,40,640]{2,1,0:T(8,128)(2,1)} %get-tuple-element.19), calls=%async_computation | async-start | bytes 819200 | tf_op jit(solution)/shard_map/all_to_all | solution.py:338
  12.7 0.0 copy-start.1
  12.7 0.0 copy-done
  12.7 2.1 %shard_map.92 = (f32[10,512,128]{2,1,0:T(8,128)}, bf16[160,512]{1,0:T(8,128)(2,1)S(1)}, bf16[320,512]{1,0:T(8,128)(2,1)S(1)}) custom-call(bf16[512,128]{1,0:T(8,128)(2,1)S(1)} %get-tuple-element.20.onehot, bf16[512,1280]{1,0:T(8,128)(2,1)S(1)} %copy-done, bf16[128,1280]{1,0:T(8,128)(2,1)S(1)} %get-tuple-element.21.tables, ...), custom_call_target="tpu_custom_call" | custom-call | flops 629145600 | bytes 8388608 | tf_op jit(solution)/shard_map/pallas_call | solution.py:340
  14.8 2.9 %collective-permute-start = (bf16[320,512]{1,0:T(8,128)(2,1)S(1)}, bf16[320,512]{1,0:T(8,128)(2,1)S(1)}, u32[]{:S(2)}, u32[]{:S(2)}) collective-permute-start(bf16[320,512]{1,0:T(8,128)(2,1)S(1)} %get-tuple-element.24.near), channel_id=1, source_target_pairs={{0,1},{1,0},{2,3},{3,2},{4,5},{5,4},{6,7},{7,6},{8,9},{9,8},{10,11... | collective-permute-start | bytes 983048 | tf_op jit(solution)/shard_map/ppermute | solution.py:25
  17.7 0.0 copy-done.1
  17.7 1.7 %shard_map.93 = (f32[160,512]{1,0:T(8,128)S(1)}, f32[4,512]{1,0:T(4,128)S(1)}) custom-call(s32[64]{0:T(128)S(1)} %copy-done.1, bf16[160,512]{1,0:T(8,128)(2,1)S(1)} %get-tuple-element.23.queries, bf16[320,512]{1,0:T(8,128)(2,1)S(1)} %get-tuple-element.24.near), custom_call_target="tpu_custom_call" | custom-call | flops 167772160 | bytes 2097152 | tf_op jit(solution)/shard_map/pallas_call | solution.py:359
  19.4 0.0 collective-permute-done.far
  19.5 2.8 %shard_map.94 = bf16[8,160,512]{2,1,0:T(8,128)(2,1)} custom-call(s32[64]{0:T(128)S(1)} %copy-done.1, bf16[160,512]{1,0:T(8,128)(2,1)S(1)} %get-tuple-element.23.queries, bf16[320,512]{1,0:T(8,128)(2,1)S(1)} %collective-permute-done.far, f32[160,512]{1,0:T(8,128)S(1)} %get-tuple-element.25.near_mixed, f32[4,512]{1,0:T(4,128)S(1)} %get-tuple-element.26.stats), custom_call_target="tpu_custom_call" | custom-call | tf_op jit(solution)/shard_map/pallas_call | solution.py:374
  22.3 5.1 %all-to-all-done = bf16[8,40,640]{2,1,0:T(8,128)(2,1)S(1)} async-done(((bf16[8,40,640]{2,1,0:T(8,128)(2,1)}), bf16[8,40,640]{2,1,0:T(8,128)(2,1)S(1)}, u32[]{:S(2)}, u32[]{:S(2)}) %all-to-all-start) | async-done | bytes 409632 | tf_op jit(solution)/shard_map/all_to_all | solution.py:338
  27.5 3.6 %all-to-all-start.1 = ((bf16[8,160,512]{2,1,0:T(8,128)(2,1)}), bf16[8,160,512]{2,1,0:T(8,128)(2,1)S(1)}, u32[]{:S(2)}, u32[]{:S(2)}) async-start(bf16[8,160,512]{2,1,0:T(8,128)(2,1)} %shard_map.94), calls=%async_computation.1 | async-start | bytes 2621440 | tf_op jit(solution)/shard_map/all_to_all | solution.py:393
  31.1 12.8 %all_gather.6 = bf16[4,160,640]{2,1,0:T(8,128)(2,1)S(1)} all-gather(bf16[4,40,640]{2,1,0:T(8,128)(2,1)S(1)} %get-tuple-element.33), channel_id=1, replica_groups={{0,16,32,48},{1,17,33,49},{2,18,34,50},{3,19,35,51},{4,20,36,52},{5,21,..., dimensions={1}, use_global_device_ids=true | all-gather | bytes 1024000 | tf_op jit(solution)/shard_map/all_gather | solution.py:387
  43.9 11.4 %all_gather.7 = bf16[4,160,640]{2,1,0:T(8,128)(2,1)S(1)} all-gather(bf16[4,40,640]{2,1,0:T(8,128)(2,1)S(1)} %get-tuple-element.34), channel_id=1, replica_groups={{0,16,32,48},{1,17,33,49},{2,18,34,50},{3,19,35,51},{4,20,36,52},{5,21,..., dimensions={1}, use_global_device_ids=true | all-gather | bytes 1024000 | tf_op jit(solution)/shard_map/all_gather | solution.py:387
  55.3 0.0 copy-start.3
  55.3 0.2 pad_maximum_fusion
  55.5 6.7 %collective-permute-start.1 = (bf16[1280,640]{1,0:T(8,128)(2,1)S(1)}, bf16[1280,640]{1,0:T(8,128)(2,1)}, u32[]{:S(2)}, u32[]{:S(2)}) collective-permute-start(bf16[1280,640]{1,0:T(8,128)(2,1)S(1)} %bitcast.12), channel_id=1, source_target_pairs={{0,1},{1,0},{2,3},{3,2},{4,5},{5,4},{6,7},{7,6},{8,9},{9,8},{10,11... | collective-permute-start | bytes 4915208 | tf_op jit(solution)/shard_map/ppermute | solution.py:25
  62.2 0.0 copy-done.3
  62.2 0.1 select_reduce_fusion
  62.3 3.5 %all-to-all-done.1.gathered = bf16[8,160,512]{2,1,0:T(8,128)(2,1)S(1)} async-done(((bf16[8,160,512]{2,1,0:T(8,128)(2,1)}), bf16[8,160,512]{2,1,0:T(8,128)(2,1)S(1)}, u32[]{:S(2)}, u32[]{:S(2)}) %all-to-all-start.1) | async-done | bytes 1310752 | tf_op jit(solution)/shard_map/all_to_all | solution.py:393
  65.8 3.4 %shard_map.95 = (bf16[512,1280]{1,0:T(8,128)(2,1)S(1)}, f32[10,512,128]{2,1,0:T(8,128)S(1)}, bf16[160,5120]{1,0:T(8,128)(2,1)S(1)}) custom-call(bf16[8,160,512]{2,1,0:T(8,128)(2,1)S(1)} %all-to-all-done.1.gathered, bf16[1280,640]{1,0:T(8,128)(2,1)S(1)} %bitcast.13, f32[10,512,128]{2,1,0:T(8,128)} %get-tuple-element.29.resid_hbm, bf16[160,5120]{1,0:T(8,128)(2,1)} %merge_hbm.1), custom_call_target="tpu_custom_call" | custom-call | flops 838860800 | bytes 8388608 | tf_op jit(solution)/shard_map/pallas_call | solution.py:398
  69.1 0.0 collective-permute-done.1.weight_hbm
  69.2 0.0 copy-start.2
  69.2 5.5 %shard_map.96 = bf16[8,160,128]{2,1,0:T(8,128)(2,1)} custom-call(bf16[512,1280]{1,0:T(8,128)(2,1)S(1)} %get-tuple-element.30.attended, bf16[1280,640]{1,0:T(8,128)(2,1)} %collective-permute-done.1.weight_hbm, f32[10,512,128]{2,1,0:T(8,128)S(1)} %get-tuple-element.31.partial, bf16[160,5120]{1,0:T(8,128)(2,1)S(1)} %get-tuple-element.32.merge_weight), custom_call_target="tpu_custom_call" | custom-call | tf_op jit(solution)/shard_map/pallas_call | solution.py:417
  74.7 6.8 %all-to-all-start.2 = ((bf16[8,160,128]{2,1,0:T(8,128)(2,1)}), bf16[8,160,128]{2,1,0:T(8,128)(2,1)S(1)}, u32[]{:S(2)}, u32[]{:S(2)}) async-start(bf16[8,160,128]{2,1,0:T(8,128)(2,1)} %shard_map.96), calls=%async_computation.2 | async-start | bytes 655360 | tf_op jit(solution)/shard_map/all_to_all | solution.py:445
  81.5 0.1 reduce_sum.31
  81.6 0.1 fusion.3
  81.7 0.1 reshape.156.wanted
  81.8 0.0 copy-done.2
  81.8 12.6 %all-to-all-done.2.blocks = bf16[8,160,128]{2,1,0:T(8,128)(2,1)S(1)} async-done(((bf16[8,160,128]{2,1,0:T(8,128)(2,1)}), bf16[8,160,128]{2,1,0:T(8,128)(2,1)S(1)}, u32[]{:S(2)}, u32[]{:S(2)}) %all-to-all-start.2) | async-done | bytes 327712 | tf_op jit(solution)/shard_map/all_to_all | solution.py:445
  94.4 1.3 %shard_map.97 = bf16[8,160,128]{2,1,0:T(8,128)(2,1)} custom-call(s32[8]{0:T(128)S(1)} %reshape.156.wanted, bf16[8,160,128]{2,1,0:T(8,128)(2,1)S(1)} %all-to-all-done.2.blocks), custom_call_target="tpu_custom_call" | custom-call | tf_op jit(solution)/shard_map/pallas_call | solution.py:446
  95.7 5.7 %all-to-all-start.3 = ((bf16[8,160,128]{2,1,0:T(8,128)(2,1)}), bf16[8,160,128]{2,1,0:T(8,128)(2,1)S(1)}, u32[]{:S(2)}, u32[]{:S(2)}) async-start(bf16[8,160,128]{2,1,0:T(8,128)(2,1)} %shard_map.97), calls=%async_computation.3 | async-start | bytes 655360 | tf_op jit(solution)/shard_map/all_to_all | solution.py:454
  101.4 0.1 fusion.5.facts
  101.5 7.0 %all-to-all-done.3.blocks = bf16[8,160,128]{2,1,0:T(8,128)(2,1)S(1)} async-done(((bf16[8,160,128]{2,1,0:T(8,128)(2,1)}), bf16[8,160,128]{2,1,0:T(8,128)(2,1)S(1)}, u32[]{:S(2)}, u32[]{:S(2)}) %all-to-all-start.3) | async-done | bytes 327712 | tf_op jit(solution)/shard_map/all_to_all | solution.py:454
  108.5 1.4 %shard_map.98 = bf16[160,248]{1,0:T(8,128)(2,1)} custom-call(s32[3]{0:T(128)S(1)} %fusion.5.facts, bf16[8,160,128]{2,1,0:T(8,128)(2,1)S(1)} %all-to-all-done.3.blocks), custom_call_target="tpu_custom_call" | custom-call | tf_op jit(solution)/shard_map/pallas_call | solution.py:455
  (5 shorter events, 0.1 us)
Async XLA Ops:
  0.0 12.7 %copy-start = (bf16[512,1280]{1,0:T(8,128)(2,1)S(1)}, bf16[512,1280]{1,0:T(8,128)(2,1)}, u32[]{:S(2)}) copy-start(bf16[512,1280]{1,0:T(8,128)(2,1)} %patches.1) | copy-start | bytes 3932164
  1.8 25.6 %all-to-all-start = ((bf16[8,40,640]{2,1,0:T(8,128)(2,1)}), bf16[8,40,640]{2,1,0:T(8,128)(2,1)S(1)}, u32[]{:S(2)}, u32[]{:S(2)}) async-start(bf16[8,40,640]{2,1,0:T(8,128)(2,1)} %get-tuple-element.19), calls=%async_computation | async-start | bytes 819200 | tf_op jit(solution)/shard_map/all_to_all | solution.py:338
  12.7 5.0 %copy-start.1 = (s32[64]{0:T(128)S(1)}, s32[64]{0:T(128)}, u32[]{:S(2)}) copy-start(s32[64]{0:T(128)} %offsets.3) | copy-start | bytes 772
  14.8 4.6 %collective-permute-start = (bf16[320,512]{1,0:T(8,128)(2,1)S(1)}, bf16[320,512]{1,0:T(8,128)(2,1)S(1)}, u32[]{:S(2)}, u32[]{:S(2)}) collective-permute-start(bf16[320,512]{1,0:T(8,128)(2,1)S(1)} %get-tuple-element.24.near), channel_id=1, source_target_pairs={{0,1},{1,0},{2,3},{3,2},{4,5},{5,4},{6,7},{7,6},{8,9},{9,8},{10,11... | collective-permute-start | bytes 983048 | tf_op jit(solution)/shard_map/ppermute | solution.py:25
  27.5 38.3 %all-to-all-start.1 = ((bf16[8,160,512]{2,1,0:T(8,128)(2,1)}), bf16[8,160,512]{2,1,0:T(8,128)(2,1)S(1)}, u32[]{:S(2)}, u32[]{:S(2)}) async-start(bf16[8,160,512]{2,1,0:T(8,128)(2,1)} %shard_map.94), calls=%async_computation.1 | async-start | bytes 2621440 | tf_op jit(solution)/shard_map/all_to_all | solution.py:393
  55.3 6.9 %copy-start.3 = (s32[64]{0:T(128)S(1)}, s32[64]{0:T(128)}, u32[]{:S(2)}) copy-start(s32[64]{0:T(128)} %param.18) | copy-start | bytes 772
  55.5 13.7 %collective-permute-start.1 = (bf16[1280,640]{1,0:T(8,128)(2,1)S(1)}, bf16[1280,640]{1,0:T(8,128)(2,1)}, u32[]{:S(2)}, u32[]{:S(2)}) collective-permute-start(bf16[1280,640]{1,0:T(8,128)(2,1)S(1)} %bitcast.12), channel_id=1, source_target_pairs={{0,1},{1,0},{2,3},{3,2},{4,5},{5,4},{6,7},{7,6},{8,9},{9,8},{10,11... | collective-permute-start | bytes 4915208 | tf_op jit(solution)/shard_map/ppermute | solution.py:25
  69.2 12.7 %copy-start.2 = (s32[64,2]{0,1:T(2,128)S(1)}, s32[64,2]{0,1:T(2,128)}, u32[]{:S(2)}) copy-start(s32[64,2]{0,1:T(2,128)} %param.16) | copy-start | bytes 1540
  74.7 19.7 %all-to-all-start.2 = ((bf16[8,160,128]{2,1,0:T(8,128)(2,1)}), bf16[8,160,128]{2,1,0:T(8,128)(2,1)S(1)}, u32[]{:S(2)}, u32[]{:S(2)}) async-start(bf16[8,160,128]{2,1,0:T(8,128)(2,1)} %shard_map.96), calls=%async_computation.2 | async-start | bytes 655360 | tf_op jit(solution)/shard_map/all_to_all | solution.py:445
  95.7 12.8 %all-to-all-start.3 = ((bf16[8,160,128]{2,1,0:T(8,128)(2,1)}), bf16[8,160,128]{2,1,0:T(8,128)(2,1)S(1)}, u32[]{:S(2)}, u32[]{:S(2)}) async-start(bf16[8,160,128]{2,1,0:T(8,128)(2,1)} %shard_map.97), calls=%async_computation.3 | async-start | bytes 655360 | tf_op jit(solution)/shard_map/all_to_all | solution.py:454

commit v10 on v9

--- a/solution.py
+++ b/solution.py
@@ -172,77 +172,67 @@
         copy.wait()
 
 
-def project_kernel(
-    gathered,
-    weight,
-    resid_hbm,
-    merge_hbm,
-    attended,
-    partial,
-    merge_weight,
-    resid,
-    resid_sems,
-    merge_sems,
+def turn_kernel(
+    gathered, resid_hbm, merge_hbm, attended, resid, merge_weight, resid_sems, merge_sems
 ):
-    resid_copies = [
+    tiles = resid.shape[0]
+    loads = [
         pltpu.make_async_copy(resid_hbm.at[tile], resid.at[tile], resid_sems.at[tile])
-        for tile in range(resid.shape[0])
+        for tile in range(tiles)
     ]
     depth = merge_weight.shape[0] // 4
-    merge_copies = [
-        pltpu.make_async_copy(
-            merge_hbm.at[pl.ds(i * depth, depth), :],
-            merge_weight.at[pl.ds(i * depth, depth), :],
-            merge_sems.at[i],
+    for i in range(4):
+        part = pl.ds(i * depth, depth)
+        loads.append(
+            pltpu.make_async_copy(merge_hbm.at[part, :], merge_weight.at[part, :], merge_sems.at[i])
         )
-        for i in range(4)
-    ]
-    for copy in resid_copies + merge_copies:
-        copy.start()
-    core = lax.axis_index("tok") % 2
-    group, depth, rows = gathered.shape
-    whole = gathered[...].reshape(group * depth, rows)
-    tiles = resid.shape[0]
+    for load in loads:
+        load.start()
+    whole = gathered[...].reshape(gathered.shape[0] * gathered.shape[1], gathered.shape[2])
     for tile in range(tiles):
         part = slice(tile * LANES, (tile + 1) * LANES)
         attended[:, part] = whole[part, :].T
-    part = dot(attended[...], weight[...], ((1,), (0,)))
-    for copy in resid_copies:
-        copy.wait()
-    for tile in range(tiles // 2):
-        place = core * (tiles // 2) + tile
-        partial[place] = resid[place] + part[:, tile * LANES : (tile + 1) * LANES]
-        place = (1 - core) * (tiles // 2) + tile
-        partial[place] = resid[place]
-    for copy in merge_copies:
-        copy.wait()
+    for load in loads:
+        load.wait()
 
 
 def merge_kernel(
-    attended, weight_hbm, partial, merge_weight, out, weight, total, block, weight_sems, sems
+    attended,
+    own_weight,
+    other_hbm,
+    resid,
+    merge_weight,
+    out,
+    other_weight,
+    total,
+    block,
+    other_sems,
+    sems,
 ):
-    chunks = [(start, min(256, weight.shape[1] - start)) for start in range(0, weight.shape[1], 256)]
+    columns = own_weight.shape[1]
+    chunks = [(start, min(256, columns - start)) for start in range(0, columns, 256)]
     loads = [
         pltpu.make_async_copy(
-            weight_hbm.at[:, pl.ds(start, size)],
-            weight.at[:, pl.ds(start, size)],
-            weight_sems.at[chunk],
+            other_hbm.at[:, pl.ds(start, size)],
+            other_weight.at[:, pl.ds(start, size)],
+            other_sems.at[chunk],
         )
         for chunk, (start, size) in enumerate(chunks)
     ]
     for load in loads:
         load.start()
     core = lax.axis_index("tok") % 2
-    tiles, rows = partial.shape[:2]
+    tiles, rows = resid.shape[:2]
+    part = dot(attended[...], own_weight[...], ((1,), (0,)))
     for tile in range(tiles // 2):
         place = core * (tiles // 2) + tile
-        total[place] = partial[place]
+        total[place] = resid[place] + part[:, tile * LANES : (tile + 1) * LANES]
     for load, (start, size) in zip(loads, chunks):
         load.wait()
-        part = dot(attended[...], weight[:, start : start + size], ((1,), (0,)))
+        part = dot(attended[...], other_weight[:, start : start + size], ((1,), (0,)))
         for tile in range(size // LANES):
             place = (1 - core) * (tiles // 2) + start // LANES + tile
-            total[place] = partial[place] + part[:, tile * LANES : (tile + 1) * LANES]
+            total[place] = resid[place] + part[:, tile * LANES : (tile + 1) * LANES]
     values = jnp.concatenate([total[tile] for tile in range(tiles)], axis=1)
     normed = normalize(values)
     for tile in range(tiles):
@@ -382,7 +372,7 @@
         ],
         compiler_params=params,
     )(image_offsets, queries, far, mixed, stats)
-    pieces, sent = lax.optimization_barrier((pieces, sent))
+    pieces, _ = lax.optimization_barrier((pieces, sent))
     own_weight = [
         lax.all_gather(part, "tok", axis=1, axis_index_groups=rings_x, tiled=True)
         for part in jnp.split(pieces, 2)
@@ -394,30 +384,28 @@
     rows_here = block_rows // 4
     blocks_shape = pltpu.HBM((RING, width_here, rows_here), jnp.bfloat16)
     tiles = width // LANES
-    half_flops = 2 * block_rows * width * columns
-    attended, partial, merge_here = pl.pallas_call(
-        project_kernel,
+    attended, resid, merge_here = pl.pallas_call(
+        turn_kernel,
         out_shape=(
             jax.ShapeDtypeStruct((block_rows, width), jnp.bfloat16),
             jax.ShapeDtypeStruct((tiles, block_rows, LANES), jnp.float32),
             jax.ShapeDtypeStruct(merge_weight.shape, jnp.bfloat16),
         ),
-        in_specs=[VMEM, VMEM, HBM, HBM],
+        in_specs=[VMEM, HBM, HBM],
         out_specs=(VMEM, VMEM, VMEM),
         scratch_shapes=[
-            pltpu.VMEM((tiles, block_rows, LANES), jnp.float32),
             pltpu.SemaphoreType.DMA((tiles,)),
             pltpu.SemaphoreType.DMA((4,)),
         ],
         compiler_params=params,
         cost_estimate=pl.CostEstimate(
-            flops=half_flops, bytes_accessed=8 * 2**20, transcendentals=0
-        ),
-    )(gathered, own_weight, at_hbm(resid), at_hbm(merge_weight))
+            flops=2 * block_rows * width * columns, bytes_accessed=8 * 2**20, transcendentals=0
+        ),
+    )(gathered, at_hbm(resid), at_hbm(merge_weight))
     projected = pl.pallas_call(
         merge_kernel,
         out_shape=blocks_shape,
-        in_specs=[VMEM, HBM, VMEM, VMEM],
+        in_specs=[VMEM, VMEM, HBM, VMEM, VMEM],
         out_specs=HBM,
         scratch_shapes=[
             pltpu.VMEM(other_weight.shape, jnp.bfloat16),
@@ -427,7 +415,7 @@
             pltpu.SemaphoreType.DMA((RING,)),
         ],
         compiler_params=params,
-    )(attended, at_hbm(other_weight), partial, merge_here)
+    )(attended, own_weight, at_hbm(other_weight), resid, merge_here)
 
     image_ids = jnp.arange(owners.shape[0], dtype=jnp.int32)
     place_ids = jnp.arange(places, dtype=jnp.int32)

time: 110 us -> 111 us (level)
  transfers between devices with their start and end apart: 6 -> 6, of which waited for: 4 -> 4; matrix products, arithmetic and copies ran while one was open for 1% -> 1% of each run, Pallas kernels for 9% -> 8%
where the time goes in v10:
time: 111 us; the launch traced here: 110 us
  starting transfers between devices  36.6 us (33%)
  waiting for transfers between devices  28.1 us (25%)
  blocking collectives  24.2 us (22%)
  Pallas kernels  20.4 us (18%)
    all_gather x2, blocking collectives, on_device(): lax.all_gather(part, 'tok', axis=1, axis_index_groups=rings_x, tiled=True)  24.2 us
    all_to_all x1, waiting for transfers between devices, on_device(): lax.all_to_all(projected, 'tok', 0, 0, axis_index_groups=rings_y, tiled=T...  12.5 us
    all_to_all x1, starting transfers between devices, on_device(): pieces = lax.all_to_all(pieces, 'head', 0, 0, tiled=True)  10.9 us
    ppermute x2, starting transfers between devices, partner(): lax.ppermute(x, axis, [(i, i ^ 1 << apart) for i in range(lax.axis_size(a...  9.59 us
    all_to_all x1, waiting for transfers between devices, on_device(): lax.all_to_all(blocks, 'tok', 0, 0, axis_index_groups=planes, tiled=True)  6.98 us
    pallas_call x1, Pallas kernels, on_device(): pl.pallas_call(merge_kernel, out_shape=blocks_shape, in_specs=[VMEM, VMEM...  6.96 us
    all_to_all x1, starting transfers between devices, on_device(): lax.all_to_all(projected, 'tok', 0, 0, axis_index_groups=rings_y, tiled=T...  6.83 us
    all_to_all x1, starting transfers between devices, on_device(): lax.all_to_all(blocks, 'tok', 0, 0, axis_index_groups=planes, tiled=True)  5.68 us
  transfers between devices with their start and end apart: 6, of which 4 were waited for; matrix products, arithmetic and copies ran while one was open for 1% of the time, Pallas kernels for 8%

profile of v10, /device:TPU:1, one launch (start us, length us, event | category | flops | bytes accessed | tf_op | source)
XLA Modules:
  0.0 110.2 jit_solution(762595245877054750)
XLA Ops:
  0.0 0.0 copy-start
  0.0 1.8 %shard_map.91 = (bf16[8,40,640]{2,1,0:T(8,128)(2,1)}, bf16[128,1280]{1,0:T(8,128)(2,1)S(1)}, bf16[3,160,1280]{2,1,0:T(8,128)(2,1)S(1)}, bf16[512,128]{1,0:T(8,128)(2,1)S(1)}) custom-call(bf16[160,1280]{1,0:T(8,128)(2,1)} %out_weight.1, bf16[64,1280]{1,0:T(8,128)(2,1)} %row_hbm.1, bf16[64,1280]{1,0:T(8,128)(2,1)} %col_hbm.1, bf16[3,160,1280]{2,1,0:T(8,128)(2,1)} %qkv_hbm.1, ...), custom_call_target="tpu_custom_call" | custom-call | tf_op jit(solution)/shard_map/pallas_call | solution.py:310
  1.8 10.9 %all-to-all-start.1 = ((bf16[8,40,640]{2,1,0:T(8,128)(2,1)}), bf16[8,40,640]{2,1,0:T(8,128)(2,1)S(1)}, u32[]{:S(2)}, u32[]{:S(2)}) async-start(bf16[8,40,640]{2,1,0:T(8,128)(2,1)} %get-tuple-element.27), calls=%async_computation.1 | async-start | bytes 819200 | tf_op jit(solution)/shard_map/all_to_all | solution.py:328
  12.7 0.0 copy-start.1
  12.7 0.0 copy-done
  12.7 2.1 %shard_map.92 = (f32[10,512,128]{2,1,0:T(8,128)}, bf16[160,512]{1,0:T(8,128)(2,1)S(1)}, bf16[320,512]{1,0:T(8,128)(2,1)S(1)}) custom-call(bf16[512,128]{1,0:T(8,128)(2,1)S(1)} %get-tuple-element.18.onehot, bf16[512,1280]{1,0:T(8,128)(2,1)S(1)} %copy-done, bf16[128,1280]{1,0:T(8,128)(2,1)S(1)} %get-tuple-element.19.tables, ...), custom_call_target="tpu_custom_call" | custom-call | flops 629145600 | bytes 8388608 | tf_op jit(solution)/shard_map/pallas_call | solution.py:330
  14.8 2.9 %collective-permute-start = (bf16[320,512]{1,0:T(8,128)(2,1)S(1)}, bf16[320,512]{1,0:T(8,128)(2,1)S(1)}, u32[]{:S(2)}, u32[]{:S(2)}) collective-permute-start(bf16[320,512]{1,0:T(8,128)(2,1)S(1)} %get-tuple-element.22.near), channel_id=1, source_target_pairs={{0,1},{1,0},{2,3},{3,2},{4,5},{5,4},{6,7},{7,6},{8,9},{9,8},{10,11... | collective-permute-start | bytes 983048 | tf_op jit(solution)/shard_map/ppermute | solution.py:25
  17.7 0.0 copy-done.1
  17.7 1.7 %shard_map.93 = (f32[160,512]{1,0:T(8,128)S(1)}, f32[4,512]{1,0:T(4,128)S(1)}) custom-call(s32[64]{0:T(128)S(1)} %copy-done.1, bf16[160,512]{1,0:T(8,128)(2,1)S(1)} %get-tuple-element.21.queries, bf16[320,512]{1,0:T(8,128)(2,1)S(1)} %get-tuple-element.22.near), custom_call_target="tpu_custom_call" | custom-call | flops 167772160 | bytes 2097152 | tf_op jit(solution)/shard_map/pallas_call | solution.py:349
  19.4 0.0 collective-permute-done.far
  19.5 2.8 %shard_map.94 = bf16[8,160,512]{2,1,0:T(8,128)(2,1)} custom-call(s32[64]{0:T(128)S(1)} %copy-done.1, bf16[160,512]{1,0:T(8,128)(2,1)S(1)} %get-tuple-element.21.queries, bf16[320,512]{1,0:T(8,128)(2,1)S(1)} %collective-permute-done.far, f32[160,512]{1,0:T(8,128)S(1)} %get-tuple-element.23.near_mixed, f32[4,512]{1,0:T(4,128)S(1)} %get-tuple-element.24.stats), custom_call_target="tpu_custom_call" | custom-call | tf_op jit(solution)/shard_map/pallas_call | solution.py:364
  22.3 5.1 %all-to-all-done.1 = bf16[8,40,640]{2,1,0:T(8,128)(2,1)S(1)} async-done(((bf16[8,40,640]{2,1,0:T(8,128)(2,1)}), bf16[8,40,640]{2,1,0:T(8,128)(2,1)S(1)}, u32[]{:S(2)}, u32[]{:S(2)}) %all-to-all-start.1) | async-done | bytes 409632 | tf_op jit(solution)/shard_map/all_to_all | solution.py:328
  27.4 3.6 %all-to-all-start = ((bf16[8,160,512]{2,1,0:T(8,128)(2,1)}), bf16[8,160,512]{2,1,0:T(8,128)(2,1)S(1)}, u32[]{:S(2)}, u32[]{:S(2)}) async-start(bf16[8,160,512]{2,1,0:T(8,128)(2,1)} %shard_map.94), calls=%async_computation | async-start | bytes 2621440 | tf_op jit(solution)/shard_map/all_to_all | solution.py:383
  31.1 12.8 %all_gather.6 = bf16[4,160,640]{2,1,0:T(8,128)(2,1)S(1)} all-gather(bf16[4,40,640]{2,1,0:T(8,128)(2,1)S(1)} %get-tuple-element.31), channel_id=1, replica_groups={{0,16,32,48},{1,17,33,49},{2,18,34,50},{3,19,35,51},{4,20,36,52},{5,21,..., dimensions={1}, use_global_device_ids=true | all-gather | bytes 1024000 | tf_op jit(solution)/shard_map/all_gather | solution.py:377
  43.9 11.4 %all_gather.7 = bf16[4,160,640]{2,1,0:T(8,128)(2,1)S(1)} all-gather(bf16[4,40,640]{2,1,0:T(8,128)(2,1)S(1)} %get-tuple-element.32), channel_id=1, replica_groups={{0,16,32,48},{1,17,33,49},{2,18,34,50},{3,19,35,51},{4,20,36,52},{5,21,..., dimensions={1}, use_global_device_ids=true | all-gather | bytes 1024000 | tf_op jit(solution)/shard_map/all_gather | solution.py:377
  55.3 0.0 copy-start.3
  55.3 0.2 pad_maximum_fusion
  55.4 6.7 %collective-permute-start.1 = (bf16[1280,640]{1,0:T(8,128)(2,1)S(1)}, bf16[1280,640]{1,0:T(8,128)(2,1)}, u32[]{:S(2)}, u32[]{:S(2)}) collective-permute-start(bf16[1280,640]{1,0:T(8,128)(2,1)S(1)} %bitcast.12), channel_id=1, source_target_pairs={{0,1},{1,0},{2,3},{3,2},{4,5},{5,4},{6,7},{7,6},{8,9},{9,8},{10,11... | collective-permute-start | bytes 4915208 | tf_op jit(solution)/shard_map/ppermute | solution.py:25
  62.2 0.0 copy-done.3
  62.2 0.1 select_reduce_fusion
  62.3 3.4 %all-to-all-done.gathered = bf16[8,160,512]{2,1,0:T(8,128)(2,1)S(1)} async-done(((bf16[8,160,512]{2,1,0:T(8,128)(2,1)}), bf16[8,160,512]{2,1,0:T(8,128)(2,1)S(1)}, u32[]{:S(2)}, u32[]{:S(2)}) %all-to-all-start) | async-done | bytes 1310752 | tf_op jit(solution)/shard_map/all_to_all | solution.py:383
  65.7 2.3 %shard_map.95 = (bf16[512,1280]{1,0:T(8,128)(2,1)S(1)}, f32[10,512,128]{2,1,0:T(8,128)S(1)}, bf16[160,5120]{1,0:T(8,128)(2,1)S(1)}) custom-call(bf16[8,160,512]{2,1,0:T(8,128)(2,1)S(1)} %all-to-all-done.gathered, f32[10,512,128]{2,1,0:T(8,128)} %get-tuple-element.25.resid_hbm, bf16[160,5120]{1,0:T(8,128)(2,1)} %merge_hbm.1), custom_call_target="tpu_custom_call" | custom-call | flops 838860800 | bytes 8388608 | tf_op jit(solution)/shard_map/pallas_call | solution.py:387
  68.0 0.0 collective-permute-done.1.other_hbm
  68.0 0.0 copy-start.2
  68.1 7.0 %shard_map.96 = bf16[8,160,128]{2,1,0:T(8,128)(2,1)} custom-call(bf16[512,1280]{1,0:T(8,128)(2,1)S(1)} %get-tuple-element.26.attended, bf16[1280,640]{1,0:T(8,128)(2,1)S(1)} %bitcast.13, bf16[1280,640]{1,0:T(8,128)(2,1)} %collective-permute-done.1.other_hbm, f32[10,512,128]{2,1,0:T(8,128)S(1)} %get-tuple-element.29.resid, ...), custom_call_target="tpu_custom_call" | custom-call | tf_op jit(solution)/shard_map/pallas_call | solution.py:405
  75.0 6.8 %all-to-all-start.2 = ((bf16[8,160,128]{2,1,0:T(8,128)(2,1)}), bf16[8,160,128]{2,1,0:T(8,128)(2,1)S(1)}, u32[]{:S(2)}, u32[]{:S(2)}) async-start(bf16[8,160,128]{2,1,0:T(8,128)(2,1)} %shard_map.96), calls=%async_computation.2 | async-start | bytes 655360 | tf_op jit(solution)/shard_map/all_to_all | solution.py:433
  81.9 0.1 reduce_sum.31
  82.0 0.1 fusion.3
  82.1 0.1 reshape.156.wanted
  82.2 0.0 copy-done.2
  82.2 12.5 %all-to-all-done.2.blocks = bf16[8,160,128]{2,1,0:T(8,128)(2,1)S(1)} async-done(((bf16[8,160,128]{2,1,0:T(8,128)(2,1)}), bf16[8,160,128]{2,1,0:T(8,128)(2,1)S(1)}, u32[]{:S(2)}, u32[]{:S(2)}) %all-to-all-start.2) | async-done | bytes 327712 | tf_op jit(solution)/shard_map/all_to_all | solution.py:433
  94.7 1.3 %shard_map.97 = bf16[8,160,128]{2,1,0:T(8,128)(2,1)} custom-call(s32[8]{0:T(128)S(1)} %reshape.156.wanted, bf16[8,160,128]{2,1,0:T(8,128)(2,1)S(1)} %all-to-all-done.2.blocks), custom_call_target="tpu_custom_call" | custom-call | tf_op jit(solution)/shard_map/pallas_call | solution.py:434
  96.1 5.7 %all-to-all-start.3 = ((bf16[8,160,128]{2,1,0:T(8,128)(2,1)}), bf16[8,160,128]{2,1,0:T(8,128)(2,1)S(1)}, u32[]{:S(2)}, u32[]{:S(2)}) async-start(bf16[8,160,128]{2,1,0:T(8,128)(2,1)} %shard_map.97), calls=%async_computation.3 | async-start | bytes 655360 | tf_op jit(solution)/shard_map/all_to_all | solution.py:442
  101.8 0.1 fusion.5.facts
  101.9 7.0 %all-to-all-done.3.blocks = bf16[8,160,128]{2,1,0:T(8,128)(2,1)S(1)} async-done(((bf16[8,160,128]{2,1,0:T(8,128)(2,1)}), bf16[8,160,128]{2,1,0:T(8,128)(2,1)S(1)}, u32[]{:S(2)}, u32[]{:S(2)}) %all-to-all-start.3) | async-done | bytes 327712 | tf_op jit(solution)/shard_map/all_to_all | solution.py:442
  108.9 1.4 %shard_map.98 = bf16[160,248]{1,0:T(8,128)(2,1)} custom-call(s32[3]{0:T(128)S(1)} %fusion.5.facts, bf16[8,160,128]{2,1,0:T(8,128)(2,1)S(1)} %all-to-all-done.3.blocks), custom_call_target="tpu_custom_call" | custom-call | tf_op jit(solution)/shard_map/pallas_call | solution.py:443
  (5 shorter events, 0.1 us)
Async XLA Ops:
  0.0 12.7 %copy-start = (bf16[512,1280]{1,0:T(8,128)(2,1)S(1)}, bf16[512,1280]{1,0:T(8,128)(2,1)}, u32[]{:S(2)}) copy-start(bf16[512,1280]{1,0:T(8,128)(2,1)} %patches.1) | copy-start | bytes 3932164
  1.8 25.6 %all-to-all-start.1 = ((bf16[8,40,640]{2,1,0:T(8,128)(2,1)}), bf16[8,40,640]{2,1,0:T(8,128)(2,1)S(1)}, u32[]{:S(2)}, u32[]{:S(2)}) async-start(bf16[8,40,640]{2,1,0:T(8,128)(2,1)} %get-tuple-element.27), calls=%async_computation.1 | async-start | bytes 819200 | tf_op jit(solution)/shard_map/all_to_all | solution.py:328
  12.7 5.0 %copy-start.1 = (s32[64]{0:T(128)S(1)}, s32[64]{0:T(128)}, u32[]{:S(2)}) copy-start(s32[64]{0:T(128)} %offsets.3) | copy-start | bytes 772
  14.8 4.6 %collective-permute-start = (bf16[320,512]{1,0:T(8,128)(2,1)S(1)}, bf16[320,512]{1,0:T(8,128)(2,1)S(1)}, u32[]{:S(2)}, u32[]{:S(2)}) collective-permute-start(bf16[320,512]{1,0:T(8,128)(2,1)S(1)} %get-tuple-element.22.near), channel_id=1, source_target_pairs={{0,1},{1,0},{2,3},{3,2},{4,5},{5,4},{6,7},{7,6},{8,9},{9,8},{10,11... | collective-permute-start | bytes 983048 | tf_op jit(solution)/shard_map/ppermute | solution.py:25
  27.4 38.3 %all-to-all-start = ((bf16[8,160,512]{2,1,0:T(8,128)(2,1)}), bf16[8,160,512]{2,1,0:T(8,128)(2,1)S(1)}, u32[]{:S(2)}, u32[]{:S(2)}) async-start(bf16[8,160,512]{2,1,0:T(8,128)(2,1)} %shard_map.94), calls=%async_computation | async-start | bytes 2621440 | tf_op jit(solution)/shard_map/all_to_all | solution.py:383
  55.3 6.9 %copy-start.3 = (s32[64]{0:T(128)S(1)}, s32[64]{0:T(128)}, u32[]{:S(2)}) copy-start(s32[64]{0:T(128)} %param.18) | copy-start | bytes 772
  55.4 12.6 %collective-permute-start.1 = (bf16[1280,640]{1,0:T(8,128)(2,1)S(1)}, bf16[1280,640]{1,0:T(8,128)(2,1)}, u32[]{:S(2)}, u32[]{:S(2)}) collective-permute-start(bf16[1280,640]{1,0:T(8,128)(2,1)S(1)} %bitcast.12), channel_id=1, source_target_pairs={{0,1},{1,0},{2,3},{3,2},{4,5},{5,4},{6,7},{7,6},{8,9},{9,8},{10,11... | collective-permute-start | bytes 4915208 | tf_op jit(solution)/shard_map/ppermute | solution.py:25
  68.0 14.1 %copy-start.2 = (s32[64,2]{0,1:T(2,128)S(1)}, s32[64,2]{0,1:T(2,128)}, u32[]{:S(2)}) copy-start(s32[64,2]{0,1:T(2,128)} %param.16) | copy-start | bytes 1540
  75.0 19.7 %all-to-all-start.2 = ((bf16[8,160,128]{2,1,0:T(8,128)(2,1)}), bf16[8,160,128]{2,1,0:T(8,128)(2,1)S(1)}, u32[]{:S(2)}, u32[]{:S(2)}) async-start(bf16[8,160,128]{2,1,0:T(8,128)(2,1)} %shard_map.96), calls=%async_computation.2 | async-start | bytes 655360 | tf_op jit(solution)/shard_map/all_to_all | solution.py:433
  96.1 12.8 %all-to-all-start.3 = ((bf16[8,160,128]{2,1,0:T(8,128)(2,1)}), bf16[8,160,128]{2,1,0:T(8,128)(2,1)S(1)}, u32[]{:S(2)}, u32[]{:S(2)}) async-start(bf16[8,160,128]{2,1,0:T(8,128)(2,1)} %shard_map.97), calls=%async_computation.3 | async-start | bytes 655360 | tf_op jit(solution)/shard_map/all_to_all | solution.py:442

commit v11 on v7

--- a/solution.py
+++ b/solution.py
@@ -148,12 +148,24 @@
 
 
 def project_kernel(
-    gathered, weight, resid_hbm, merge_hbm, attended, partial, merge_weight, resid, sems
+    gathered,
+    weight,
+    resid_hbm,
+    merge_hbm,
+    early_hbm,
+    attended,
+    partial,
+    merge_weight,
+    early,
+    resid,
+    sems,
 ):
     resid_copy = pltpu.make_async_copy(resid_hbm, resid, sems.at[0])
     resid_copy.start()
     merge_copy = pltpu.make_async_copy(merge_hbm, merge_weight, sems.at[1])
     merge_copy.start()
+    early_copy = pltpu.make_async_copy(early_hbm, early, sems.at[2])
+    early_copy.start()
     core = lax.axis_index("tok") % 2
     group, depth, rows = gathered.shape
     whole = gathered[...].reshape(group * depth, rows)
@@ -169,33 +181,22 @@
         place = (1 - core) * (tiles // 2) + tile
         partial[place] = resid[place]
     merge_copy.wait()
+    early_copy.wait()
 
 
 def merge_kernel(
-    attended, weight_hbm, partial, merge_weight, out, weight, total, block, weight_sems, sems
+    attended, first_weight, second_weight, partial, merge_weight, out, total, block, sems
 ):
-    chunks = [(start, min(256, weight.shape[1] - start)) for start in range(0, weight.shape[1], 256)]
-    loads = [
-        pltpu.make_async_copy(
-            weight_hbm.at[:, pl.ds(start, size)],
-            weight.at[:, pl.ds(start, size)],
-            weight_sems.at[chunk],
-        )
-        for chunk, (start, size) in enumerate(chunks)
-    ]
-    for load in loads:
-        load.start()
     core = lax.axis_index("tok") % 2
     tiles, rows = partial.shape[:2]
+    depth = first_weight.shape[0]
+    part = dot(attended[:, :depth], first_weight[...], ((1,), (0,)))
+    part += dot(attended[:, depth:], second_weight[...], ((1,), (0,)))
     for tile in range(tiles // 2):
         place = core * (tiles // 2) + tile
         total[place] = partial[place]
-    for load, (start, size) in zip(loads, chunks):
-        load.wait()
-        part = dot(attended[...], weight[:, start : start + size], ((1,), (0,)))
-        for tile in range(size // LANES):
-            place = (1 - core) * (tiles // 2) + start // LANES + tile
-            total[place] = partial[place] + part[:, tile * LANES : (tile + 1) * LANES]
+        place = (1 - core) * (tiles // 2) + tile
+        total[place] = partial[place] + part[:, tile * LANES : (tile + 1) * LANES]
     values = jnp.concatenate([total[tile] for tile in range(tiles)], axis=1)
     normed = normalize(values)
     for tile in range(tiles):
@@ -322,51 +323,51 @@
         compiler_params=params,
     )(image_offsets, queries, far, mixed, stats)
     pieces, sent = lax.optimization_barrier((pieces, sent))
-    own_weight = [
-        lax.all_gather(part, "tok", axis=0, axis_index_groups=rings_x)
+    halves = [
+        lax.all_gather(part, "tok", axis=1, axis_index_groups=rings_x, tiled=True).reshape(
+            group * width_here // 2, columns
+        )
         for part in jnp.split(pieces, 2)
     ]
-    own_weight = jnp.concatenate([part.transpose(1, 0, 2, 3) for part in own_weight], axis=0)
-    own_weight = own_weight.reshape(group * width_here, columns)
-    other_weight = partner(own_weight, "tok", 0)
+    own_weight = jnp.concatenate(halves, axis=0)
+    other_halves = [partner(half, "tok", 0) for half in halves]
 
     gathered = lax.all_to_all(sent, "head", 0, 0, tiled=True)
     rows_here = block_rows // 4
     blocks_shape = pltpu.HBM((RING, width_here, rows_here), jnp.bfloat16)
     tiles = width // LANES
     half_flops = 2 * block_rows * width * columns
-    attended, partial, merge_here = pl.pallas_call(
+    attended, partial, merge_here, early = pl.pallas_call(
         project_kernel,
         out_shape=(
             jax.ShapeDtypeStruct((block_rows, width), jnp.bfloat16),
             jax.ShapeDtypeStruct((tiles, block_rows, LANES), jnp.float32),
             jax.ShapeDtypeStruct(merge_weight.shape, jnp.bfloat16),
-        ),
-        in_specs=[VMEM, VMEM, HBM, HBM],
-        out_specs=(VMEM, VMEM, VMEM),
+            jax.ShapeDtypeStruct(other_halves[1].shape, jnp.bfloat16),
+        ),
+        in_specs=[VMEM, VMEM, HBM, HBM, HBM],
+        out_specs=(VMEM, VMEM, VMEM, VMEM),
         scratch_shapes=[
             pltpu.VMEM((tiles, block_rows, LANES), jnp.float32),
-            pltpu.SemaphoreType.DMA((2,)),
+            pltpu.SemaphoreType.DMA((3,)),
         ],
         compiler_params=params,
         cost_estimate=pl.CostEstimate(
             flops=half_flops, bytes_accessed=8 * 2**20, transcendentals=0
         ),
-    )(gathered, own_weight, at_hbm(resid), at_hbm(merge_weight))
+    )(gathered, own_weight, *map(at_hbm, (resid, merge_weight, other_halves[1])))
     projected = pl.pallas_call(
         merge_kernel,
         out_shape=blocks_shape,
-        in_specs=[VMEM, HBM, VMEM, VMEM],
+        in_specs=[VMEM] * 5,
         out_specs=HBM,
         scratch_shapes=[
-            pltpu.VMEM(other_weight.shape, jnp.bfloat16),
             pltpu.VMEM((tiles, block_rows, LANES), jnp.float32),
             pltpu.VMEM((width_here, rows_here), jnp.bfloat16),
-            pltpu.SemaphoreType.DMA((columns // 256 + 1,)),
             pltpu.SemaphoreType.DMA((RING,)),
         ],
         compiler_params=params,
-    )(attended, at_hbm(other_weight), partial, merge_here)
+    )(attended, other_halves[0], early, partial, merge_here)
 
     image_ids = jnp.arange(owners.shape[0], dtype=jnp.int32)
     place_ids = jnp.arange(places, dtype=jnp.int32)

time: 110 us -> 113 us (1.027)
  blocking collectives: 24.1 us -> 27.3 us
  waiting for transfers between devices: 26.7 us -> 24.3 us
  other arithmetic: 0.53 us -> 1.9 us
    all_to_all x1, waiting for transfers between devices: 3.31 us -> 0.01 us  [on_device(): gathered = lax.all_to_all(sent, 'head', 0, 0, tiled=True)]
    all_gather x2, blocking collectives: 24.1 us -> 27.3 us  [on_device(): lax.all_gather(part, 'tok', axis=1, axis_index_groups=rings_x, tiled=True)]
    concatenate x1, other arithmetic: 0.17 us -> 1.54 us  [on_device(): own_weight = jnp.concatenate(halves, axis=0)]
    ppermute x2 -> x3, starting transfers between devices: 9.66 us -> 10.6 us  [partner(): lax.ppermute(x, axis, [(i, i ^ 1 << apart) for i in range(lax.axis_size(a...]
  transfers between devices with their start and end apart: 6 -> 7, of which waited for: 4 -> 3; matrix products, arithmetic and copies ran while one was open for 1% -> 2% of each run, Pallas kernels for 10% -> 10%
where the time goes in v11:
time: 113 us; the launch traced here: 112 us
  starting transfers between devices  37 us (33%)
  blocking collectives  27.3 us (24%)
  waiting for transfers between devices  24.3 us (22%)
  Pallas kernels  19.5 us (17%)
  local copies, waits for them, and re-layouts  1.94 us (2%)
  other arithmetic  1.9 us (2%)
    all_gather x2, blocking collectives, on_device(): lax.all_gather(part, 'tok', axis=1, axis_index_groups=rings_x, tiled=True)  27.3 us
    all_to_all x1, waiting for transfers between devices, on_device(): lax.all_to_all(projected, 'tok', 0, 0, axis_index_groups=rings_y, tiled=T...  13.5 us
    all_to_all x1, starting transfers between devices, on_device(): pieces = lax.all_to_all(pieces, 'head', 0, 0, tiled=True)  10.9 us
    ppermute x3, starting transfers between devices, partner(): lax.ppermute(x, axis, [(i, i ^ 1 << apart) for i in range(lax.axis_size(a...  10.6 us
    all_to_all x1, waiting for transfers between devices, on_device(): lax.all_to_all(blocks, 'tok', 0, 0, axis_index_groups=planes, tiled=True)  6.98 us
    all_to_all x1, starting transfers between devices, on_device(): lax.all_to_all(projected, 'tok', 0, 0, axis_index_groups=rings_y, tiled=T...  6.83 us
    pallas_call x1, Pallas kernels, on_device(): pl.pallas_call(merge_kernel, out_shape=blocks_shape, in_specs=[VMEM] * 5,...  5.33 us
    all_to_all x1, starting transfers between devices, on_device(): lax.all_to_all(blocks, 'tok', 0, 0, axis_index_groups=planes, tiled=True)  5.13 us
  transfers between devices with their start and end apart: 7, of which 3 were waited for; matrix products, arithmetic and copies ran while one was open for 2% of the time, Pallas kernels for 10%

profile of v11, /device:TPU:1, one launch (start us, length us, event | category | flops | bytes accessed | tf_op | source)
XLA Modules:
  0.0 112.1 jit_solution(1575783986902564590)
XLA Ops:
  0.0 0.0 copy-start
  0.0 0.9 dynamic_slice.3
  0.9 0.8 broadcast_in_dim.50
  1.7 10.9 %all-to-all-start = ((bf16[8,40,640]{2,1,0:T(8,128)(2,1)}), bf16[8,40,640]{2,1,0:T(8,128)(2,1)S(1)}, u32[]{:S(2)}, u32[]{:S(2)}) async-start(bf16[8,40,640]{2,1,0:T(8,128)(2,1)} %broadcast_in_dim.50), calls=%async_computation | async-start | bytes 819200 | tf_op jit(solution)/shard_map/all_to_all | solution.py:275
  12.6 0.0 copy-done
  12.6 0.0 copy-start.1
  12.6 3.4 %shard_map.91 = (f32[10,512,128]{2,1,0:T(8,128)}, bf16[160,512]{1,0:T(8,128)(2,1)S(1)}, bf16[320,512]{1,0:T(8,128)(2,1)S(1)}) custom-call(s32[64]{0:T(128)} %offsets.3, bf16[512,1280]{1,0:T(8,128)(2,1)S(1)} %copy-done, bf16[64,1280]{1,0:T(8,128)(2,1)} %row_hbm.1, bf16[64,1280]{1,0:T(8,128)(2,1)} %col_hbm.1, bf16[3,160,1280]{2,1,0:T(8,128)(2,1)} %weight_hbm.1), custom_call_target="tpu_custom_call" | custom-call | flops 629145600 | bytes 8388608 | tf_op jit(solution)/shard_map/pallas_call | solution.py:277
  16.0 2.9 %collective-permute-start = (bf16[320,512]{1,0:T(8,128)(2,1)S(1)}, bf16[320,512]{1,0:T(8,128)(2,1)S(1)}, u32[]{:S(2)}, u32[]{:S(2)}) collective-permute-start(bf16[320,512]{1,0:T(8,128)(2,1)S(1)} %get-tuple-element.17.near), channel_id=1, source_target_pairs={{0,1},{1,0},{2,3},{3,2},{4,5},{5,4},{6,7},{7,6},{8,9},{9,8},{10,11... | collective-permute-start | bytes 983048 | tf_op jit(solution)/shard_map/ppermute | solution.py:25
  18.9 0.0 copy-done.1
  18.9 1.7 %shard_map.92 = (f32[160,512]{1,0:T(8,128)S(1)}, f32[4,512]{1,0:T(4,128)S(1)}) custom-call(s32[64]{0:T(128)S(1)} %copy-done.1, bf16[160,512]{1,0:T(8,128)(2,1)S(1)} %get-tuple-element.16.queries, bf16[320,512]{1,0:T(8,128)(2,1)S(1)} %get-tuple-element.17.near), custom_call_target="tpu_custom_call" | custom-call | flops 167772160 | bytes 2097152 | tf_op jit(solution)/shard_map/pallas_call | solution.py:299
  20.6 0.0 collective-permute-done.far
  20.6 2.8 %shard_map.93 = bf16[8,160,512]{2,1,0:T(8,128)(2,1)} custom-call(s32[64]{0:T(128)S(1)} %copy-done.1, bf16[160,512]{1,0:T(8,128)(2,1)S(1)} %get-tuple-element.16.queries, bf16[320,512]{1,0:T(8,128)(2,1)S(1)} %collective-permute-done.far, f32[160,512]{1,0:T(8,128)S(1)} %get-tuple-element.18.near_mixed, f32[4,512]{1,0:T(4,128)S(1)} %get-tuple-element.19.stats), custom_call_target="tpu_custom_call" | custom-call | tf_op jit(solution)/shard_map/pallas_call | solution.py:314
  23.4 3.9 %all-to-all-done = bf16[8,40,640]{2,1,0:T(8,128)(2,1)S(1)} async-done(((bf16[8,40,640]{2,1,0:T(8,128)(2,1)}), bf16[8,40,640]{2,1,0:T(8,128)(2,1)S(1)}, u32[]{:S(2)}, u32[]{:S(2)}) %all-to-all-start) | async-done | bytes 409632 | tf_op jit(solution)/shard_map/all_to_all | solution.py:275
  27.3 3.6 %all-to-all-start.1 = ((bf16[8,160,512]{2,1,0:T(8,128)(2,1)}), bf16[8,160,512]{2,1,0:T(8,128)(2,1)S(1)}, u32[]{:S(2)}, u32[]{:S(2)}) async-start(bf16[8,160,512]{2,1,0:T(8,128)(2,1)} %shard_map.93), calls=%async_computation.1 | async-start | bytes 2621440 | tf_op jit(solution)/shard_map/all_to_all | solution.py:335
  30.9 0.0 copy-start.3
  30.9 13.5 %all_gather.7 = bf16[4,160,640]{2,1,0:T(8,128)(2,1)} all-gather(bf16[4,40,640]{2,1,0:T(8,128)(2,1)S(1)} %get-tuple-element.28), channel_id=1, replica_groups={{0,16,32,48},{1,17,33,49},{2,18,34,50},{3,19,35,51},{4,20,36,52},{5,21,..., dimensions={1}, use_global_device_ids=true | all-gather | bytes 1024000 | tf_op jit(solution)/shard_map/all_gather | solution.py:327
  44.4 4.2 %collective-permute-start.1 = (bf16[640,640]{1,0:T(8,128)(2,1)}, bf16[640,640]{1,0:T(8,128)(2,1)}, u32[]{:S(2)}, u32[]{:S(2)}) collective-permute-start(bf16[640,640]{1,0:T(8,128)(2,1)} %bitcast.3), channel_id=1, source_target_pairs={{0,1},{1,0},{2,3},{3,2},{4,5},{5,4},{6,7},{7,6},{8,9},{9,8},{10,11... | collective-permute-start | bytes 2457608 | tf_op jit(solution)/shard_map/ppermute | solution.py:25
  48.6 13.8 %all_gather.6 = bf16[4,160,640]{2,1,0:T(8,128)(2,1)} all-gather(bf16[4,40,640]{2,1,0:T(8,128)(2,1)S(1)} %get-tuple-element.27), channel_id=1, replica_groups={{0,16,32,48},{1,17,33,49},{2,18,34,50},{3,19,35,51},{4,20,36,52},{5,21,..., dimensions={1}, use_global_device_ids=true | all-gather | bytes 1024000 | tf_op jit(solution)/shard_map/all_gather | solution.py:327
  62.4 3.5 %collective-permute-start.2 = (bf16[640,640]{1,0:T(8,128)(2,1)}, bf16[640,640]{1,0:T(8,128)(2,1)}, u32[]{:S(2)}, u32[]{:S(2)}) collective-permute-start(bf16[640,640]{1,0:T(8,128)(2,1)} %bitcast.2), channel_id=1, source_target_pairs={{0,1},{1,0},{2,3},{3,2},{4,5},{5,4},{6,7},{7,6},{8,9},{9,8},{10,11... | collective-permute-start | bytes 2457608 | tf_op jit(solution)/shard_map/ppermute | solution.py:25
  65.9 0.0 copy-done.3
  65.9 0.1 select_reduce_fusion
  66.1 1.5 %pad_maximum_fusion.weight = bf16[1280,640]{1,0:T(8,128)(2,1)S(1)} fusion(bf16[640,640]{1,0:T(8,128)(2,1)} %bitcast.3, bf16[640,640]{1,0:T(8,128)(2,1)} %bitcast.2), kind=kLoop, calls=%fused_computation | loop fusion | flops 3276800 | bytes 3276800 | tf_op jit(solution)/shard_map/concatenate | solution.py:332
  67.6 0.0 collective-permute-done.1.early_hbm
  67.6 0.0 all-to-all-done.1.gathered
  67.6 3.6 %shard_map.94 = (bf16[512,1280]{1,0:T(8,128)(2,1)S(1)}, f32[10,512,128]{2,1,0:T(8,128)S(1)}, bf16[160,5120]{1,0:T(8,128)(2,1)S(1)}, bf16[640,640]{1,0:T(8,128)(2,1)S(1)}) custom-call(bf16[8,160,512]{2,1,0:T(8,128)(2,1)S(1)} %all-to-all-done.1.gathered, bf16[1280,640]{1,0:T(8,128)(2,1)S(1)} %pad_maximum_fusion.weight, ...), custom_call_target="tpu_custom_call" | custom-call | flops 838860800 | bytes 8388608 | tf_op jit(solution)/shard_map/pallas_call | solution.py:340
  71.2 0.0 collective-permute-done.2.first_weight
  71.2 0.0 copy-start.2
  71.2 5.3 %shard_map.95 = bf16[8,160,128]{2,1,0:T(8,128)(2,1)} custom-call(bf16[512,1280]{1,0:T(8,128)(2,1)S(1)} %get-tuple-element.23.attended, bf16[640,640]{1,0:T(8,128)(2,1)} %collective-permute-done.2.first_weight, bf16[640,640]{1,0:T(8,128)(2,1)S(1)} %get-tuple-element.24.second_weight, f32[10,512,128]{2,1,0:T(8,128)S(1)} %get-tuple-element.25.partial, ...), custom_call_target="tpu_custom_call" | custom-call | tf_op jit(solution)/shard_map/pallas_call | solution.py:359
  76.6 6.8 %all-to-all-start.2 = ((bf16[8,160,128]{2,1,0:T(8,128)(2,1)}), bf16[8,160,128]{2,1,0:T(8,128)(2,1)S(1)}, u32[]{:S(2)}, u32[]{:S(2)}) async-start(bf16[8,160,128]{2,1,0:T(8,128)(2,1)} %shard_map.95), calls=%async_computation.2 | async-start | bytes 655360 | tf_op jit(solution)/shard_map/all_to_all | solution.py:385
  83.4 0.1 reduce_sum.31
  83.5 0.1 fusion.3
  83.6 0.1 reshape.160.wanted
  83.7 0.0 copy-done.2
  83.7 13.5 %all-to-all-done.2.blocks = bf16[8,160,128]{2,1,0:T(8,128)(2,1)S(1)} async-done(((bf16[8,160,128]{2,1,0:T(8,128)(2,1)}), bf16[8,160,128]{2,1,0:T(8,128)(2,1)S(1)}, u32[]{:S(2)}, u32[]{:S(2)}) %all-to-all-start.2) | async-done | bytes 327712 | tf_op jit(solution)/shard_map/all_to_all | solution.py:385
  97.2 1.3 %shard_map.96 = bf16[8,160,128]{2,1,0:T(8,128)(2,1)} custom-call(s32[8]{0:T(128)S(1)} %reshape.160.wanted, bf16[8,160,128]{2,1,0:T(8,128)(2,1)S(1)} %all-to-all-done.2.blocks), custom_call_target="tpu_custom_call" | custom-call | tf_op jit(solution)/shard_map/pallas_call | solution.py:386
  98.5 5.1 %all-to-all-start.3 = ((bf16[8,160,128]{2,1,0:T(8,128)(2,1)}), bf16[8,160,128]{2,1,0:T(8,128)(2,1)S(1)}, u32[]{:S(2)}, u32[]{:S(2)}) async-start(bf16[8,160,128]{2,1,0:T(8,128)(2,1)} %shard_map.96), calls=%async_computation.3 | async-start | bytes 655360 | tf_op jit(solution)/shard_map/all_to_all | solution.py:394
  103.7 0.1 fusion.5.facts
  103.8 7.0 %all-to-all-done.3.blocks = bf16[8,160,128]{2,1,0:T(8,128)(2,1)S(1)} async-done(((bf16[8,160,128]{2,1,0:T(8,128)(2,1)}), bf16[8,160,128]{2,1,0:T(8,128)(2,1)S(1)}, u32[]{:S(2)}, u32[]{:S(2)}) %all-to-all-start.3) | async-done | bytes 327712 | tf_op jit(solution)/shard_map/all_to_all | solution.py:394
  110.8 1.4 %shard_map.97 = bf16[160,248]{1,0:T(8,128)(2,1)} custom-call(s32[3]{0:T(128)S(1)} %fusion.5.facts, bf16[8,160,128]{2,1,0:T(8,128)(2,1)S(1)} %all-to-all-done.3.blocks), custom_call_target="tpu_custom_call" | custom-call | tf_op jit(solution)/shard_map/pallas_call | solution.py:395
  (5 shorter events, 0.1 us)
Async XLA Ops:
  0.0 12.6 %copy-start = (bf16[512,1280]{1,0:T(8,128)(2,1)S(1)}, bf16[512,1280]{1,0:T(8,128)(2,1)}, u32[]{:S(2)}) copy-start(bf16[512,1280]{1,0:T(8,128)(2,1)} %patches.1) | copy-start | bytes 3932164
  1.7 25.6 %all-to-all-start = ((bf16[8,40,640]{2,1,0:T(8,128)(2,1)}), bf16[8,40,640]{2,1,0:T(8,128)(2,1)S(1)}, u32[]{:S(2)}, u32[]{:S(2)}) async-start(bf16[8,40,640]{2,1,0:T(8,128)(2,1)} %broadcast_in_dim.50), calls=%async_computation | async-start | bytes 819200 | tf_op jit(solution)/shard_map/all_to_all | solution.py:275
  12.6 6.3 %copy-start.1 = (s32[64]{0:T(128)S(1)}, s32[64]{0:T(128)}, u32[]{:S(2)}) copy-start(s32[64]{0:T(128)} %offsets.3) | copy-start | bytes 772
  16.0 4.6 %collective-permute-start = (bf16[320,512]{1,0:T(8,128)(2,1)S(1)}, bf16[320,512]{1,0:T(8,128)(2,1)S(1)}, u32[]{:S(2)}, u32[]{:S(2)}) collective-permute-start(bf16[320,512]{1,0:T(8,128)(2,1)S(1)} %get-tuple-element.17.near), channel_id=1, source_target_pairs={{0,1},{1,0},{2,3},{3,2},{4,5},{5,4},{6,7},{7,6},{8,9},{9,8},{10,11... | collective-permute-start | bytes 983048 | tf_op jit(solution)/shard_map/ppermute | solution.py:25
  27.3 40.3 %all-to-all-start.1 = ((bf16[8,160,512]{2,1,0:T(8,128)(2,1)}), bf16[8,160,512]{2,1,0:T(8,128)(2,1)S(1)}, u32[]{:S(2)}, u32[]{:S(2)}) async-start(bf16[8,160,512]{2,1,0:T(8,128)(2,1)} %shard_map.93), calls=%async_computation.1 | async-start | bytes 2621440 | tf_op jit(solution)/shard_map/all_to_all | solution.py:335
  30.9 35.1 %copy-start.3 = (s32[64]{0:T(128)S(1)}, s32[64]{0:T(128)}, u32[]{:S(2)}) copy-start(s32[64]{0:T(128)} %param.18) | copy-start | bytes 772
  44.4 23.2 %collective-permute-start.1 = (bf16[640,640]{1,0:T(8,128)(2,1)}, bf16[640,640]{1,0:T(8,128)(2,1)}, u32[]{:S(2)}, u32[]{:S(2)}) collective-permute-start(bf16[640,640]{1,0:T(8,128)(2,1)} %bitcast.3), channel_id=1, source_target_pairs={{0,1},{1,0},{2,3},{3,2},{4,5},{5,4},{6,7},{7,6},{8,9},{9,8},{10,11... | collective-permute-start | bytes 2457608 | tf_op jit(solution)/shard_map/ppermute | solution.py:25
  62.4 8.8 %collective-permute-start.2 = (bf16[640,640]{1,0:T(8,128)(2,1)}, bf16[640,640]{1,0:T(8,128)(2,1)}, u32[]{:S(2)}, u32[]{:S(2)}) collective-permute-start(bf16[640,640]{1,0:T(8,128)(2,1)} %bitcast.2), channel_id=1, source_target_pairs={{0,1},{1,0},{2,3},{3,2},{4,5},{5,4},{6,7},{7,6},{8,9},{9,8},{10,11... | collective-permute-start | bytes 2457608 | tf_op jit(solution)/shard_map/ppermute | solution.py:25
  71.2 12.5 %copy-start.2 = (s32[64,2]{0,1:T(2,128)S(1)}, s32[64,2]{0,1:T(2,128)}, u32[]{:S(2)}) copy-start(s32[64,2]{0,1:T(2,128)} %param.16) | copy-start | bytes 1540
  76.6 20.6 %all-to-all-start.2 = ((bf16[8,160,128]{2,1,0:T(8,128)(2,1)}), bf16[8,160,128]{2,1,0:T(8,128)(2,1)S(1)}, u32[]{:S(2)}, u32[]{:S(2)}) async-start(bf16[8,160,128]{2,1,0:T(8,128)(2,1)} %shard_map.95), calls=%async_computation.2 | async-start | bytes 655360 | tf_op jit(solution)/shard_map/all_to_all | solution.py:385
  98.5 12.2 %all-to-all-start.3 = ((bf16[8,160,128]{2,1,0:T(8,128)(2,1)}), bf16[8,160,128]{2,1,0:T(8,128)(2,1)S(1)}, u32[]{:S(2)}, u32[]{:S(2)}) async-start(bf16[8,160,128]{2,1,0:T(8,128)(2,1)} %shard_map.96), calls=%async_computation.3 | async-start | bytes 655360 | tf_op jit(solution)/shard_map/all_to_all | solution.py:394
